TPU v7x, 512 devices: a whole 4x8x8 slice. The times are simulated.
512 devices in a mesh: row: 32 (over z, y_lo, core), col: 16 (over x, y_hi).
Axes of the slice: x: 4, y: 8 (y_hi: 4, y_lo: 2; y = y_hi * 2 + y_lo), z: 8, core: 2. Of those that a mesh axis runs over, the one named last changes fastest.
Arguments:
- view_a: float32 [128, 512, 768], P('col', 'row'), may hold values from 0.25 to 4
- view_b: float32 [128, 768, 512], P('col', 'row'), may hold values from 0.25 to 4
- estimate: float32 [128, 512, 768], P('col', 'row'), may hold values from 0.5 to 2
- axial_kernel: float32 [2, 31], replicated, may hold values from 0.05 to 1
- lateral_kernel: float32 [2, 2, 11], replicated, may hold values from 0.05 to 1
Outputs:
- restored: float32 [128, 512, 768], P('col', 'row')
All inputs are finite; a program needn't handle non-finite values.
Results may differ from a plain program's by a relative error of at most 0.00002.
Values sent between devices are 32-bit elements; how exact they have to be, the bound alone decides.
No kernel may reach another device: no remote copies, remote signals or barrier semaphores. Data moves between devices by JAX's collectives and lax.ppermute only.
A program may use at most 64 MiB of HBM per device.

v0:
```python
import functools
import jax
import jax.numpy as jnp
from jax import lax
from jax.experimental import pallas as pl
from jax.experimental.pallas import tpu as pltpu
from jax.sharding import PartitionSpec as P

ITERS = 2
LANES = 128
SHIFT = 64
CHUNKS = 1
CHUNK_LIMIT = 8 * 2**20
HIGH = lax.Precision.HIGHEST
VMEM = pl.BlockSpec(memory_space=pltpu.VMEM)
LIMIT = pltpu.CompilerParams(vmem_limit_bytes=CHUNK_LIMIT)
SMEM = pl.BlockSpec(memory_space=pltpu.SMEM)


def splat(value):
    return jnp.full((8, LANES), value, jnp.float32)


def normalized(read, count):
    taps = [read(k) for k in range(count)]
    total = taps[0]
    for tap in taps[1:]:
        total = total + tap
    total = splat(total)
    return [splat(tap) / total for tap in taps]


def fill_band(band_ref, taps, sign):
    half = len(taps) // 2
    lane = lax.broadcasted_iota(jnp.int32, (8, LANES), 1)
    sub = lax.broadcasted_iota(jnp.int32, (8, LANES), 0)

    def fill(step, carry):
        distance = sign * (sub + step * 8 - lane - SHIFT)
        value = jnp.zeros((8, LANES), jnp.float32)
        for k, tap in enumerate(taps):
            value = jnp.where(distance == k - half, tap, value)
        band_ref[pl.ds(pl.multiple_of(step * 8, 8), 8), :] = value
        return carry

    lax.fori_loop(0, 2 * LANES // 8, fill, 0, unroll=8)


def prepare_body(axial_ref, lateral_ref, ya_ref, yb_ref, za_ref, zb_ref, *band_refs):
    axial, lateral = axial_ref.shape[1], lateral_ref.shape[2]
    rows = (
        (ya_ref, lambda k: axial_ref[0, k], axial),
        (yb_ref, lambda k: lateral_ref[1, 1, k], lateral),
        (za_ref, lambda k: lateral_ref[0, 0, k], lateral),
        (zb_ref, lambda k: lateral_ref[1, 0, k], lateral),
    )
    for target, read, count in rows:
        for k, tap in enumerate(normalized(read, count)):
            target[k] = tap
    xa = normalized(lambda k: lateral_ref[0, 1, k], lateral)
    xb = normalized(lambda k: axial_ref[1, k], axial)
    for taps, refs in ((xa, band_refs[:2]), (xb, band_refs[2:])):
        fill_band(refs[0], taps, 1)
        fill_band(refs[1], taps, -1)


def local(*shape):
    return pltpu.VMEM(shape, jnp.float32)


def call(body, operands, shapes, scratch=()):
    operands = [pltpu.with_memory_space_constraint(operand, pltpu.VMEM) for operand in operands]
    return pl.pallas_call(
        body,
        out_shape=shapes,
        in_specs=[VMEM] * len(operands),
        out_specs=[VMEM] * len(shapes),
        scratch_shapes=scratch,
        compiler_params=LIMIT,
    )(*operands)


def prepare(axial_kernel, lateral_kernel):
    axial, lateral = axial_kernel.shape[1], lateral_kernel.shape[2]
    shapes = [local(count, 8, LANES) for count in (axial, lateral, lateral, lateral)]
    shapes += [local(2 * LANES, LANES)] * 4
    outs = pl.pallas_call(
        prepare_body,
        out_shape=shapes,
        in_specs=[SMEM, SMEM],
        out_specs=[VMEM] * len(shapes),
        compiler_params=LIMIT,
        name="prepare",
    )(axial_kernel, lateral_kernel)
    return outs[:2], outs[2:4], (outs[4:6], outs[6:8])


def correlate(taps, rows, extent, reverse):
    count = len(taps)
    sums = [None] * extent
    for r in range(extent + count - 1):
        value = rows(r)
        for i in range(max(0, r - count + 1), min(extent, r + 1)):
            k = r - i
            term = taps[count - 1 - k if reverse else k] * value
            sums[i] = term if sums[i] is None else sums[i] + term
    return sums


def padded_rows(low, mid, high, pick):
    margin, extent = low.shape[0], mid.shape[0]

    def rows(r):
        if r < margin:
            return pick(low, r)
        if r < margin + extent:
            return pick(mid, r - margin)
        return pick(high, r - margin - extent)

    return rows


def lanes_at(j):
    return pl.ds(pl.multiple_of(j * LANES, LANES), LANES)


def put(out_refs, i, at, lanes, value):
    mid_ref, first_ref, last_ref = out_refs
    extent, margin = mid_ref.shape[0], first_ref.shape[0]
    mid_ref[i, at, lanes] = value
    if i < margin:
        first_ref[i, at, lanes] = value
    if i >= extent - margin:
        last_ref[i - extent + margin, at, lanes] = value


def along_z(taps_ref, low_ref, mid_ref, high_ref, reverse, store):
    rows_y, width = mid_ref.shape[1], mid_ref.shape[2]

    def tile(j, carry):
        lanes = lanes_at(j)
        taps = [taps_ref[k] for k in range(taps_ref.shape[0])]
        for y in range(0, rows_y, 8):
            pick = lambda ref, r: ref[r, y:y + 8, lanes]
            sums = correlate(taps, padded_rows(low_ref, mid_ref, high_ref, pick), mid_ref.shape[0], reverse)
            store(y, j, sums)
        return carry

    lax.fori_loop(0, width // LANES, tile, 0)


def depth_body(reverse, taps_ref, low_ref, mid_ref, high_ref, *out_refs):
    def store(y, j, sums):
        turned = jnp.swapaxes(jnp.stack(sums), 0, 1)
        for i in range(8):
            put(out_refs, y + i, slice(None), lanes_at(j), turned[i])

    along_z(taps_ref, low_ref, mid_ref, high_ref, reverse, store)


def depth(taps, low, mid, high, reverse, margin):
    nz, ny, nx = mid.shape
    shapes = [local(ny, nz, nx), local(margin, nz, nx), local(margin, nz, nx)]
    return call(functools.partial(depth_body, reverse), (taps, low, mid, high), shapes)


def plane_body(reverse, divide, taps_ref, low_ref, mid_ref, high_ref, *refs):
    view_ref, out_refs = (refs[0], refs[1:]) if divide else (None, refs)

    def tile(j, carry):
        lanes = lanes_at(j)
        taps = [taps_ref[k] for k in range(taps_ref.shape[0])]
        pick = lambda ref, r: ref[r, :, lanes]
        sums = correlate(taps, padded_rows(low_ref, mid_ref, high_ref, pick), mid_ref.shape[0], reverse)
        if divide:
            for i, value in enumerate(sums):
                put(out_refs, i, slice(None), lanes, view_ref[i, :, lanes] / value)
        else:
            for y in range(0, len(sums), 8):
                turned = jnp.swapaxes(jnp.stack(sums[y:y + 8]), 0, 1)
                for z in range(8):
                    put(out_refs, z, slice(y, y + 8), lanes, turned[z])
        return carry

    lax.fori_loop(0, mid_ref.shape[2] // LANES, tile, 0)


def plane(taps, low, mid, high, reverse, margin, view=None):
    ny, nz, nx = mid.shape
    outer, inner = (nz, ny) if view is None else (ny, nz)
    shapes = [local(outer, inner, nx), local(margin, inner, nx), local(margin, inner, nx)]
    operands = (taps, low, mid, high) + (() if view is None else (view,))
    return call(functools.partial(plane_body, reverse, view is not None), operands, shapes)


def deep_body(taps_ref, low_ref, mid_ref, high_ref, view_low_ref, view_ref, view_high_ref, *out_refs):
    extent = mid_ref.shape[0]

    def tile(j, carry):
        lanes = lanes_at(j)
        taps = [taps_ref[k] for k in range(taps_ref.shape[0])]
        pick = lambda ref, r: ref[r, :, lanes]
        wide = extent + len(taps) - 1
        sums = correlate(taps, padded_rows(low_ref, mid_ref, high_ref, pick), wide, False)
        seen = padded_rows(view_low_ref, view_ref, view_high_ref, pick)
        quotient = [seen(r) / value for r, value in enumerate(sums)]
        sums = correlate(taps, lambda r: quotient[r], extent, True)
        for y in range(0, extent, 8):
            turned = jnp.swapaxes(jnp.stack(sums[y:y + 8]), 0, 1)
            for z in range(8):
                put(out_refs, z, slice(y, y + 8), lanes, turned[z])
        return carry

    lax.fori_loop(0, mid_ref.shape[2] // LANES, tile, 0)


def deep(taps, halo, view, margin):
    ny, nz, nx = halo[1].shape
    shapes = [local(nz, ny, nx), local(margin, ny, nx), local(margin, ny, nx)]
    return call(deep_body, (taps, *halo, *view), shapes)


def clear_edges(wide_ref):
    blank = jnp.zeros((wide_ref.shape[0], LANES), jnp.float32)
    wide_ref[:, :LANES] = blank
    wide_ref[:, wide_ref.shape[1] - LANES:] = blank


def along_x(wide_ref, band):
    width = wide_ref.shape[1] - LANES
    for j in range(width // LANES):
        yield j, jnp.dot(
            wide_ref[:, j * LANES:(j + 2) * LANES], band, precision=HIGH, preferred_element_type=jnp.float32
        )


def put_ahead(wide_ref, band_ref, out_refs, ny):
    per_chunk = out_refs[0].shape[2] // LANES
    for j, value in along_x(wide_ref, band_ref[...]):
        chunk, inside = divmod(j, per_chunk)
        refs = out_refs[3 * chunk:3 * chunk + 3]
        lanes = slice(inside * LANES, (inside + 1) * LANES)
        for z in range(refs[0].shape[0]):
            put(refs, z, slice(None), lanes, value[z * ny:(z + 1) * ny])


def first_body(lateral_ref, estimate_ref, *refs):
    out_refs, (wide_ref, band_ref) = refs[:-2], refs[-2:]
    nz, ny, nx = estimate_ref.shape
    count = lateral_ref.shape[2]
    fill_band(band_ref, normalized(lambda k: lateral_ref[0, 1, k], count), 1)
    clear_edges(wide_ref)
    wide_ref[:, SHIFT:SHIFT + nx] = estimate_ref[...].reshape(nz * ny, nx)
    put_ahead(wide_ref, band_ref, out_refs, ny)


def ahead_shapes(shape, margin):
    nz, ny, nx = shape
    part = nx // CHUNKS
    return [local(nz, ny, part), local(margin, ny, part), local(margin, ny, part)] * CHUNKS


def chunked(outs):
    return [tuple(outs[3 * c:3 * c + 3]) for c in range(CHUNKS)]


def first(lateral_kernel, estimate, margin):
    nz, ny, nx = estimate.shape
    shapes = ahead_shapes(estimate.shape, margin)
    outs = pl.pallas_call(
        first_body,
        out_shape=shapes,
        in_specs=[SMEM, VMEM],
        out_specs=[VMEM] * len(shapes),
        scratch_shapes=[local(nz * ny, nx + LANES), local(2 * LANES, LANES)],
        compiler_params=LIMIT,
        name="first",
    )(lateral_kernel, pltpu.with_memory_space_constraint(estimate, pltpu.VMEM))
    return chunked(outs)


def update_body(last, taps_ref, band_ref, estimate_ref, *refs):
    halo_refs, refs = refs[:3 * CHUNKS], refs[3 * CHUNKS:]
    refs, (wide_ref, mixed_ref) = refs[:-2], refs[-2:]
    if last:
        (out_ref,) = refs
    else:
        next_ref, out_ref, *ahead_refs = refs
    nz, ny, nx = estimate_ref.shape
    per_chunk = nx // CHUNKS // LANES
    for c in range(CHUNKS):
        def store(y, j, sums):
            for z, value in enumerate(sums):
                mixed_ref[z * ny + y:z * ny + y + 8, lanes_at(j + c * per_chunk)] = value

        along_z(taps_ref, *halo_refs[3 * c:3 * c + 3], True, store)
    clear_edges(wide_ref)
    wide_ref[:, SHIFT:SHIFT + nx] = mixed_ref[...]
    for j, value in along_x(wide_ref, band_ref[...]):
        at = slice(j * LANES, (j + 1) * LANES)
        out_ref[:, :, at] = estimate_ref[:, :, at] * value.reshape(nz, ny, LANES)
    if not last:
        wide_ref[:, SHIFT:SHIFT + nx] = out_ref[...].reshape(nz * ny, nx)
        put_ahead(wide_ref, next_ref, ahead_refs, ny)


def update(taps, halos, band, estimate, band_next=None):
    nz, ny, nx = estimate.shape
    last = band_next is None
    operands = (taps, band, estimate) + sum(halos, ()) + (() if last else (band_next,))
    shapes = [local(nz, ny, nx)]
    if last:
        shapes = [jax.ShapeDtypeStruct((nz, ny, nx), jnp.float32)]
    else:
        shapes += ahead_shapes(estimate.shape, taps.shape[0] // 2)
    scratch = [local(nz * ny, nx + LANES), local(nz * ny, nx)]
    outs = call(functools.partial(update_body, last), operands, shapes, scratch)
    return outs[0], (None if last else chunked(outs[1:]))


def exchange(parts, axis):
    block, first_rows, last_rows = parts
    count = lax.axis_size(axis)
    forward = [(i, i + 1) for i in range(count - 1)]
    backward = [(target, source) for source, target in forward]
    low = lax.ppermute(last_rows, axis, forward)
    high = lax.ppermute(first_rows, axis, backward)
    return low, block, high


def pack_body(view_ref, out_ref):
    nz, nx, ny = view_ref.shape
    group = LANES // nz
    slot = lax.broadcasted_iota(jnp.int32, (8, LANES), 1) // group

    def tile(step, carry):
        t, at = step // (nx // 8), pl.ds(pl.multiple_of(step % (nx // 8) * 8, 8), 8)
        parts = [view_ref[z, at, lanes_at(t)] for z in range(nz)]
        span = nz // 2
        while span:
            odd = (slot & span) != 0
            for z in range(nz):
                if not z & span:
                    one, two = parts[z], parts[z + span]
                    parts[z] = jnp.where(odd, pltpu.roll(two, group * span, 1), one)
                    parts[z + span] = jnp.where(odd, two, pltpu.roll(one, LANES - group * span, 1))
            span //= 2
        for z in range(nz):
            out_ref[t * nz + z, at, :] = parts[z]
        return carry

    lax.fori_loop(0, ny // LANES * (nx // 8), tile, 0, unroll=True)


def unpack_body(arrived_ref, *out_refs):
    count, nx = arrived_ref.shape[0], arrived_ref.shape[1]
    nz, ny = out_refs[0].shape[1], out_refs[0].shape[0]
    flat = arrived_ref[...].reshape(count * nx, LANES)
    for j in range(count * nx // LANES):
        lanes = slice(j * LANES, (j + 1) * LANES)
        turned = jnp.swapaxes(flat[lanes].T.reshape(nz, ny, LANES), 0, 1)
        for y in range(ny):
            put(out_refs, y, slice(None), lanes, turned[y])


def reframe(view, margin):
    nz, nx, ny = view.shape
    count = lax.axis_size("row")
    rows = ny // count
    (pieces,) = call(pack_body, (view,), [local(count, nx, rows * nz)])
    arrived = lax.all_to_all(pieces, "row", 0, 0, tiled=True)
    shapes = [local(rows, nz, count * nx), local(margin, nz, count * nx), local(margin, nz, count * nx)]
    return call(unpack_body, (arrived,), shapes)


def per_device(view_a, view_b, estimate, axial_kernel, lateral_kernel):
    margin_a, margin = axial_kernel.shape[1] // 2, lateral_kernel.shape[2] // 2
    seen_a = jnp.swapaxes(view_a, 0, 1)
    seen_b = exchange(reframe(view_b, margin), "row")
    ytaps, ztaps, bands = prepare(axial_kernel, lateral_kernel)
    (ahead,) = first(lateral_kernel, estimate, margin)
    steps = 2 * ITERS
    for step in range(steps):
        v = step % 2
        yt, zt = ytaps[v], ztaps[v]
        ahead = depth(zt, *exchange(ahead, "col"), False, 2 * margin if v else margin_a)
        if v:
            ahead = deep(yt, exchange(ahead, "row"), seen_b, margin)
        else:
            ahead = plane(yt, *exchange(ahead, "row"), False, margin_a, seen_a)
            ahead = plane(yt, *exchange(ahead, "row"), True, margin)
        halo = exchange(ahead, "col")
        if step == steps - 1:
            estimate, _ = update(zt, [halo], bands[v][1], estimate)
        else:
            estimate, (ahead,) = update(zt, [halo], bands[v][1], estimate, bands[1 - v][0])
    return estimate


def solution(mesh):
    in_specs = (P("col", "row", None), P("col", "row", None), P("col", "row", None), P(), P())
    out_specs = P("col", "row", None)
    return jax.shard_map(
        per_device, mesh=mesh, in_specs=in_specs, out_specs=out_specs, check_vma=False
    )
```

profile of v0, /device:TPU:115, one launch (start us, length us, event | category | flops | bytes accessed | tf_op | source)
XLA Modules:
  0.0 261.0 jit_solution(3940444485396337635)
XLA Ops:
  0.0 1.0 copy-done
  1.7 1.5 first.1
  3.2 2.4 collective-permute-start
  5.7 3.7 %collective-permute-start.1 = (f32[5,16,768]{2,1,0:T(8,128)S(1)}, f32[5,16,768]{2,1,0:T(8,128)S(1)}, u32[]{:S(2)}, u32[]{:S(2)}) collective-permute-start(f32[5,16,768]{2,1,0:T(8,128)S(1)} %get-tuple-element.68), channel_id=1, source_target_pairs={{1,0},{2,1},{3,2},{4,3},{5,4},{6,5},{7,6},{8,7},{9,8},{10,9},{11,1... | collective-permute-start | bytes 737288 | tf_op jit(solution)/shard_map/ppermute | solution.py:327
  9.5 1.6 prepare.1
  11.0 3.7 %collective-permute-done.low_ref = f32[5,16,768]{2,1,0:T(8,128)S(1)} collective-permute-done((f32[5,16,768]{2,1,0:T(8,128)S(1)}, f32[5,16,768]{2,1,0:T(8,128)S(1)}, u32[]{:S(2)}, u32[]{:S(2)}) %collective-permute-start) | collective-permute-done | bytes 245792 | tf_op jit(solution)/shard_map/ppermute | solution.py:326
  14.8 7.8 %collective-permute-done.1.high_ref = f32[5,16,768]{2,1,0:T(8,128)S(1)} collective-permute-done((f32[5,16,768]{2,1,0:T(8,128)S(1)}, f32[5,16,768]{2,1,0:T(8,128)S(1)}, u32[]{:S(2)}, u32[]{:S(2)}) %collective-permute-start.1) | collective-permute-done | bytes 245792 | tf_op jit(solution)/shard_map/ppermute | solution.py:327
  23.0 1.9 collective-permute-start.2
  25.0 3.5 %collective-permute-start.3 = (f32[15,8,768]{2,1,0:T(8,128)S(1)}, f32[15,8,768]{2,1,0:T(8,128)S(1)}, u32[]{:S(2)}, u32[]{:S(2)}) collective-permute-start(f32[15,8,768]{2,1,0:T(8,128)S(1)} %get-tuple-element.71), channel_id=1, source_target_pairs={{16,0},{32,16},{48,32},{64,48},{80,64},{96,80},{112,96},{128,112},... | collective-permute-start | bytes 1105928 | tf_op jit(solution)/shard_map/ppermute | solution.py:327
  29.4 7.7 %collective-permute-done.3.high_ref = f32[15,8,768]{2,1,0:T(8,128)S(1)} collective-permute-done((f32[15,8,768]{2,1,0:T(8,128)S(1)}, f32[15,8,768]{2,1,0:T(8,128)S(1)}, u32[]{:S(2)}, u32[]{:S(2)}) %collective-permute-start.3) | collective-permute-done | bytes 368672 | tf_op jit(solution)/shard_map/ppermute | solution.py:327
  37.1 1.8 shard_map.56
  38.9 1.9 collective-permute-start.4
  40.8 2.4 collective-permute-start.5
  43.2 1.7 shard_map.60
  44.9 13.4 %all-to-all-start = ((f32[32,24,128]{2,1,0:T(8,128)}), f32[32,24,128]{2,1,0:T(8,128)S(1)}, u32[]{:S(2)}, u32[]{:S(2)}) async-start(f32[32,24,128]{2,1,0:T(8,128)} %shard_map.60), calls=%async_computation | async-start | bytes 786432 | tf_op jit(solution)/shard_map/all_to_all | solution.py:371
  58.4 0.9 shard_map.57
  59.3 4.3 %collective-permute-start.6 = (f32[5,16,768]{2,1,0:T(8,128)S(1)}, f32[5,16,768]{2,1,0:T(8,128)S(1)}, u32[]{:S(2)}, u32[]{:S(2)}) collective-permute-start(f32[5,16,768]{2,1,0:T(8,128)S(1)} %get-tuple-element.75), channel_id=1, source_target_pairs={{0,1},{1,2},{2,3},{3,4},{4,5},{5,6},{6,7},{7,8},{8,9},{9,10},{10,1... | collective-permute-start | bytes 737288 | tf_op jit(solution)/shard_map/ppermute | solution.py:326
  63.6 1.9 collective-permute-start.7
  65.5 6.1 %collective-permute-done.6.refs_0_ = f32[5,16,768]{2,1,0:T(8,128)S(1)} collective-permute-done((f32[5,16,768]{2,1,0:T(8,128)S(1)}, f32[5,16,768]{2,1,0:T(8,128)S(1)}, u32[]{:S(2)}, u32[]{:S(2)}) %collective-permute-start.6) | collective-permute-done | bytes 245792 | tf_op jit(solution)/shard_map/ppermute | solution.py:326
  71.7 6.3 %collective-permute-done.7.refs_2_ = f32[5,16,768]{2,1,0:T(8,128)S(1)} collective-permute-done((f32[5,16,768]{2,1,0:T(8,128)S(1)}, f32[5,16,768]{2,1,0:T(8,128)S(1)}, u32[]{:S(2)}, u32[]{:S(2)}) %collective-permute-start.7) | collective-permute-done | bytes 245792 | tf_op jit(solution)/shard_map/ppermute | solution.py:327
  78.0 1.8 shard_map.58
  79.8 3.2 %collective-permute-start.8 = (f32[5,16,768]{2,1,0:T(8,128)S(1)}, f32[5,16,768]{2,1,0:T(8,128)S(1)}, u32[]{:S(2)}, u32[]{:S(2)}) collective-permute-start(f32[5,16,768]{2,1,0:T(8,128)S(1)} %get-tuple-element.81), channel_id=1, source_target_pairs={{0,1},{1,2},{2,3},{3,4},{4,5},{5,6},{6,7},{7,8},{8,9},{9,10},{10,1... | collective-permute-start | bytes 737288 | tf_op jit(solution)/shard_map/ppermute | solution.py:326
  83.0 3.0 %collective-permute-start.9 = (f32[5,16,768]{2,1,0:T(8,128)S(1)}, f32[5,16,768]{2,1,0:T(8,128)S(1)}, u32[]{:S(2)}, u32[]{:S(2)}) collective-permute-start(f32[5,16,768]{2,1,0:T(8,128)S(1)} %get-tuple-element.83), channel_id=1, source_target_pairs={{1,0},{2,1},{3,2},{4,3},{5,4},{6,5},{7,6},{8,7},{9,8},{10,9},{11,1... | collective-permute-start | bytes 737288 | tf_op jit(solution)/shard_map/ppermute | solution.py:327
  86.0 8.4 %collective-permute-done.8.low_ref = f32[5,16,768]{2,1,0:T(8,128)S(1)} collective-permute-done((f32[5,16,768]{2,1,0:T(8,128)S(1)}, f32[5,16,768]{2,1,0:T(8,128)S(1)}, u32[]{:S(2)}, u32[]{:S(2)}) %collective-permute-start.8) | collective-permute-done | bytes 245792 | tf_op jit(solution)/shard_map/ppermute | solution.py:326
  94.8 11.4 %collective-permute-start.10 = (f32[10,8,768]{2,1,0:T(8,128)S(1)}, f32[10,8,768]{2,1,0:T(8,128)S(1)}, u32[]{:S(2)}, u32[]{:S(2)}) collective-permute-start(f32[10,8,768]{2,1,0:T(8,128)S(1)} %get-tuple-element.84), channel_id=1, source_target_pairs={{0,16},{16,32},{32,48},{48,64},{64,80},{80,96},{96,112},{112,128},... | collective-permute-start | bytes 737288 | tf_op jit(solution)/shard_map/ppermute | solution.py:326
  106.2 1.9 collective-permute-start.11
  108.3 3.6 %collective-permute-start.12 = (f32[5,8,768]{2,1,0:T(8,128)S(1)}, f32[5,8,768]{2,1,0:T(8,128)S(1)}, u32[]{:S(2)}, u32[]{:S(2)}) collective-permute-start(f32[5,8,768]{2,1,0:T(8,128)S(1)} %get-tuple-element.87), channel_id=1, source_target_pairs={{0,16},{16,32},{32,48},{48,64},{64,80},{80,96},{96,112},{112,128},... | collective-permute-start | bytes 368648 | tf_op jit(solution)/shard_map/ppermute | solution.py:326
  112.0 1.9 collective-permute-start.13
  113.9 4.3 %collective-permute-done.13.view_high_ref = f32[5,8,768]{2,1,0:T(8,128)S(1)} collective-permute-done((f32[5,8,768]{2,1,0:T(8,128)S(1)}, f32[5,8,768]{2,1,0:T(8,128)S(1)}, u32[]{:S(2)}, u32[]{:S(2)}) %collective-permute-start.13) | collective-permute-done | bytes 122912 | tf_op jit(solution)/shard_map/ppermute | solution.py:327
  119.1 1.9 collective-permute-start.14
  121.0 4.3 %collective-permute-start.15 = (f32[5,16,768]{2,1,0:T(8,128)S(1)}, f32[5,16,768]{2,1,0:T(8,128)S(1)}, u32[]{:S(2)}, u32[]{:S(2)}) collective-permute-start(f32[5,16,768]{2,1,0:T(8,128)S(1)} %get-tuple-element.92), channel_id=1, source_target_pairs={{1,0},{2,1},{3,2},{4,3},{5,4},{6,5},{7,6},{8,7},{9,8},{10,9},{11,1... | collective-permute-start | bytes 737288 | tf_op jit(solution)/shard_map/ppermute | solution.py:327
  125.3 2.3 collective-permute-done.14.refs_0_
  127.6 10.7 %collective-permute-done.15.refs_2_ = f32[5,16,768]{2,1,0:T(8,128)S(1)} collective-permute-done((f32[5,16,768]{2,1,0:T(8,128)S(1)}, f32[5,16,768]{2,1,0:T(8,128)S(1)}, u32[]{:S(2)}, u32[]{:S(2)}) %collective-permute-start.15) | collective-permute-done | bytes 245792 | tf_op jit(solution)/shard_map/ppermute | solution.py:327
  138.3 1.8 shard_map.63
  140.0 1.9 collective-permute-start.16
  142.0 4.3 %collective-permute-start.17 = (f32[5,16,768]{2,1,0:T(8,128)S(1)}, f32[5,16,768]{2,1,0:T(8,128)S(1)}, u32[]{:S(2)}, u32[]{:S(2)}) collective-permute-start(f32[5,16,768]{2,1,0:T(8,128)S(1)} %get-tuple-element.97), channel_id=1, source_target_pairs={{1,0},{2,1},{3,2},{4,3},{5,4},{6,5},{7,6},{8,7},{9,8},{10,9},{11,1... | collective-permute-start | bytes 737288 | tf_op jit(solution)/shard_map/ppermute | solution.py:327
  146.2 6.9 %collective-permute-done.16.low_ref = f32[5,16,768]{2,1,0:T(8,128)S(1)} collective-permute-done((f32[5,16,768]{2,1,0:T(8,128)S(1)}, f32[5,16,768]{2,1,0:T(8,128)S(1)}, u32[]{:S(2)}, u32[]{:S(2)}) %collective-permute-start.16) | collective-permute-done | bytes 245792 | tf_op jit(solution)/shard_map/ppermute | solution.py:326
  153.1 1.7 collective-permute-done.17.high_ref
  155.3 5.4 %collective-permute-start.18 = (f32[15,8,768]{2,1,0:T(8,128)S(1)}, f32[15,8,768]{2,1,0:T(8,128)S(1)}, u32[]{:S(2)}, u32[]{:S(2)}) collective-permute-start(f32[15,8,768]{2,1,0:T(8,128)S(1)} %get-tuple-element.98), channel_id=1, source_target_pairs={{0,16},{16,32},{32,48},{48,64},{64,80},{80,96},{96,112},{112,128},... | collective-permute-start | bytes 1105928 | tf_op jit(solution)/shard_map/ppermute | solution.py:326
  160.6 1.9 collective-permute-start.19
  162.6 6.2 %collective-permute-done.18.low_ref = f32[15,8,768]{2,1,0:T(8,128)S(1)} collective-permute-done((f32[15,8,768]{2,1,0:T(8,128)S(1)}, f32[15,8,768]{2,1,0:T(8,128)S(1)}, u32[]{:S(2)}, u32[]{:S(2)}) %collective-permute-start.18) | collective-permute-done | bytes 368672 | tf_op jit(solution)/shard_map/ppermute | solution.py:326
  168.8 4.1 %collective-permute-done.19.high_ref = f32[15,8,768]{2,1,0:T(8,128)S(1)} collective-permute-done((f32[15,8,768]{2,1,0:T(8,128)S(1)}, f32[15,8,768]{2,1,0:T(8,128)S(1)}, u32[]{:S(2)}, u32[]{:S(2)}) %collective-permute-start.19) | collective-permute-done | bytes 368672 | tf_op jit(solution)/shard_map/ppermute | solution.py:327
  172.9 1.0 shard_map.65
  173.9 1.9 collective-permute-start.20
  175.9 2.4 collective-permute-start.21
  178.3 3.4 %collective-permute-done.20.low_ref = f32[15,8,768]{2,1,0:T(8,128)S(1)} collective-permute-done((f32[15,8,768]{2,1,0:T(8,128)S(1)}, f32[15,8,768]{2,1,0:T(8,128)S(1)}, u32[]{:S(2)}, u32[]{:S(2)}) %collective-permute-start.20) | collective-permute-done | bytes 368672 | tf_op jit(solution)/shard_map/ppermute | solution.py:326
  181.7 5.5 %collective-permute-done.21.high_ref = f32[15,8,768]{2,1,0:T(8,128)S(1)} collective-permute-done((f32[15,8,768]{2,1,0:T(8,128)S(1)}, f32[15,8,768]{2,1,0:T(8,128)S(1)}, u32[]{:S(2)}, u32[]{:S(2)}) %collective-permute-start.21) | collective-permute-done | bytes 368672 | tf_op jit(solution)/shard_map/ppermute | solution.py:327
  188.1 1.9 collective-permute-start.22
  190.0 4.3 %collective-permute-start.23 = (f32[5,16,768]{2,1,0:T(8,128)S(1)}, f32[5,16,768]{2,1,0:T(8,128)S(1)}, u32[]{:S(2)}, u32[]{:S(2)}) collective-permute-start(f32[5,16,768]{2,1,0:T(8,128)S(1)} %get-tuple-element.106), channel_id=1, source_target_pairs={{1,0},{2,1},{3,2},{4,3},{5,4},{6,5},{7,6},{8,7},{9,8},{10,9},{11,1... | collective-permute-start | bytes 737288 | tf_op jit(solution)/shard_map/ppermute | solution.py:327
  194.3 3.2 %collective-permute-done.22.refs_0_ = f32[5,16,768]{2,1,0:T(8,128)S(1)} collective-permute-done((f32[5,16,768]{2,1,0:T(8,128)S(1)}, f32[5,16,768]{2,1,0:T(8,128)S(1)}, u32[]{:S(2)}, u32[]{:S(2)}) %collective-permute-start.22) | collective-permute-done | bytes 245792 | tf_op jit(solution)/shard_map/ppermute | solution.py:326
  197.5 5.8 %collective-permute-done.23.refs_2_ = f32[5,16,768]{2,1,0:T(8,128)S(1)} collective-permute-done((f32[5,16,768]{2,1,0:T(8,128)S(1)}, f32[5,16,768]{2,1,0:T(8,128)S(1)}, u32[]{:S(2)}, u32[]{:S(2)}) %collective-permute-start.23) | collective-permute-done | bytes 245792 | tf_op jit(solution)/shard_map/ppermute | solution.py:327
  203.3 1.8 shard_map.67
  205.1 2.9 %collective-permute-start.24 = (f32[5,16,768]{2,1,0:T(8,128)S(1)}, f32[5,16,768]{2,1,0:T(8,128)S(1)}, u32[]{:S(2)}, u32[]{:S(2)}) collective-permute-start(f32[5,16,768]{2,1,0:T(8,128)S(1)} %get-tuple-element.108), channel_id=1, source_target_pairs={{0,1},{1,2},{2,3},{3,4},{4,5},{5,6},{6,7},{7,8},{8,9},{9,10},{10,1... | collective-permute-start | bytes 737288 | tf_op jit(solution)/shard_map/ppermute | solution.py:326
  208.0 3.3 %collective-permute-start.25 = (f32[5,16,768]{2,1,0:T(8,128)S(1)}, f32[5,16,768]{2,1,0:T(8,128)S(1)}, u32[]{:S(2)}, u32[]{:S(2)}) collective-permute-start(f32[5,16,768]{2,1,0:T(8,128)S(1)} %get-tuple-element.110), channel_id=1, source_target_pairs={{1,0},{2,1},{3,2},{4,3},{5,4},{6,5},{7,6},{8,7},{9,8},{10,9},{11,1... | collective-permute-start | bytes 737288 | tf_op jit(solution)/shard_map/ppermute | solution.py:327
  211.3 9.6 %collective-permute-done.24.low_ref = f32[5,16,768]{2,1,0:T(8,128)S(1)} collective-permute-done((f32[5,16,768]{2,1,0:T(8,128)S(1)}, f32[5,16,768]{2,1,0:T(8,128)S(1)}, u32[]{:S(2)}, u32[]{:S(2)}) %collective-permute-start.24) | collective-permute-done | bytes 245792 | tf_op jit(solution)/shard_map/ppermute | solution.py:326
  221.3 7.4 %collective-permute-start.26 = (f32[10,8,768]{2,1,0:T(8,128)S(1)}, f32[10,8,768]{2,1,0:T(8,128)S(1)}, u32[]{:S(2)}, u32[]{:S(2)}) collective-permute-start(f32[10,8,768]{2,1,0:T(8,128)S(1)} %get-tuple-element.111), channel_id=1, source_target_pairs={{0,16},{16,32},{32,48},{48,64},{64,80},{80,96},{96,112},{112,128},... | collective-permute-start | bytes 737288 | tf_op jit(solution)/shard_map/ppermute | solution.py:326
  228.7 2.1 collective-permute-start.27
  230.8 1.0 collective-permute-done.26.low_ref
  231.8 4.4 %collective-permute-done.27.high_ref = f32[10,8,768]{2,1,0:T(8,128)S(1)} collective-permute-done((f32[10,8,768]{2,1,0:T(8,128)S(1)}, f32[10,8,768]{2,1,0:T(8,128)S(1)}, u32[]{:S(2)}, u32[]{:S(2)}) %collective-permute-start.27) | collective-permute-done | bytes 245792 | tf_op jit(solution)/shard_map/ppermute | solution.py:327
  237.1 4.8 %collective-permute-start.28 = (f32[5,16,768]{2,1,0:T(8,128)S(1)}, f32[5,16,768]{2,1,0:T(8,128)S(1)}, u32[]{:S(2)}, u32[]{:S(2)}) collective-permute-start(f32[5,16,768]{2,1,0:T(8,128)S(1)} %get-tuple-element.114), channel_id=1, source_target_pairs={{0,1},{1,2},{2,3},{3,4},{4,5},{5,6},{6,7},{7,8},{8,9},{9,10},{10,1... | collective-permute-start | bytes 737288 | tf_op jit(solution)/shard_map/ppermute | solution.py:326
  241.9 1.9 collective-permute-start.29
  243.8 8.1 %collective-permute-done.28.refs_0_ = f32[5,16,768]{2,1,0:T(8,128)S(1)} collective-permute-done((f32[5,16,768]{2,1,0:T(8,128)S(1)}, f32[5,16,768]{2,1,0:T(8,128)S(1)}, u32[]{:S(2)}, u32[]{:S(2)}) %collective-permute-start.28) | collective-permute-done | bytes 245792 | tf_op jit(solution)/shard_map/ppermute | solution.py:326
  251.9 7.2 %collective-permute-done.29.refs_2_ = f32[5,16,768]{2,1,0:T(8,128)S(1)} collective-permute-done((f32[5,16,768]{2,1,0:T(8,128)S(1)}, f32[5,16,768]{2,1,0:T(8,128)S(1)}, u32[]{:S(2)}, u32[]{:S(2)}) %collective-permute-start.29) | collective-permute-done | bytes 245792 | tf_op jit(solution)/shard_map/ppermute | solution.py:327
  259.1 1.9 shard_map.70
  (31 shorter events, 6.2 us)
Async XLA Ops:
  0.0 1.0 copy-start
  1.0 0.7 copy-start.3
  3.2 6.2 %copy-start.4 = (f32[2,2,11]{2,1,0:T(2,128)S(1)}, f32[2,2,11]{2,1,0:T(2,128)}, u32[]{:S(2)}) copy-start(f32[2,2,11]{2,1,0:T(2,128)} %lateral_ref.3) | copy-start | bytes 532
  3.2 6.2 %copy-start.5 = (f32[2,31]{1,0:T(2,128)S(1)}, f32[2,31]{1,0:T(2,128)}, u32[]{:S(2)}) copy-start(f32[2,31]{1,0:T(2,128)} %axial_ref.1) | copy-start | bytes 748
  3.2 11.5 %collective-permute-start = (f32[5,16,768]{2,1,0:T(8,128)S(1)}, f32[5,16,768]{2,1,0:T(8,128)S(1)}, u32[]{:S(2)}, u32[]{:S(2)}) collective-permute-start(f32[5,16,768]{2,1,0:T(8,128)S(1)} %get-tuple-element.66), channel_id=1, source_target_pairs={{0,1},{1,2},{2,3},{3,4},{4,5},{5,6},{6,7},{7,8},{8,9},{9,10},{10,1... | collective-permute-start | bytes 737288 | tf_op jit(solution)/shard_map/ppermute | solution.py:326
  5.7 16.9 %collective-permute-start.1 = (f32[5,16,768]{2,1,0:T(8,128)S(1)}, f32[5,16,768]{2,1,0:T(8,128)S(1)}, u32[]{:S(2)}, u32[]{:S(2)}) collective-permute-start(f32[5,16,768]{2,1,0:T(8,128)S(1)} %get-tuple-element.68), channel_id=1, source_target_pairs={{1,0},{2,1},{3,2},{4,3},{5,4},{6,5},{7,6},{8,7},{9,8},{10,9},{11,1... | collective-permute-start | bytes 737288 | tf_op jit(solution)/shard_map/ppermute | solution.py:327
  22.6 5.9 %copy-start.6 = (f32[8,16,768]{2,1,0:T(8,128)S(1)}, f32[8,16,768]{2,1,0:T(8,128)}, u32[]{:S(2)}) copy-start(f32[8,16,768]{2,1,0:T(8,128)} %param.5) | copy-start | bytes 1179652
  23.0 6.4 %collective-permute-start.2 = (f32[15,8,768]{2,1,0:T(8,128)S(1)}, f32[15,8,768]{2,1,0:T(8,128)S(1)}, u32[]{:S(2)}, u32[]{:S(2)}) collective-permute-start(f32[15,8,768]{2,1,0:T(8,128)S(1)} %get-tuple-element.69), channel_id=1, source_target_pairs={{0,16},{16,32},{32,48},{48,64},{64,80},{80,96},{96,112},{112,128},... | collective-permute-start | bytes 1105928 | tf_op jit(solution)/shard_map/ppermute | solution.py:326
  25.0 12.2 %collective-permute-start.3 = (f32[15,8,768]{2,1,0:T(8,128)S(1)}, f32[15,8,768]{2,1,0:T(8,128)S(1)}, u32[]{:S(2)}, u32[]{:S(2)}) collective-permute-start(f32[15,8,768]{2,1,0:T(8,128)S(1)} %get-tuple-element.71), channel_id=1, source_target_pairs={{16,0},{32,16},{48,32},{64,48},{80,64},{96,80},{112,96},{128,112},... | collective-permute-start | bytes 1105928 | tf_op jit(solution)/shard_map/ppermute | solution.py:327
  37.1 6.1 %copy-start.2 = (f32[8,24,512]{2,1,0:T(8,128)S(1)}, f32[8,24,512]{2,1,0:T(8,128)}, u32[]{:S(2)}) copy-start(f32[8,24,512]{2,1,0:T(8,128)} %view_ref.1) | copy-start | bytes 1179652
  38.9 19.5 %collective-permute-start.4 = (f32[15,8,768]{2,1,0:T(8,128)}, f32[15,8,768]{2,1,0:T(8,128)S(1)}, u32[]{:S(2)}, u32[]{:S(2)}) collective-permute-start(f32[15,8,768]{2,1,0:T(8,128)} %get-tuple-element.72), channel_id=1, source_target_pairs={{0,16},{16,32},{32,48},{48,64},{64,80},{80,96},{96,112},{112,128},... | collective-permute-start | bytes 1105928 | tf_op jit(solution)/shard_map/ppermute | solution.py:326
  40.8 17.5 %collective-permute-start.5 = (f32[15,8,768]{2,1,0:T(8,128)S(1)}, f32[15,8,768]{2,1,0:T(8,128)S(1)}, u32[]{:S(2)}, u32[]{:S(2)}) collective-permute-start(f32[15,8,768]{2,1,0:T(8,128)S(1)} %get-tuple-element.74), channel_id=1, source_target_pairs={{16,0},{32,16},{48,32},{64,48},{80,64},{96,80},{112,96},{128,112},... | collective-permute-start | bytes 1105928 | tf_op jit(solution)/shard_map/ppermute | solution.py:327
  44.9 63.2 %all-to-all-start = ((f32[32,24,128]{2,1,0:T(8,128)}), f32[32,24,128]{2,1,0:T(8,128)S(1)}, u32[]{:S(2)}, u32[]{:S(2)}) async-start(f32[32,24,128]{2,1,0:T(8,128)} %shard_map.60), calls=%async_computation | async-start | bytes 786432 | tf_op jit(solution)/shard_map/all_to_all | solution.py:371
  58.4 19.6 %copy-start.1 = (f32[8,16,768]{2,1,0:T(8,128)S(1)}, f32[8,16,768]{2,1,0:T(8,128)}, u32[]{:S(2)}) copy-start(f32[8,16,768]{2,1,0:T(8,128)} %estimate_ref.3) | copy-start | bytes 1179652
  59.3 12.4 %collective-permute-start.6 = (f32[5,16,768]{2,1,0:T(8,128)S(1)}, f32[5,16,768]{2,1,0:T(8,128)S(1)}, u32[]{:S(2)}, u32[]{:S(2)}) collective-permute-start(f32[5,16,768]{2,1,0:T(8,128)S(1)} %get-tuple-element.75), channel_id=1, source_target_pairs={{0,1},{1,2},{2,3},{3,4},{4,5},{5,6},{6,7},{7,8},{8,9},{9,10},{10,1... | collective-permute-start | bytes 737288 | tf_op jit(solution)/shard_map/ppermute | solution.py:326
  63.6 14.4 %collective-permute-start.7 = (f32[5,16,768]{2,1,0:T(8,128)S(1)}, f32[5,16,768]{2,1,0:T(8,128)S(1)}, u32[]{:S(2)}, u32[]{:S(2)}) collective-permute-start(f32[5,16,768]{2,1,0:T(8,128)S(1)} %get-tuple-element.77), channel_id=1, source_target_pairs={{1,0},{2,1},{3,2},{4,3},{5,4},{6,5},{7,6},{8,7},{9,8},{10,9},{11,1... | collective-permute-start | bytes 737288 | tf_op jit(solution)/shard_map/ppermute | solution.py:327
  79.8 14.6 %collective-permute-start.8 = (f32[5,16,768]{2,1,0:T(8,128)S(1)}, f32[5,16,768]{2,1,0:T(8,128)S(1)}, u32[]{:S(2)}, u32[]{:S(2)}) collective-permute-start(f32[5,16,768]{2,1,0:T(8,128)S(1)} %get-tuple-element.81), channel_id=1, source_target_pairs={{0,1},{1,2},{2,3},{3,4},{4,5},{5,6},{6,7},{7,8},{8,9},{9,10},{10,1... | collective-permute-start | bytes 737288 | tf_op jit(solution)/shard_map/ppermute | solution.py:326
  83.0 11.4 %collective-permute-start.9 = (f32[5,16,768]{2,1,0:T(8,128)S(1)}, f32[5,16,768]{2,1,0:T(8,128)S(1)}, u32[]{:S(2)}, u32[]{:S(2)}) collective-permute-start(f32[5,16,768]{2,1,0:T(8,128)S(1)} %get-tuple-element.83), channel_id=1, source_target_pairs={{1,0},{2,1},{3,2},{4,3},{5,4},{6,5},{7,6},{8,7},{9,8},{10,9},{11,1... | collective-permute-start | bytes 737288 | tf_op jit(solution)/shard_map/ppermute | solution.py:327
  94.8 23.4 %collective-permute-start.10 = (f32[10,8,768]{2,1,0:T(8,128)S(1)}, f32[10,8,768]{2,1,0:T(8,128)S(1)}, u32[]{:S(2)}, u32[]{:S(2)}) collective-permute-start(f32[10,8,768]{2,1,0:T(8,128)S(1)} %get-tuple-element.84), channel_id=1, source_target_pairs={{0,16},{16,32},{32,48},{48,64},{64,80},{80,96},{96,112},{112,128},... | collective-permute-start | bytes 737288 | tf_op jit(solution)/shard_map/ppermute | solution.py:326
  106.2 12.0 %collective-permute-start.11 = (f32[10,8,768]{2,1,0:T(8,128)S(1)}, f32[10,8,768]{2,1,0:T(8,128)S(1)}, u32[]{:S(2)}, u32[]{:S(2)}) collective-permute-start(f32[10,8,768]{2,1,0:T(8,128)S(1)} %get-tuple-element.86), channel_id=1, source_target_pairs={{16,0},{32,16},{48,32},{64,48},{80,64},{96,80},{112,96},{128,112},... | collective-permute-start | bytes 737288 | tf_op jit(solution)/shard_map/ppermute | solution.py:327
  108.3 5.6 %collective-permute-start.12 = (f32[5,8,768]{2,1,0:T(8,128)S(1)}, f32[5,8,768]{2,1,0:T(8,128)S(1)}, u32[]{:S(2)}, u32[]{:S(2)}) collective-permute-start(f32[5,8,768]{2,1,0:T(8,128)S(1)} %get-tuple-element.87), channel_id=1, source_target_pairs={{0,16},{16,32},{32,48},{48,64},{64,80},{80,96},{96,112},{112,128},... | collective-permute-start | bytes 368648 | tf_op jit(solution)/shard_map/ppermute | solution.py:326
  112.0 6.2 %collective-permute-start.13 = (f32[5,8,768]{2,1,0:T(8,128)S(1)}, f32[5,8,768]{2,1,0:T(8,128)S(1)}, u32[]{:S(2)}, u32[]{:S(2)}) collective-permute-start(f32[5,8,768]{2,1,0:T(8,128)S(1)} %get-tuple-element.89), channel_id=1, source_target_pairs={{16,0},{32,16},{48,32},{64,48},{80,64},{96,80},{112,96},{128,112},... | collective-permute-start | bytes 368648 | tf_op jit(solution)/shard_map/ppermute | solution.py:327
  119.1 8.5 %collective-permute-start.14 = (f32[5,16,768]{2,1,0:T(8,128)S(1)}, f32[5,16,768]{2,1,0:T(8,128)S(1)}, u32[]{:S(2)}, u32[]{:S(2)}) collective-permute-start(f32[5,16,768]{2,1,0:T(8,128)S(1)} %get-tuple-element.90), channel_id=1, source_target_pairs={{0,1},{1,2},{2,3},{3,4},{4,5},{5,6},{6,7},{7,8},{8,9},{9,10},{10,1... | collective-permute-start | bytes 737288 | tf_op jit(solution)/shard_map/ppermute | solution.py:326
  121.0 17.2 %collective-permute-start.15 = (f32[5,16,768]{2,1,0:T(8,128)S(1)}, f32[5,16,768]{2,1,0:T(8,128)S(1)}, u32[]{:S(2)}, u32[]{:S(2)}) collective-permute-start(f32[5,16,768]{2,1,0:T(8,128)S(1)} %get-tuple-element.92), channel_id=1, source_target_pairs={{1,0},{2,1},{3,2},{4,3},{5,4},{6,5},{7,6},{8,7},{9,8},{10,9},{11,1... | collective-permute-start | bytes 737288 | tf_op jit(solution)/shard_map/ppermute | solution.py:327
  140.0 13.1 %collective-permute-start.16 = (f32[5,16,768]{2,1,0:T(8,128)S(1)}, f32[5,16,768]{2,1,0:T(8,128)S(1)}, u32[]{:S(2)}, u32[]{:S(2)}) collective-permute-start(f32[5,16,768]{2,1,0:T(8,128)S(1)} %get-tuple-element.95), channel_id=1, source_target_pairs={{0,1},{1,2},{2,3},{3,4},{4,5},{5,6},{6,7},{7,8},{8,9},{9,10},{10,1... | collective-permute-start | bytes 737288 | tf_op jit(solution)/shard_map/ppermute | solution.py:326
  142.0 12.9 %collective-permute-start.17 = (f32[5,16,768]{2,1,0:T(8,128)S(1)}, f32[5,16,768]{2,1,0:T(8,128)S(1)}, u32[]{:S(2)}, u32[]{:S(2)}) collective-permute-start(f32[5,16,768]{2,1,0:T(8,128)S(1)} %get-tuple-element.97), channel_id=1, source_target_pairs={{1,0},{2,1},{3,2},{4,3},{5,4},{6,5},{7,6},{8,7},{9,8},{10,9},{11,1... | collective-permute-start | bytes 737288 | tf_op jit(solution)/shard_map/ppermute | solution.py:327
  155.3 13.5 %collective-permute-start.18 = (f32[15,8,768]{2,1,0:T(8,128)S(1)}, f32[15,8,768]{2,1,0:T(8,128)S(1)}, u32[]{:S(2)}, u32[]{:S(2)}) collective-permute-start(f32[15,8,768]{2,1,0:T(8,128)S(1)} %get-tuple-element.98), channel_id=1, source_target_pairs={{0,16},{16,32},{32,48},{48,64},{64,80},{80,96},{96,112},{112,128},... | collective-permute-start | bytes 1105928 | tf_op jit(solution)/shard_map/ppermute | solution.py:326
  160.6 12.3 %collective-permute-start.19 = (f32[15,8,768]{2,1,0:T(8,128)S(1)}, f32[15,8,768]{2,1,0:T(8,128)S(1)}, u32[]{:S(2)}, u32[]{:S(2)}) collective-permute-start(f32[15,8,768]{2,1,0:T(8,128)S(1)} %get-tuple-element.100), channel_id=1, source_target_pairs={{16,0},{32,16},{48,32},{64,48},{80,64},{96,80},{112,96},{128,112},... | collective-permute-start | bytes 1105928 | tf_op jit(solution)/shard_map/ppermute | solution.py:327
  173.9 7.7 %collective-permute-start.20 = (f32[15,8,768]{2,1,0:T(8,128)S(1)}, f32[15,8,768]{2,1,0:T(8,128)S(1)}, u32[]{:S(2)}, u32[]{:S(2)}) collective-permute-start(f32[15,8,768]{2,1,0:T(8,128)S(1)} %get-tuple-element.101), channel_id=1, source_target_pairs={{0,16},{16,32},{32,48},{48,64},{64,80},{80,96},{96,112},{112,128},... | collective-permute-start | bytes 1105928 | tf_op jit(solution)/shard_map/ppermute | solution.py:326
  175.9 11.3 %collective-permute-start.21 = (f32[15,8,768]{2,1,0:T(8,128)S(1)}, f32[15,8,768]{2,1,0:T(8,128)S(1)}, u32[]{:S(2)}, u32[]{:S(2)}) collective-permute-start(f32[15,8,768]{2,1,0:T(8,128)S(1)} %get-tuple-element.103), channel_id=1, source_target_pairs={{16,0},{32,16},{48,32},{64,48},{80,64},{96,80},{112,96},{128,112},... | collective-permute-start | bytes 1105928 | tf_op jit(solution)/shard_map/ppermute | solution.py:327
  188.1 9.4 %collective-permute-start.22 = (f32[5,16,768]{2,1,0:T(8,128)S(1)}, f32[5,16,768]{2,1,0:T(8,128)S(1)}, u32[]{:S(2)}, u32[]{:S(2)}) collective-permute-start(f32[5,16,768]{2,1,0:T(8,128)S(1)} %get-tuple-element.104), channel_id=1, source_target_pairs={{0,1},{1,2},{2,3},{3,4},{4,5},{5,6},{6,7},{7,8},{8,9},{9,10},{10,1... | collective-permute-start | bytes 737288 | tf_op jit(solution)/shard_map/ppermute | solution.py:326
  190.0 13.3 %collective-permute-start.23 = (f32[5,16,768]{2,1,0:T(8,128)S(1)}, f32[5,16,768]{2,1,0:T(8,128)S(1)}, u32[]{:S(2)}, u32[]{:S(2)}) collective-permute-start(f32[5,16,768]{2,1,0:T(8,128)S(1)} %get-tuple-element.106), channel_id=1, source_target_pairs={{1,0},{2,1},{3,2},{4,3},{5,4},{6,5},{7,6},{8,7},{9,8},{10,9},{11,1... | collective-permute-start | bytes 737288 | tf_op jit(solution)/shard_map/ppermute | solution.py:327
  205.1 15.8 %collective-permute-start.24 = (f32[5,16,768]{2,1,0:T(8,128)S(1)}, f32[5,16,768]{2,1,0:T(8,128)S(1)}, u32[]{:S(2)}, u32[]{:S(2)}) collective-permute-start(f32[5,16,768]{2,1,0:T(8,128)S(1)} %get-tuple-element.108), channel_id=1, source_target_pairs={{0,1},{1,2},{2,3},{3,4},{4,5},{5,6},{6,7},{7,8},{8,9},{9,10},{10,1... | collective-permute-start | bytes 737288 | tf_op jit(solution)/shard_map/ppermute | solution.py:326
  208.0 12.9 %collective-permute-start.25 = (f32[5,16,768]{2,1,0:T(8,128)S(1)}, f32[5,16,768]{2,1,0:T(8,128)S(1)}, u32[]{:S(2)}, u32[]{:S(2)}) collective-permute-start(f32[5,16,768]{2,1,0:T(8,128)S(1)} %get-tuple-element.110), channel_id=1, source_target_pairs={{1,0},{2,1},{3,2},{4,3},{5,4},{6,5},{7,6},{8,7},{9,8},{10,9},{11,1... | collective-permute-start | bytes 737288 | tf_op jit(solution)/shard_map/ppermute | solution.py:327
  221.3 10.5 %collective-permute-start.26 = (f32[10,8,768]{2,1,0:T(8,128)S(1)}, f32[10,8,768]{2,1,0:T(8,128)S(1)}, u32[]{:S(2)}, u32[]{:S(2)}) collective-permute-start(f32[10,8,768]{2,1,0:T(8,128)S(1)} %get-tuple-element.111), channel_id=1, source_target_pairs={{0,16},{16,32},{32,48},{48,64},{64,80},{80,96},{96,112},{112,128},... | collective-permute-start | bytes 737288 | tf_op jit(solution)/shard_map/ppermute | solution.py:326
  228.7 7.5 %collective-permute-start.27 = (f32[10,8,768]{2,1,0:T(8,128)S(1)}, f32[10,8,768]{2,1,0:T(8,128)S(1)}, u32[]{:S(2)}, u32[]{:S(2)}) collective-permute-start(f32[10,8,768]{2,1,0:T(8,128)S(1)} %get-tuple-element.113), channel_id=1, source_target_pairs={{16,0},{32,16},{48,32},{64,48},{80,64},{96,80},{112,96},{128,112},... | collective-permute-start | bytes 737288 | tf_op jit(solution)/shard_map/ppermute | solution.py:327
  237.1 14.8 %collective-permute-start.28 = (f32[5,16,768]{2,1,0:T(8,128)S(1)}, f32[5,16,768]{2,1,0:T(8,128)S(1)}, u32[]{:S(2)}, u32[]{:S(2)}) collective-permute-start(f32[5,16,768]{2,1,0:T(8,128)S(1)} %get-tuple-element.114), channel_id=1, source_target_pairs={{0,1},{1,2},{2,3},{3,4},{4,5},{5,6},{6,7},{7,8},{8,9},{9,10},{10,1... | collective-permute-start | bytes 737288 | tf_op jit(solution)/shard_map/ppermute | solution.py:326
  241.9 17.2 %collective-permute-start.29 = (f32[5,16,768]{2,1,0:T(8,128)S(1)}, f32[5,16,768]{2,1,0:T(8,128)S(1)}, u32[]{:S(2)}, u32[]{:S(2)}) collective-permute-start(f32[5,16,768]{2,1,0:T(8,128)S(1)} %get-tuple-element.116), channel_id=1, source_target_pairs={{1,0},{2,1},{3,2},{4,3},{5,4},{6,5},{7,6},{8,7},{9,8},{10,9},{11,1... | collective-permute-start | bytes 737288 | tf_op jit(solution)/shard_map/ppermute | solution.py:327
where the time goes:
time: 262 us; the launch traced here: 261 us
  waiting for transfers between devices  125 us (48%)
  starting transfers between devices  113 us (43%)
  Pallas kernels  20.2 us (8%)
    ppermute x15, waiting for transfers between devices, exchange(): high = lax.ppermute(first_rows, axis, backward)  65.5 us
    ppermute x15, waiting for transfers between devices, exchange(): low = lax.ppermute(last_rows, axis, forward)  59.6 us
    ppermute x15, starting transfers between devices, exchange(): low = lax.ppermute(last_rows, axis, forward)  56.9 us
    ppermute x15, starting transfers between devices, exchange(): high = lax.ppermute(first_rows, axis, backward)  42.8 us
    pallas_call x16, Pallas kernels, call(): pl.pallas_call(body, out_shape=shapes, in_specs=[VMEM] * len(operands), o...  17.1 us
    all_to_all x1, starting transfers between devices, reframe(): arrived = lax.all_to_all(pieces, 'row', 0, 0, tiled=True)  13.4 us
  transfers between devices with their start and end apart: 31, of which 23 were waited for; matrix products, arithmetic and copies ran while one was open for 0% of the time, Pallas kernels for 2%

commit v1 on v0

--- a/solution.py
+++ b/solution.py
@@ -11,7 +11,6 @@
 SHIFT = 64
 CHUNKS = 1
 CHUNK_LIMIT = 8 * 2**20
-HIGH = lax.Precision.HIGHEST
 VMEM = pl.BlockSpec(memory_space=pltpu.VMEM)
 LIMIT = pltpu.CompilerParams(vmem_limit_bytes=CHUNK_LIMIT)
 SMEM = pl.BlockSpec(memory_space=pltpu.SMEM)
@@ -46,7 +45,17 @@
     lax.fori_loop(0, 2 * LANES // 8, fill, 0, unroll=8)
 
 
+def halves(value):
+    high = value.astype(jnp.bfloat16)
+    return high, (value - high.astype(jnp.float32)).astype(jnp.bfloat16)
+
+
+def split_band(wide_ref, out_ref):
+    out_ref[:, :LANES], out_ref[:, LANES:] = halves(wide_ref[...])
+
+
 def prepare_body(axial_ref, lateral_ref, ya_ref, yb_ref, za_ref, zb_ref, *band_refs):
+    band_refs, full_ref = band_refs[:-1], band_refs[-1]
     axial, lateral = axial_ref.shape[1], lateral_ref.shape[2]
     rows = (
         (ya_ref, lambda k: axial_ref[0, k], axial),
@@ -60,8 +69,9 @@
     xa = normalized(lambda k: lateral_ref[0, 1, k], lateral)
     xb = normalized(lambda k: axial_ref[1, k], axial)
     for taps, refs in ((xa, band_refs[:2]), (xb, band_refs[2:])):
-        fill_band(refs[0], taps, 1)
-        fill_band(refs[1], taps, -1)
+        for ref, sign in zip(refs, (1, -1)):
+            fill_band(full_ref, taps, sign)
+            split_band(full_ref, ref)
 
 
 def local(*shape):
@@ -83,26 +93,31 @@
 def prepare(axial_kernel, lateral_kernel):
     axial, lateral = axial_kernel.shape[1], lateral_kernel.shape[2]
     shapes = [local(count, 8, LANES) for count in (axial, lateral, lateral, lateral)]
-    shapes += [local(2 * LANES, LANES)] * 4
+    shapes += [pltpu.VMEM((2 * LANES, 2 * LANES), jnp.bfloat16)] * 4
     outs = pl.pallas_call(
         prepare_body,
         out_shape=shapes,
         in_specs=[SMEM, SMEM],
         out_specs=[VMEM] * len(shapes),
+        scratch_shapes=[local(2 * LANES, LANES)],
         compiler_params=LIMIT,
         name="prepare",
     )(axial_kernel, lateral_kernel)
     return outs[:2], outs[2:4], (outs[4:6], outs[6:8])
 
 
-def correlate(taps, rows, extent, reverse):
+def correlate(taps, rows, extent, reverse, begun=None):
     count = len(taps)
     sums = [None] * extent
     for r in range(extent + count - 1):
         value = rows(r)
+        if value is None:
+            continue
         for i in range(max(0, r - count + 1), min(extent, r + 1)):
             k = r - i
             term = taps[count - 1 - k if reverse else k] * value
+            if sums[i] is None and begun is not None:
+                sums[i] = begun(i)
             sums[i] = term if sums[i] is None else sums[i] + term
     return sums
 
@@ -118,6 +133,42 @@
         return pick(high, r - margin - extent)
 
     return rows
+
+
+def outer_rows(low, high, extent, pick):
+    margin = low.shape[0]
+
+    def rows(r):
+        if r < margin:
+            return pick(low, r)
+        return pick(high, r - margin - extent) if r >= margin + extent else None
+
+    return rows
+
+
+def inner_rows(mid, margin, pick):
+    return lambda r: pick(mid, r - margin) if margin <= r < margin + mid.shape[0] else None
+
+
+def own_body(reverse, taps_ref, mid_ref, out_ref):
+    extent, inner, width = mid_ref.shape
+    margin = taps_ref.shape[0] // 2
+
+    def tile(j, carry):
+        lanes = lanes_at(j)
+        taps = [taps_ref[k] for k in range(taps_ref.shape[0])]
+        for at in range(0, inner, 8):
+            pick = lambda ref, r: ref[r, at:at + 8, lanes]
+            for i, value in enumerate(correlate(taps, inner_rows(mid_ref, margin, pick), extent, reverse)):
+                out_ref[i, at:at + 8, lanes] = value
+        return carry
+
+    lax.fori_loop(0, width // LANES, tile, 0)
+
+
+def own(taps, mid, reverse):
+    (part,) = call(functools.partial(own_body, reverse), (taps, mid), [local(*mid.shape)])
+    return part
 
 
 def lanes_at(j):
@@ -142,8 +193,9 @@
         taps = [taps_ref[k] for k in range(taps_ref.shape[0])]
         for y in range(0, rows_y, 8):
             pick = lambda ref, r: ref[r, y:y + 8, lanes]
-            sums = correlate(taps, padded_rows(low_ref, mid_ref, high_ref, pick), mid_ref.shape[0], reverse)
-            store(y, j, sums)
+            extent = mid_ref.shape[0]
+            begun = lambda i: mid_ref[i, y:y + 8, lanes]
+            store(y, j, correlate(taps, outer_rows(low_ref, high_ref, extent, pick), extent, reverse, begun))
         return carry
 
     lax.fori_loop(0, width // LANES, tile, 0)
@@ -171,7 +223,9 @@
         lanes = lanes_at(j)
         taps = [taps_ref[k] for k in range(taps_ref.shape[0])]
         pick = lambda ref, r: ref[r, :, lanes]
-        sums = correlate(taps, padded_rows(low_ref, mid_ref, high_ref, pick), mid_ref.shape[0], reverse)
+        extent = mid_ref.shape[0]
+        begun = lambda i: mid_ref[i, :, lanes]
+        sums = correlate(taps, outer_rows(low_ref, high_ref, extent, pick), extent, reverse, begun)
         if divide:
             for i, value in enumerate(sums):
                 put(out_refs, i, slice(None), lanes, view_ref[i, :, lanes] / value)
@@ -226,12 +280,16 @@
     wide_ref[:, wide_ref.shape[1] - LANES:] = blank
 
 
+def product(left, right):
+    return jnp.dot(left, right, preferred_element_type=jnp.float32)
+
+
 def along_x(wide_ref, band):
-    width = wide_ref.shape[1] - LANES
-    for j in range(width // LANES):
-        yield j, jnp.dot(
-            wide_ref[:, j * LANES:(j + 2) * LANES], band, precision=HIGH, preferred_element_type=jnp.float32
-        )
+    high, low = halves(wide_ref[...])
+    for j in range(wide_ref.shape[1] // LANES - 1):
+        window = slice(j * LANES, (j + 2) * LANES)
+        both = product(high[:, window], band)
+        yield j, both[:, :LANES] + (both[:, LANES:] + product(low[:, window], band[:, :LANES]))
 
 
 def put_ahead(wide_ref, band_ref, out_refs, ny):
@@ -245,10 +303,11 @@
 
 
 def first_body(lateral_ref, estimate_ref, *refs):
-    out_refs, (wide_ref, band_ref) = refs[:-2], refs[-2:]
+    out_refs, (wide_ref, full_ref, band_ref) = refs[:-3], refs[-3:]
     nz, ny, nx = estimate_ref.shape
     count = lateral_ref.shape[2]
-    fill_band(band_ref, normalized(lambda k: lateral_ref[0, 1, k], count), 1)
+    fill_band(full_ref, normalized(lambda k: lateral_ref[0, 1, k], count), 1)
+    split_band(full_ref, band_ref)
     clear_edges(wide_ref)
     wide_ref[:, SHIFT:SHIFT + nx] = estimate_ref[...].reshape(nz * ny, nx)
     put_ahead(wide_ref, band_ref, out_refs, ny)
@@ -272,7 +331,11 @@
         out_shape=shapes,
         in_specs=[SMEM, VMEM],
         out_specs=[VMEM] * len(shapes),
-        scratch_shapes=[local(nz * ny, nx + LANES), local(2 * LANES, LANES)],
+        scratch_shapes=[
+            local(nz * ny, nx + LANES),
+            local(2 * LANES, LANES),
+            pltpu.VMEM((2 * LANES, 2 * LANES), jnp.bfloat16),
+        ],
         compiler_params=LIMIT,
         name="first",
     )(lateral_kernel, pltpu.with_memory_space_constraint(estimate, pltpu.VMEM))
@@ -363,6 +426,11 @@
             put(out_refs, y, slice(None), lanes, turned[y])
 
 
+def halo(taps, parts, axis, reverse):
+    low, block, high = exchange(parts, axis)
+    return low, own(taps, block, reverse), high
+
+
 def reframe(view, margin):
     nz, nx, ny = view.shape
     count = lax.axis_size("row")
@@ -383,23 +451,21 @@
     for step in range(steps):
         v = step % 2
         yt, zt = ytaps[v], ztaps[v]
-        ahead = depth(zt, *exchange(ahead, "col"), False, 2 * margin if v else margin_a)
+        ahead = depth(zt, *halo(zt, ahead, "col", False), False, 2 * margin if v else margin_a)
         if v:
             ahead = deep(yt, exchange(ahead, "row"), seen_b, margin)
         else:
-            ahead = plane(yt, *exchange(ahead, "row"), False, margin_a, seen_a)
-            ahead = plane(yt, *exchange(ahead, "row"), True, margin)
-        halo = exchange(ahead, "col")
+            ahead = plane(yt, *halo(yt, ahead, "row", False), False, margin_a, seen_a)
+            ahead = plane(yt, *halo(yt, ahead, "row", True), True, margin)
+        outer = halo(zt, ahead, "col", True)
         if step == steps - 1:
-            estimate, _ = update(zt, [halo], bands[v][1], estimate)
+            estimate, _ = update(zt, [outer], bands[v][1], estimate)
         else:
-            estimate, (ahead,) = update(zt, [halo], bands[v][1], estimate, bands[1 - v][0])
+            estimate, (ahead,) = update(zt, [outer], bands[v][1], estimate, bands[1 - v][0])
     return estimate
 
 
 def solution(mesh):
     in_specs = (P("col", "row", None), P("col", "row", None), P("col", "row", None), P(), P())
     out_specs = P("col", "row", None)
-    return jax.shard_map(
-        per_device, mesh=mesh, in_specs=in_specs, out_specs=out_specs, check_vma=False
-    )
+    return jax.shard_map(per_device, mesh=mesh, in_specs=in_specs, out_specs=out_specs, check_vma=False)

time: 262 us -> 257 us (0.981)
    ppermute x15, waiting for transfers between devices: 59.6 us -> 52.1 us  [exchange(): low = lax.ppermute(last_rows, axis, forward)]
    ppermute x15, waiting for transfers between devices: 65.5 us -> 70.5 us  [exchange(): high = lax.ppermute(first_rows, axis, backward)]
    pallas_call x16 -> x28, Pallas kernels: 17.1 us -> 14.9 us  [call(): pl.pallas_call(body, out_shape=shapes, in_specs=[VMEM] * len(operands), o...]
  transfers between devices with their start and end apart: 31 -> 31, of which waited for: 23 -> 24; matrix products, arithmetic and copies ran while one was open for 0% -> 0% of each run, Pallas kernels for 2% -> 3%
where the time goes in v1:
time: 257 us; the launch traced here: 256 us
  waiting for transfers between devices  123 us (48%)
  starting transfers between devices  113 us (44%)
  Pallas kernels  17.7 us (7%)
    ppermute x15, waiting for transfers between devices, exchange(): high = lax.ppermute(first_rows, axis, backward)  70.5 us
    ppermute x15, starting transfers between devices, exchange(): low = lax.ppermute(last_rows, axis, forward)  55.4 us
    ppermute x15, waiting for transfers between devices, exchange(): low = lax.ppermute(last_rows, axis, forward)  52.1 us
    ppermute x15, starting transfers between devices, exchange(): high = lax.ppermute(first_rows, axis, backward)  44 us
    pallas_call x28, Pallas kernels, call(): pl.pallas_call(body, out_shape=shapes, in_specs=[VMEM] * len(operands), o...  14.9 us
    all_to_all x1, starting transfers between devices, reframe(): arrived = lax.all_to_all(pieces, 'row', 0, 0, tiled=True)  13.4 us
  transfers between devices with their start and end apart: 31, of which 24 were waited for; matrix products, arithmetic and copies ran while one was open for 0% of the time, Pallas kernels for 3%

profile of v1, /device:TPU:115, one launch (start us, length us, event | category | flops | bytes accessed | tf_op | source)
XLA Modules:
  0.0 255.6 jit_solution(3054934584559624772)
XLA Ops:
  0.0 1.0 copy-done
  1.7 1.1 first.1
  2.8 2.4 collective-permute-start
  5.3 3.7 %collective-permute-start.1 = (f32[5,16,768]{2,1,0:T(8,128)S(1)}, f32[5,16,768]{2,1,0:T(8,128)S(1)}, u32[]{:S(2)}, u32[]{:S(2)}) collective-permute-start(f32[5,16,768]{2,1,0:T(8,128)S(1)} %get-tuple-element.68), channel_id=1, source_target_pairs={{1,0},{2,1},{3,2},{4,3},{5,4},{6,5},{7,6},{8,7},{9,8},{10,9},{11,1... | collective-permute-start | bytes 737288 | tf_op jit(solution)/shard_map/ppermute | solution.py:390
  9.1 1.7 prepare.1
  11.0 3.4 %collective-permute-done.low_ref = f32[5,16,768]{2,1,0:T(8,128)S(1)} collective-permute-done((f32[5,16,768]{2,1,0:T(8,128)S(1)}, f32[5,16,768]{2,1,0:T(8,128)S(1)}, u32[]{:S(2)}, u32[]{:S(2)}) %collective-permute-start) | collective-permute-done | bytes 245792 | tf_op jit(solution)/shard_map/ppermute | solution.py:389
  14.4 7.8 %collective-permute-done.1.high_ref = f32[5,16,768]{2,1,0:T(8,128)S(1)} collective-permute-done((f32[5,16,768]{2,1,0:T(8,128)S(1)}, f32[5,16,768]{2,1,0:T(8,128)S(1)}, u32[]{:S(2)}, u32[]{:S(2)}) %collective-permute-start.1) | collective-permute-done | bytes 245792 | tf_op jit(solution)/shard_map/ppermute | solution.py:390
  22.5 1.9 collective-permute-start.2
  24.4 3.5 %collective-permute-start.3 = (f32[15,8,768]{2,1,0:T(8,128)S(1)}, f32[15,8,768]{2,1,0:T(8,128)S(1)}, u32[]{:S(2)}, u32[]{:S(2)}) collective-permute-start(f32[15,8,768]{2,1,0:T(8,128)S(1)} %get-tuple-element.71), channel_id=1, source_target_pairs={{16,0},{32,16},{48,32},{64,48},{80,64},{96,80},{112,96},{128,112},... | collective-permute-start | bytes 1105928 | tf_op jit(solution)/shard_map/ppermute | solution.py:390
  28.8 7.7 %collective-permute-done.3.high_ref = f32[15,8,768]{2,1,0:T(8,128)S(1)} collective-permute-done((f32[15,8,768]{2,1,0:T(8,128)S(1)}, f32[15,8,768]{2,1,0:T(8,128)S(1)}, u32[]{:S(2)}, u32[]{:S(2)}) %collective-permute-start.3) | collective-permute-done | bytes 368672 | tf_op jit(solution)/shard_map/ppermute | solution.py:390
  36.6 1.3 shard_map.58
  37.8 1.9 collective-permute-start.4
  39.8 2.4 collective-permute-start.5
  42.2 1.7 shard_map.65
  43.8 13.4 %all-to-all-start = ((f32[32,24,128]{2,1,0:T(8,128)}), f32[32,24,128]{2,1,0:T(8,128)S(1)}, u32[]{:S(2)}, u32[]{:S(2)}) async-start(f32[32,24,128]{2,1,0:T(8,128)} %shard_map.65), calls=%async_computation | async-start | bytes 786432 | tf_op jit(solution)/shard_map/all_to_all | solution.py:439
  58.3 4.3 %collective-permute-start.6 = (f32[5,16,768]{2,1,0:T(8,128)S(1)}, f32[5,16,768]{2,1,0:T(8,128)S(1)}, u32[]{:S(2)}, u32[]{:S(2)}) collective-permute-start(f32[5,16,768]{2,1,0:T(8,128)S(1)} %get-tuple-element.75), channel_id=1, source_target_pairs={{0,1},{1,2},{2,3},{3,4},{4,5},{5,6},{6,7},{7,8},{8,9},{9,10},{10,1... | collective-permute-start | bytes 737288 | tf_op jit(solution)/shard_map/ppermute | solution.py:389
  62.6 1.9 collective-permute-start.7
  64.8 5.6 %collective-permute-done.6.refs_0_ = f32[5,16,768]{2,1,0:T(8,128)S(1)} collective-permute-done((f32[5,16,768]{2,1,0:T(8,128)S(1)}, f32[5,16,768]{2,1,0:T(8,128)S(1)}, u32[]{:S(2)}, u32[]{:S(2)}) %collective-permute-start.6) | collective-permute-done | bytes 245792 | tf_op jit(solution)/shard_map/ppermute | solution.py:389
  70.4 6.6 %collective-permute-done.7.refs_2_ = f32[5,16,768]{2,1,0:T(8,128)S(1)} collective-permute-done((f32[5,16,768]{2,1,0:T(8,128)S(1)}, f32[5,16,768]{2,1,0:T(8,128)S(1)}, u32[]{:S(2)}, u32[]{:S(2)}) %collective-permute-start.7) | collective-permute-done | bytes 245792 | tf_op jit(solution)/shard_map/ppermute | solution.py:390
  77.0 0.8 shard_map.62
  77.8 3.2 %collective-permute-start.8 = (f32[5,16,768]{2,1,0:T(8,128)S(1)}, f32[5,16,768]{2,1,0:T(8,128)S(1)}, u32[]{:S(2)}, u32[]{:S(2)}) collective-permute-start(f32[5,16,768]{2,1,0:T(8,128)S(1)} %get-tuple-element.81), channel_id=1, source_target_pairs={{0,1},{1,2},{2,3},{3,4},{4,5},{5,6},{6,7},{7,8},{8,9},{9,10},{10,1... | collective-permute-start | bytes 737288 | tf_op jit(solution)/shard_map/ppermute | solution.py:389
  81.1 3.0 %collective-permute-start.9 = (f32[5,16,768]{2,1,0:T(8,128)S(1)}, f32[5,16,768]{2,1,0:T(8,128)S(1)}, u32[]{:S(2)}, u32[]{:S(2)}) collective-permute-start(f32[5,16,768]{2,1,0:T(8,128)S(1)} %get-tuple-element.83), channel_id=1, source_target_pairs={{1,0},{2,1},{3,2},{4,3},{5,4},{6,5},{7,6},{8,7},{9,8},{10,9},{11,1... | collective-permute-start | bytes 737288 | tf_op jit(solution)/shard_map/ppermute | solution.py:390
  84.3 8.2 %collective-permute-done.8.low_ref = f32[5,16,768]{2,1,0:T(8,128)S(1)} collective-permute-done((f32[5,16,768]{2,1,0:T(8,128)S(1)}, f32[5,16,768]{2,1,0:T(8,128)S(1)}, u32[]{:S(2)}, u32[]{:S(2)}) %collective-permute-start.8) | collective-permute-done | bytes 245792 | tf_op jit(solution)/shard_map/ppermute | solution.py:389
  92.7 11.5 %collective-permute-start.10 = (f32[10,8,768]{2,1,0:T(8,128)S(1)}, f32[10,8,768]{2,1,0:T(8,128)S(1)}, u32[]{:S(2)}, u32[]{:S(2)}) collective-permute-start(f32[10,8,768]{2,1,0:T(8,128)S(1)} %get-tuple-element.84), channel_id=1, source_target_pairs={{0,16},{16,32},{32,48},{48,64},{64,80},{80,96},{96,112},{112,128},... | collective-permute-start | bytes 737288 | tf_op jit(solution)/shard_map/ppermute | solution.py:389
  104.1 1.9 collective-permute-start.11
  106.3 3.6 %collective-permute-start.12 = (f32[5,8,768]{2,1,0:T(8,128)S(1)}, f32[5,8,768]{2,1,0:T(8,128)S(1)}, u32[]{:S(2)}, u32[]{:S(2)}) collective-permute-start(f32[5,8,768]{2,1,0:T(8,128)S(1)} %get-tuple-element.87), channel_id=1, source_target_pairs={{0,16},{16,32},{32,48},{48,64},{64,80},{80,96},{96,112},{112,128},... | collective-permute-start | bytes 368648 | tf_op jit(solution)/shard_map/ppermute | solution.py:389
  109.9 1.9 collective-permute-start.13
  111.8 4.3 %collective-permute-done.13.view_high_ref = f32[5,8,768]{2,1,0:T(8,128)S(1)} collective-permute-done((f32[5,8,768]{2,1,0:T(8,128)S(1)}, f32[5,8,768]{2,1,0:T(8,128)S(1)}, u32[]{:S(2)}, u32[]{:S(2)}) %collective-permute-start.13) | collective-permute-done | bytes 122912 | tf_op jit(solution)/shard_map/ppermute | solution.py:390
  116.1 0.9 shard_map.67
  117.0 1.9 collective-permute-start.14
  118.9 4.3 %collective-permute-start.15 = (f32[5,16,768]{2,1,0:T(8,128)S(1)}, f32[5,16,768]{2,1,0:T(8,128)S(1)}, u32[]{:S(2)}, u32[]{:S(2)}) collective-permute-start(f32[5,16,768]{2,1,0:T(8,128)S(1)} %get-tuple-element.92), channel_id=1, source_target_pairs={{1,0},{2,1},{3,2},{4,3},{5,4},{6,5},{7,6},{8,7},{9,8},{10,9},{11,1... | collective-permute-start | bytes 737288 | tf_op jit(solution)/shard_map/ppermute | solution.py:390
  123.4 2.0 collective-permute-done.14.refs_0_
  125.5 10.7 %collective-permute-done.15.refs_2_ = f32[5,16,768]{2,1,0:T(8,128)S(1)} collective-permute-done((f32[5,16,768]{2,1,0:T(8,128)S(1)}, f32[5,16,768]{2,1,0:T(8,128)S(1)}, u32[]{:S(2)}, u32[]{:S(2)}) %collective-permute-start.15) | collective-permute-done | bytes 245792 | tf_op jit(solution)/shard_map/ppermute | solution.py:390
  137.0 1.9 collective-permute-start.16
  138.9 4.3 %collective-permute-start.17 = (f32[5,16,768]{2,1,0:T(8,128)S(1)}, f32[5,16,768]{2,1,0:T(8,128)S(1)}, u32[]{:S(2)}, u32[]{:S(2)}) collective-permute-start(f32[5,16,768]{2,1,0:T(8,128)S(1)} %get-tuple-element.97), channel_id=1, source_target_pairs={{1,0},{2,1},{3,2},{4,3},{5,4},{6,5},{7,6},{8,7},{9,8},{10,9},{11,1... | collective-permute-start | bytes 737288 | tf_op jit(solution)/shard_map/ppermute | solution.py:390
  143.4 6.7 %collective-permute-done.16.low_ref = f32[5,16,768]{2,1,0:T(8,128)S(1)} collective-permute-done((f32[5,16,768]{2,1,0:T(8,128)S(1)}, f32[5,16,768]{2,1,0:T(8,128)S(1)}, u32[]{:S(2)}, u32[]{:S(2)}) %collective-permute-start.16) | collective-permute-done | bytes 245792 | tf_op jit(solution)/shard_map/ppermute | solution.py:389
  150.1 1.6 collective-permute-done.17.high_ref
  151.9 5.4 %collective-permute-start.18 = (f32[15,8,768]{2,1,0:T(8,128)S(1)}, f32[15,8,768]{2,1,0:T(8,128)S(1)}, u32[]{:S(2)}, u32[]{:S(2)}) collective-permute-start(f32[15,8,768]{2,1,0:T(8,128)S(1)} %get-tuple-element.98), channel_id=1, source_target_pairs={{0,16},{16,32},{32,48},{48,64},{64,80},{80,96},{96,112},{112,128},... | collective-permute-start | bytes 1105928 | tf_op jit(solution)/shard_map/ppermute | solution.py:389
  157.3 1.9 collective-permute-start.19
  159.7 5.1 %collective-permute-done.18.low_ref = f32[15,8,768]{2,1,0:T(8,128)S(1)} collective-permute-done((f32[15,8,768]{2,1,0:T(8,128)S(1)}, f32[15,8,768]{2,1,0:T(8,128)S(1)}, u32[]{:S(2)}, u32[]{:S(2)}) %collective-permute-start.18) | collective-permute-done | bytes 368672 | tf_op jit(solution)/shard_map/ppermute | solution.py:389
  164.9 5.1 %collective-permute-done.19.high_ref = f32[15,8,768]{2,1,0:T(8,128)S(1)} collective-permute-done((f32[15,8,768]{2,1,0:T(8,128)S(1)}, f32[15,8,768]{2,1,0:T(8,128)S(1)}, u32[]{:S(2)}, u32[]{:S(2)}) %collective-permute-start.19) | collective-permute-done | bytes 368672 | tf_op jit(solution)/shard_map/ppermute | solution.py:390
  170.5 1.9 collective-permute-start.20
  172.4 2.4 collective-permute-start.21
  175.3 2.9 %collective-permute-done.20.low_ref = f32[15,8,768]{2,1,0:T(8,128)S(1)} collective-permute-done((f32[15,8,768]{2,1,0:T(8,128)S(1)}, f32[15,8,768]{2,1,0:T(8,128)S(1)}, u32[]{:S(2)}, u32[]{:S(2)}) %collective-permute-start.20) | collective-permute-done | bytes 368672 | tf_op jit(solution)/shard_map/ppermute | solution.py:389
  178.2 5.8 %collective-permute-done.21.high_ref = f32[15,8,768]{2,1,0:T(8,128)S(1)} collective-permute-done((f32[15,8,768]{2,1,0:T(8,128)S(1)}, f32[15,8,768]{2,1,0:T(8,128)S(1)}, u32[]{:S(2)}, u32[]{:S(2)}) %collective-permute-start.21) | collective-permute-done | bytes 368672 | tf_op jit(solution)/shard_map/ppermute | solution.py:390
  184.6 1.9 collective-permute-start.22
  186.5 4.3 %collective-permute-start.23 = (f32[5,16,768]{2,1,0:T(8,128)S(1)}, f32[5,16,768]{2,1,0:T(8,128)S(1)}, u32[]{:S(2)}, u32[]{:S(2)}) collective-permute-start(f32[5,16,768]{2,1,0:T(8,128)S(1)} %get-tuple-element.106), channel_id=1, source_target_pairs={{1,0},{2,1},{3,2},{4,3},{5,4},{6,5},{7,6},{8,7},{9,8},{10,9},{11,1... | collective-permute-start | bytes 737288 | tf_op jit(solution)/shard_map/ppermute | solution.py:390
  191.0 2.4 collective-permute-done.22.refs_0_
  193.4 6.3 %collective-permute-done.23.refs_2_ = f32[5,16,768]{2,1,0:T(8,128)S(1)} collective-permute-done((f32[5,16,768]{2,1,0:T(8,128)S(1)}, f32[5,16,768]{2,1,0:T(8,128)S(1)}, u32[]{:S(2)}, u32[]{:S(2)}) %collective-permute-start.23) | collective-permute-done | bytes 245792 | tf_op jit(solution)/shard_map/ppermute | solution.py:390
  199.7 0.8 shard_map.77
  200.5 2.2 collective-permute-start.24
  202.7 4.0 %collective-permute-start.25 = (f32[5,16,768]{2,1,0:T(8,128)S(1)}, f32[5,16,768]{2,1,0:T(8,128)S(1)}, u32[]{:S(2)}, u32[]{:S(2)}) collective-permute-start(f32[5,16,768]{2,1,0:T(8,128)S(1)} %get-tuple-element.110), channel_id=1, source_target_pairs={{1,0},{2,1},{3,2},{4,3},{5,4},{6,5},{7,6},{8,7},{9,8},{10,9},{11,1... | collective-permute-start | bytes 737288 | tf_op jit(solution)/shard_map/ppermute | solution.py:390
  206.9 3.4 %collective-permute-done.24.low_ref = f32[5,16,768]{2,1,0:T(8,128)S(1)} collective-permute-done((f32[5,16,768]{2,1,0:T(8,128)S(1)}, f32[5,16,768]{2,1,0:T(8,128)S(1)}, u32[]{:S(2)}, u32[]{:S(2)}) %collective-permute-start.24) | collective-permute-done | bytes 245792 | tf_op jit(solution)/shard_map/ppermute | solution.py:389
  210.3 6.8 %collective-permute-done.25.high_ref = f32[5,16,768]{2,1,0:T(8,128)S(1)} collective-permute-done((f32[5,16,768]{2,1,0:T(8,128)S(1)}, f32[5,16,768]{2,1,0:T(8,128)S(1)}, u32[]{:S(2)}, u32[]{:S(2)}) %collective-permute-start.25) | collective-permute-done | bytes 245792 | tf_op jit(solution)/shard_map/ppermute | solution.py:390
  217.3 7.6 %collective-permute-start.26 = (f32[10,8,768]{2,1,0:T(8,128)S(1)}, f32[10,8,768]{2,1,0:T(8,128)S(1)}, u32[]{:S(2)}, u32[]{:S(2)}) collective-permute-start(f32[10,8,768]{2,1,0:T(8,128)S(1)} %get-tuple-element.111), channel_id=1, source_target_pairs={{0,16},{16,32},{32,48},{48,64},{64,80},{80,96},{96,112},{112,128},... | collective-permute-start | bytes 737288 | tf_op jit(solution)/shard_map/ppermute | solution.py:389
  225.0 1.9 collective-permute-start.27
  226.9 3.7 %collective-permute-done.26.low_ref = f32[10,8,768]{2,1,0:T(8,128)S(1)} collective-permute-done((f32[10,8,768]{2,1,0:T(8,128)S(1)}, f32[10,8,768]{2,1,0:T(8,128)S(1)}, u32[]{:S(2)}, u32[]{:S(2)}) %collective-permute-start.26) | collective-permute-done | bytes 245792 | tf_op jit(solution)/shard_map/ppermute | solution.py:389
  230.6 1.8 collective-permute-done.27.high_ref
  232.5 0.9 shard_map.80
  233.4 3.6 %collective-permute-start.28 = (f32[5,16,768]{2,1,0:T(8,128)S(1)}, f32[5,16,768]{2,1,0:T(8,128)S(1)}, u32[]{:S(2)}, u32[]{:S(2)}) collective-permute-start(f32[5,16,768]{2,1,0:T(8,128)S(1)} %get-tuple-element.114), channel_id=1, source_target_pairs={{0,1},{1,2},{2,3},{3,4},{4,5},{5,6},{6,7},{7,8},{8,9},{9,10},{10,1... | collective-permute-start | bytes 737288 | tf_op jit(solution)/shard_map/ppermute | solution.py:389
  237.1 2.5 collective-permute-start.29
  239.8 8.4 %collective-permute-done.28.refs_0_ = f32[5,16,768]{2,1,0:T(8,128)S(1)} collective-permute-done((f32[5,16,768]{2,1,0:T(8,128)S(1)}, f32[5,16,768]{2,1,0:T(8,128)S(1)}, u32[]{:S(2)}, u32[]{:S(2)}) %collective-permute-start.28) | collective-permute-done | bytes 245792 | tf_op jit(solution)/shard_map/ppermute | solution.py:389
  248.3 6.0 %collective-permute-done.29.refs_2_ = f32[5,16,768]{2,1,0:T(8,128)S(1)} collective-permute-done((f32[5,16,768]{2,1,0:T(8,128)S(1)}, f32[5,16,768]{2,1,0:T(8,128)S(1)}, u32[]{:S(2)}, u32[]{:S(2)}) %collective-permute-start.29) | collective-permute-done | bytes 245792 | tf_op jit(solution)/shard_map/ppermute | solution.py:390
  254.3 1.3 shard_map.82
  (43 shorter events, 8.3 us)
Async XLA Ops:
  0.0 1.0 copy-start
  1.0 0.7 copy-start.3
  2.8 6.2 %copy-start.4 = (f32[2,2,11]{2,1,0:T(2,128)S(1)}, f32[2,2,11]{2,1,0:T(2,128)}, u32[]{:S(2)}) copy-start(f32[2,2,11]{2,1,0:T(2,128)} %lateral_ref.3) | copy-start | bytes 532
  2.8 6.2 %copy-start.5 = (f32[2,31]{1,0:T(2,128)S(1)}, f32[2,31]{1,0:T(2,128)}, u32[]{:S(2)}) copy-start(f32[2,31]{1,0:T(2,128)} %axial_ref.1) | copy-start | bytes 748
  2.8 11.5 %collective-permute-start = (f32[5,16,768]{2,1,0:T(8,128)S(1)}, f32[5,16,768]{2,1,0:T(8,128)S(1)}, u32[]{:S(2)}, u32[]{:S(2)}) collective-permute-start(f32[5,16,768]{2,1,0:T(8,128)S(1)} %get-tuple-element.66), channel_id=1, source_target_pairs={{0,1},{1,2},{2,3},{3,4},{4,5},{5,6},{6,7},{7,8},{8,9},{9,10},{10,1... | collective-permute-start | bytes 737288 | tf_op jit(solution)/shard_map/ppermute | solution.py:389
  5.3 16.9 %collective-permute-start.1 = (f32[5,16,768]{2,1,0:T(8,128)S(1)}, f32[5,16,768]{2,1,0:T(8,128)S(1)}, u32[]{:S(2)}, u32[]{:S(2)}) collective-permute-start(f32[5,16,768]{2,1,0:T(8,128)S(1)} %get-tuple-element.68), channel_id=1, source_target_pairs={{1,0},{2,1},{3,2},{4,3},{5,4},{6,5},{7,6},{8,7},{9,8},{10,9},{11,1... | collective-permute-start | bytes 737288 | tf_op jit(solution)/shard_map/ppermute | solution.py:390
  11.0 17.0 %copy-start.6 = (f32[8,16,768]{2,1,0:T(8,128)S(1)}, f32[8,16,768]{2,1,0:T(8,128)}, u32[]{:S(2)}) copy-start(f32[8,16,768]{2,1,0:T(8,128)} %param.5) | copy-start | bytes 1179652
  22.5 6.4 %collective-permute-start.2 = (f32[15,8,768]{2,1,0:T(8,128)S(1)}, f32[15,8,768]{2,1,0:T(8,128)S(1)}, u32[]{:S(2)}, u32[]{:S(2)}) collective-permute-start(f32[15,8,768]{2,1,0:T(8,128)S(1)} %get-tuple-element.69), channel_id=1, source_target_pairs={{0,16},{16,32},{32,48},{48,64},{64,80},{80,96},{96,112},{112,128},... | collective-permute-start | bytes 1105928 | tf_op jit(solution)/shard_map/ppermute | solution.py:389
  24.4 12.2 %collective-permute-start.3 = (f32[15,8,768]{2,1,0:T(8,128)S(1)}, f32[15,8,768]{2,1,0:T(8,128)S(1)}, u32[]{:S(2)}, u32[]{:S(2)}) collective-permute-start(f32[15,8,768]{2,1,0:T(8,128)S(1)} %get-tuple-element.71), channel_id=1, source_target_pairs={{16,0},{32,16},{48,32},{64,48},{80,64},{96,80},{112,96},{128,112},... | collective-permute-start | bytes 1105928 | tf_op jit(solution)/shard_map/ppermute | solution.py:390
  36.6 5.6 %copy-start.2 = (f32[8,24,512]{2,1,0:T(8,128)S(1)}, f32[8,24,512]{2,1,0:T(8,128)}, u32[]{:S(2)}) copy-start(f32[8,24,512]{2,1,0:T(8,128)} %view_ref.1) | copy-start | bytes 1179652
  37.8 19.9 %collective-permute-start.4 = (f32[15,8,768]{2,1,0:T(8,128)}, f32[15,8,768]{2,1,0:T(8,128)S(1)}, u32[]{:S(2)}, u32[]{:S(2)}) collective-permute-start(f32[15,8,768]{2,1,0:T(8,128)} %get-tuple-element.72), channel_id=1, source_target_pairs={{0,16},{16,32},{32,48},{48,64},{64,80},{80,96},{96,112},{112,128},... | collective-permute-start | bytes 1105928 | tf_op jit(solution)/shard_map/ppermute | solution.py:389
  39.8 18.0 %collective-permute-start.5 = (f32[15,8,768]{2,1,0:T(8,128)S(1)}, f32[15,8,768]{2,1,0:T(8,128)S(1)}, u32[]{:S(2)}, u32[]{:S(2)}) collective-permute-start(f32[15,8,768]{2,1,0:T(8,128)S(1)} %get-tuple-element.74), channel_id=1, source_target_pairs={{16,0},{32,16},{48,32},{64,48},{80,64},{96,80},{112,96},{128,112},... | collective-permute-start | bytes 1105928 | tf_op jit(solution)/shard_map/ppermute | solution.py:390
  43.8 62.2 %all-to-all-start = ((f32[32,24,128]{2,1,0:T(8,128)}), f32[32,24,128]{2,1,0:T(8,128)S(1)}, u32[]{:S(2)}, u32[]{:S(2)}) async-start(f32[32,24,128]{2,1,0:T(8,128)} %shard_map.65), calls=%async_computation | async-start | bytes 786432 | tf_op jit(solution)/shard_map/all_to_all | solution.py:439
  58.3 12.1 %collective-permute-start.6 = (f32[5,16,768]{2,1,0:T(8,128)S(1)}, f32[5,16,768]{2,1,0:T(8,128)S(1)}, u32[]{:S(2)}, u32[]{:S(2)}) collective-permute-start(f32[5,16,768]{2,1,0:T(8,128)S(1)} %get-tuple-element.75), channel_id=1, source_target_pairs={{0,1},{1,2},{2,3},{3,4},{4,5},{5,6},{6,7},{7,8},{8,9},{9,10},{10,1... | collective-permute-start | bytes 737288 | tf_op jit(solution)/shard_map/ppermute | solution.py:389
  62.6 14.4 %collective-permute-start.7 = (f32[5,16,768]{2,1,0:T(8,128)S(1)}, f32[5,16,768]{2,1,0:T(8,128)S(1)}, u32[]{:S(2)}, u32[]{:S(2)}) collective-permute-start(f32[5,16,768]{2,1,0:T(8,128)S(1)} %get-tuple-element.77), channel_id=1, source_target_pairs={{1,0},{2,1},{3,2},{4,3},{5,4},{6,5},{7,6},{8,7},{9,8},{10,9},{11,1... | collective-permute-start | bytes 737288 | tf_op jit(solution)/shard_map/ppermute | solution.py:390
  64.6 12.4 %copy-start.1 = (f32[8,16,768]{2,1,0:T(8,128)S(1)}, f32[8,16,768]{2,1,0:T(8,128)}, u32[]{:S(2)}) copy-start(f32[8,16,768]{2,1,0:T(8,128)} %estimate_ref.3) | copy-start | bytes 1179652
  77.8 14.6 %collective-permute-start.8 = (f32[5,16,768]{2,1,0:T(8,128)S(1)}, f32[5,16,768]{2,1,0:T(8,128)S(1)}, u32[]{:S(2)}, u32[]{:S(2)}) collective-permute-start(f32[5,16,768]{2,1,0:T(8,128)S(1)} %get-tuple-element.81), channel_id=1, source_target_pairs={{0,1},{1,2},{2,3},{3,4},{4,5},{5,6},{6,7},{7,8},{8,9},{9,10},{10,1... | collective-permute-start | bytes 737288 | tf_op jit(solution)/shard_map/ppermute | solution.py:389
  81.1 11.3 %collective-permute-start.9 = (f32[5,16,768]{2,1,0:T(8,128)S(1)}, f32[5,16,768]{2,1,0:T(8,128)S(1)}, u32[]{:S(2)}, u32[]{:S(2)}) collective-permute-start(f32[5,16,768]{2,1,0:T(8,128)S(1)} %get-tuple-element.83), channel_id=1, source_target_pairs={{1,0},{2,1},{3,2},{4,3},{5,4},{6,5},{7,6},{8,7},{9,8},{10,9},{11,1... | collective-permute-start | bytes 737288 | tf_op jit(solution)/shard_map/ppermute | solution.py:390
  92.7 23.4 %collective-permute-start.10 = (f32[10,8,768]{2,1,0:T(8,128)S(1)}, f32[10,8,768]{2,1,0:T(8,128)S(1)}, u32[]{:S(2)}, u32[]{:S(2)}) collective-permute-start(f32[10,8,768]{2,1,0:T(8,128)S(1)} %get-tuple-element.84), channel_id=1, source_target_pairs={{0,16},{16,32},{32,48},{48,64},{64,80},{80,96},{96,112},{112,128},... | collective-permute-start | bytes 737288 | tf_op jit(solution)/shard_map/ppermute | solution.py:389
  104.1 12.0 %collective-permute-start.11 = (f32[10,8,768]{2,1,0:T(8,128)S(1)}, f32[10,8,768]{2,1,0:T(8,128)S(1)}, u32[]{:S(2)}, u32[]{:S(2)}) collective-permute-start(f32[10,8,768]{2,1,0:T(8,128)S(1)} %get-tuple-element.86), channel_id=1, source_target_pairs={{16,0},{32,16},{48,32},{64,48},{80,64},{96,80},{112,96},{128,112},... | collective-permute-start | bytes 737288 | tf_op jit(solution)/shard_map/ppermute | solution.py:390
  106.3 5.6 %collective-permute-start.12 = (f32[5,8,768]{2,1,0:T(8,128)S(1)}, f32[5,8,768]{2,1,0:T(8,128)S(1)}, u32[]{:S(2)}, u32[]{:S(2)}) collective-permute-start(f32[5,8,768]{2,1,0:T(8,128)S(1)} %get-tuple-element.87), channel_id=1, source_target_pairs={{0,16},{16,32},{32,48},{48,64},{64,80},{80,96},{96,112},{112,128},... | collective-permute-start | bytes 368648 | tf_op jit(solution)/shard_map/ppermute | solution.py:389
  109.9 6.2 %collective-permute-start.13 = (f32[5,8,768]{2,1,0:T(8,128)S(1)}, f32[5,8,768]{2,1,0:T(8,128)S(1)}, u32[]{:S(2)}, u32[]{:S(2)}) collective-permute-start(f32[5,8,768]{2,1,0:T(8,128)S(1)} %get-tuple-element.89), channel_id=1, source_target_pairs={{16,0},{32,16},{48,32},{64,48},{80,64},{96,80},{112,96},{128,112},... | collective-permute-start | bytes 368648 | tf_op jit(solution)/shard_map/ppermute | solution.py:390
  117.0 8.5 %collective-permute-start.14 = (f32[5,16,768]{2,1,0:T(8,128)S(1)}, f32[5,16,768]{2,1,0:T(8,128)S(1)}, u32[]{:S(2)}, u32[]{:S(2)}) collective-permute-start(f32[5,16,768]{2,1,0:T(8,128)S(1)} %get-tuple-element.90), channel_id=1, source_target_pairs={{0,1},{1,2},{2,3},{3,4},{4,5},{5,6},{6,7},{7,8},{8,9},{9,10},{10,1... | collective-permute-start | bytes 737288 | tf_op jit(solution)/shard_map/ppermute | solution.py:389
  118.9 17.2 %collective-permute-start.15 = (f32[5,16,768]{2,1,0:T(8,128)S(1)}, f32[5,16,768]{2,1,0:T(8,128)S(1)}, u32[]{:S(2)}, u32[]{:S(2)}) collective-permute-start(f32[5,16,768]{2,1,0:T(8,128)S(1)} %get-tuple-element.92), channel_id=1, source_target_pairs={{1,0},{2,1},{3,2},{4,3},{5,4},{6,5},{7,6},{8,7},{9,8},{10,9},{11,1... | collective-permute-start | bytes 737288 | tf_op jit(solution)/shard_map/ppermute | solution.py:390
  137.0 13.1 %collective-permute-start.16 = (f32[5,16,768]{2,1,0:T(8,128)S(1)}, f32[5,16,768]{2,1,0:T(8,128)S(1)}, u32[]{:S(2)}, u32[]{:S(2)}) collective-permute-start(f32[5,16,768]{2,1,0:T(8,128)S(1)} %get-tuple-element.95), channel_id=1, source_target_pairs={{0,1},{1,2},{2,3},{3,4},{4,5},{5,6},{6,7},{7,8},{8,9},{9,10},{10,1... | collective-permute-start | bytes 737288 | tf_op jit(solution)/shard_map/ppermute | solution.py:389
  138.9 12.8 %collective-permute-start.17 = (f32[5,16,768]{2,1,0:T(8,128)S(1)}, f32[5,16,768]{2,1,0:T(8,128)S(1)}, u32[]{:S(2)}, u32[]{:S(2)}) collective-permute-start(f32[5,16,768]{2,1,0:T(8,128)S(1)} %get-tuple-element.97), channel_id=1, source_target_pairs={{1,0},{2,1},{3,2},{4,3},{5,4},{6,5},{7,6},{8,7},{9,8},{10,9},{11,1... | collective-permute-start | bytes 737288 | tf_op jit(solution)/shard_map/ppermute | solution.py:390
  151.9 12.9 %collective-permute-start.18 = (f32[15,8,768]{2,1,0:T(8,128)S(1)}, f32[15,8,768]{2,1,0:T(8,128)S(1)}, u32[]{:S(2)}, u32[]{:S(2)}) collective-permute-start(f32[15,8,768]{2,1,0:T(8,128)S(1)} %get-tuple-element.98), channel_id=1, source_target_pairs={{0,16},{16,32},{32,48},{48,64},{64,80},{80,96},{96,112},{112,128},... | collective-permute-start | bytes 1105928 | tf_op jit(solution)/shard_map/ppermute | solution.py:389
  157.3 12.6 %collective-permute-start.19 = (f32[15,8,768]{2,1,0:T(8,128)S(1)}, f32[15,8,768]{2,1,0:T(8,128)S(1)}, u32[]{:S(2)}, u32[]{:S(2)}) collective-permute-start(f32[15,8,768]{2,1,0:T(8,128)S(1)} %get-tuple-element.100), channel_id=1, source_target_pairs={{16,0},{32,16},{48,32},{64,48},{80,64},{96,80},{112,96},{128,112},... | collective-permute-start | bytes 1105928 | tf_op jit(solution)/shard_map/ppermute | solution.py:390
  170.5 7.7 %collective-permute-start.20 = (f32[15,8,768]{2,1,0:T(8,128)S(1)}, f32[15,8,768]{2,1,0:T(8,128)S(1)}, u32[]{:S(2)}, u32[]{:S(2)}) collective-permute-start(f32[15,8,768]{2,1,0:T(8,128)S(1)} %get-tuple-element.101), channel_id=1, source_target_pairs={{0,16},{16,32},{32,48},{48,64},{64,80},{80,96},{96,112},{112,128},... | collective-permute-start | bytes 1105928 | tf_op jit(solution)/shard_map/ppermute | solution.py:389
  172.4 11.6 %collective-permute-start.21 = (f32[15,8,768]{2,1,0:T(8,128)S(1)}, f32[15,8,768]{2,1,0:T(8,128)S(1)}, u32[]{:S(2)}, u32[]{:S(2)}) collective-permute-start(f32[15,8,768]{2,1,0:T(8,128)S(1)} %get-tuple-element.103), channel_id=1, source_target_pairs={{16,0},{32,16},{48,32},{64,48},{80,64},{96,80},{112,96},{128,112},... | collective-permute-start | bytes 1105928 | tf_op jit(solution)/shard_map/ppermute | solution.py:390
  184.6 8.8 %collective-permute-start.22 = (f32[5,16,768]{2,1,0:T(8,128)S(1)}, f32[5,16,768]{2,1,0:T(8,128)S(1)}, u32[]{:S(2)}, u32[]{:S(2)}) collective-permute-start(f32[5,16,768]{2,1,0:T(8,128)S(1)} %get-tuple-element.104), channel_id=1, source_target_pairs={{0,1},{1,2},{2,3},{3,4},{4,5},{5,6},{6,7},{7,8},{8,9},{9,10},{10,1... | collective-permute-start | bytes 737288 | tf_op jit(solution)/shard_map/ppermute | solution.py:389
  186.5 13.2 %collective-permute-start.23 = (f32[5,16,768]{2,1,0:T(8,128)S(1)}, f32[5,16,768]{2,1,0:T(8,128)S(1)}, u32[]{:S(2)}, u32[]{:S(2)}) collective-permute-start(f32[5,16,768]{2,1,0:T(8,128)S(1)} %get-tuple-element.106), channel_id=1, source_target_pairs={{1,0},{2,1},{3,2},{4,3},{5,4},{6,5},{7,6},{8,7},{9,8},{10,9},{11,1... | collective-permute-start | bytes 737288 | tf_op jit(solution)/shard_map/ppermute | solution.py:390
  200.5 9.8 %collective-permute-start.24 = (f32[5,16,768]{2,1,0:T(8,128)S(1)}, f32[5,16,768]{2,1,0:T(8,128)S(1)}, u32[]{:S(2)}, u32[]{:S(2)}) collective-permute-start(f32[5,16,768]{2,1,0:T(8,128)S(1)} %get-tuple-element.108), channel_id=1, source_target_pairs={{0,1},{1,2},{2,3},{3,4},{4,5},{5,6},{6,7},{7,8},{8,9},{9,10},{10,1... | collective-permute-start | bytes 737288 | tf_op jit(solution)/shard_map/ppermute | solution.py:389
  202.7 14.4 %collective-permute-start.25 = (f32[5,16,768]{2,1,0:T(8,128)S(1)}, f32[5,16,768]{2,1,0:T(8,128)S(1)}, u32[]{:S(2)}, u32[]{:S(2)}) collective-permute-start(f32[5,16,768]{2,1,0:T(8,128)S(1)} %get-tuple-element.110), channel_id=1, source_target_pairs={{1,0},{2,1},{3,2},{4,3},{5,4},{6,5},{7,6},{8,7},{9,8},{10,9},{11,1... | collective-permute-start | bytes 737288 | tf_op jit(solution)/shard_map/ppermute | solution.py:390
  217.3 13.3 %collective-permute-start.26 = (f32[10,8,768]{2,1,0:T(8,128)S(1)}, f32[10,8,768]{2,1,0:T(8,128)S(1)}, u32[]{:S(2)}, u32[]{:S(2)}) collective-permute-start(f32[10,8,768]{2,1,0:T(8,128)S(1)} %get-tuple-element.111), channel_id=1, source_target_pairs={{0,16},{16,32},{32,48},{48,64},{64,80},{80,96},{96,112},{112,128},... | collective-permute-start | bytes 737288 | tf_op jit(solution)/shard_map/ppermute | solution.py:389
  225.0 7.5 %collective-permute-start.27 = (f32[10,8,768]{2,1,0:T(8,128)S(1)}, f32[10,8,768]{2,1,0:T(8,128)S(1)}, u32[]{:S(2)}, u32[]{:S(2)}) collective-permute-start(f32[10,8,768]{2,1,0:T(8,128)S(1)} %get-tuple-element.113), channel_id=1, source_target_pairs={{16,0},{32,16},{48,32},{64,48},{80,64},{96,80},{112,96},{128,112},... | collective-permute-start | bytes 737288 | tf_op jit(solution)/shard_map/ppermute | solution.py:390
  233.4 14.9 %collective-permute-start.28 = (f32[5,16,768]{2,1,0:T(8,128)S(1)}, f32[5,16,768]{2,1,0:T(8,128)S(1)}, u32[]{:S(2)}, u32[]{:S(2)}) collective-permute-start(f32[5,16,768]{2,1,0:T(8,128)S(1)} %get-tuple-element.114), channel_id=1, source_target_pairs={{0,1},{1,2},{2,3},{3,4},{4,5},{5,6},{6,7},{7,8},{8,9},{9,10},{10,1... | collective-permute-start | bytes 737288 | tf_op jit(solution)/shard_map/ppermute | solution.py:389
  237.1 17.2 %collective-permute-start.29 = (f32[5,16,768]{2,1,0:T(8,128)S(1)}, f32[5,16,768]{2,1,0:T(8,128)S(1)}, u32[]{:S(2)}, u32[]{:S(2)}) collective-permute-start(f32[5,16,768]{2,1,0:T(8,128)S(1)} %get-tuple-element.116), channel_id=1, source_target_pairs={{1,0},{2,1},{3,2},{4,3},{5,4},{6,5},{7,6},{8,7},{9,8},{10,9},{11,1... | collective-permute-start | bytes 737288 | tf_op jit(solution)/shard_map/ppermute | solution.py:390

commit v2 on v1

--- a/solution.py
+++ b/solution.py
@@ -42,7 +42,10 @@
         band_ref[pl.ds(pl.multiple_of(step * 8, 8), 8), :] = value
         return carry
 
-    lax.fori_loop(0, 2 * LANES // 8, fill, 0, unroll=8)
+    start, stop = (SHIFT - 7 - half) // 8, (SHIFT + LANES - 1 + half) // 8 + 1
+    band_ref[:8 * start, :] = jnp.zeros((8 * start, LANES), jnp.float32)
+    band_ref[8 * stop:, :] = jnp.zeros((2 * LANES - 8 * stop, LANES), jnp.float32)
+    lax.fori_loop(start, stop, fill, 0, unroll=True)
 
 
 def halves(value):
@@ -119,7 +122,7 @@
             if sums[i] is None and begun is not None:
                 sums[i] = begun(i)
             sums[i] = term if sums[i] is None else sums[i] + term
-    return sums
+    return [begun(i) if value is None else value for i, value in enumerate(sums)]
 
 
 def padded_rows(low, mid, high, pick):
@@ -150,9 +153,8 @@
     return lambda r: pick(mid, r - margin) if margin <= r < margin + mid.shape[0] else None
 
 
-def own_body(reverse, taps_ref, mid_ref, out_ref):
-    extent, inner, width = mid_ref.shape
-    margin = taps_ref.shape[0] // 2
+def own_body(reverse, margin, taps_ref, mid_ref, out_ref):
+    extent, (_, inner, width) = out_ref.shape[0], mid_ref.shape
 
     def tile(j, carry):
         lanes = lanes_at(j)
@@ -166,8 +168,10 @@
     lax.fori_loop(0, width // LANES, tile, 0)
 
 
-def own(taps, mid, reverse):
-    (part,) = call(functools.partial(own_body, reverse), (taps, mid), [local(*mid.shape)])
+def own(taps, mid, margin, reverse):
+    extent = mid.shape[0] + 2 * margin - taps.shape[0] + 1
+    shapes = [local(extent, *mid.shape[1:])]
+    (part,) = call(functools.partial(own_body, reverse, margin), (taps, mid), shapes)
     return part
 
 
@@ -248,14 +252,15 @@
 
 
 def deep_body(taps_ref, low_ref, mid_ref, high_ref, view_low_ref, view_ref, view_high_ref, *out_refs):
-    extent = mid_ref.shape[0]
+    extent = view_ref.shape[0]
 
     def tile(j, carry):
         lanes = lanes_at(j)
         taps = [taps_ref[k] for k in range(taps_ref.shape[0])]
         pick = lambda ref, r: ref[r, :, lanes]
         wide = extent + len(taps) - 1
-        sums = correlate(taps, padded_rows(low_ref, mid_ref, high_ref, pick), wide, False)
+        begun = lambda i: mid_ref[i, :, lanes]
+        sums = correlate(taps, outer_rows(low_ref, high_ref, extent, pick), wide, False, begun)
         seen = padded_rows(view_low_ref, view_ref, view_high_ref, pick)
         quotient = [seen(r) / value for r, value in enumerate(sums)]
         sums = correlate(taps, lambda r: quotient[r], extent, True)
@@ -268,10 +273,10 @@
     lax.fori_loop(0, mid_ref.shape[2] // LANES, tile, 0)
 
 
-def deep(taps, halo, view, margin):
-    ny, nz, nx = halo[1].shape
+def deep(taps, outer, view, margin):
+    ny, nz, nx = view[1].shape
     shapes = [local(nz, ny, nx), local(margin, ny, nx), local(margin, ny, nx)]
-    return call(deep_body, (taps, *halo, *view), shapes)
+    return call(deep_body, (taps, *outer, *view), shapes)
 
 
 def clear_edges(wide_ref):
@@ -303,13 +308,16 @@
 
 
 def first_body(lateral_ref, estimate_ref, *refs):
-    out_refs, (wide_ref, full_ref, band_ref) = refs[:-3], refs[-3:]
+    out_refs, (wide_ref, full_ref, band_ref, held_ref, sem) = refs[:-5], refs[-5:]
     nz, ny, nx = estimate_ref.shape
     count = lateral_ref.shape[2]
+    copy = pltpu.make_async_copy(estimate_ref, held_ref, sem)
+    copy.start()
     fill_band(full_ref, normalized(lambda k: lateral_ref[0, 1, k], count), 1)
     split_band(full_ref, band_ref)
     clear_edges(wide_ref)
-    wide_ref[:, SHIFT:SHIFT + nx] = estimate_ref[...].reshape(nz * ny, nx)
+    copy.wait()
+    wide_ref[:, SHIFT:SHIFT + nx] = held_ref[...].reshape(nz * ny, nx)
     put_ahead(wide_ref, band_ref, out_refs, ny)
 
 
@@ -329,16 +337,18 @@
     outs = pl.pallas_call(
         first_body,
         out_shape=shapes,
-        in_specs=[SMEM, VMEM],
+        in_specs=[SMEM, pl.BlockSpec(memory_space=pltpu.HBM)],
         out_specs=[VMEM] * len(shapes),
         scratch_shapes=[
             local(nz * ny, nx + LANES),
             local(2 * LANES, LANES),
             pltpu.VMEM((2 * LANES, 2 * LANES), jnp.bfloat16),
+            local(nz, ny, nx),
+            pltpu.SemaphoreType.DMA(()),
         ],
         compiler_params=LIMIT,
         name="first",
-    )(lateral_kernel, pltpu.with_memory_space_constraint(estimate, pltpu.VMEM))
+    )(lateral_kernel, pltpu.with_memory_space_constraint(estimate, pltpu.HBM))
     return chunked(outs)
 
 
@@ -428,7 +438,7 @@
 
 def halo(taps, parts, axis, reverse):
     low, block, high = exchange(parts, axis)
-    return low, own(taps, block, reverse), high
+    return low, own(taps, block, low.shape[0], reverse), high
 
 
 def reframe(view, margin):
@@ -453,7 +463,7 @@
         yt, zt = ytaps[v], ztaps[v]
         ahead = depth(zt, *halo(zt, ahead, "col", False), False, 2 * margin if v else margin_a)
         if v:
-            ahead = deep(yt, exchange(ahead, "row"), seen_b, margin)
+            ahead = deep(yt, halo(yt, ahead, "row", False), seen_b, margin)
         else:
             ahead = plane(yt, *halo(yt, ahead, "row", False), False, margin_a, seen_a)
             ahead = plane(yt, *halo(yt, ahead, "row", True), True, margin)

time: 257 us -> 256 us (level)
  the two profiles are of different devices: /device:TPU:115 before, /device:TPU:123 now
where the time goes in v2:
time: 256 us; the launch traced here: 255 us
  waiting for transfers between devices  130 us (51%)
  starting transfers between devices  105 us (41%)
  Pallas kernels  18.1 us (7%)
    ppermute x15, waiting for transfers between devices, exchange(): low = lax.ppermute(last_rows, axis, forward)  76.5 us
    ppermute x15, waiting for transfers between devices, exchange(): high = lax.ppermute(first_rows, axis, backward)  53.7 us
    ppermute x15, starting transfers between devices, exchange(): low = lax.ppermute(last_rows, axis, forward)  51.6 us
    ppermute x15, starting transfers between devices, exchange(): high = lax.ppermute(first_rows, axis, backward)  41.7 us
    pallas_call x30, Pallas kernels, call(): pl.pallas_call(body, out_shape=shapes, in_specs=[VMEM] * len(operands), o...  14.9 us
    all_to_all x1, starting transfers between devices, reframe(): arrived = lax.all_to_all(pieces, 'row', 0, 0, tiled=True)  11.6 us
  transfers between devices with their start and end apart: 31, of which 25 were waited for; matrix products, arithmetic and copies ran while one was open for 0% of the time, Pallas kernels for 3%

profile of v2, /device:TPU:123, one launch (start us, length us, event | category | flops | bytes accessed | tf_op | source)
XLA Modules:
  0.0 254.7 jit_solution(17294487829545523299)
XLA Ops:
  0.7 2.0 first.1
  2.7 3.3 %collective-permute-start = (f32[5,16,768]{2,1,0:T(8,128)S(1)}, f32[5,16,768]{2,1,0:T(8,128)S(1)}, u32[]{:S(2)}, u32[]{:S(2)}) collective-permute-start(f32[5,16,768]{2,1,0:T(8,128)S(1)} %get-tuple-element.66), channel_id=1, source_target_pairs={{0,1},{1,2},{2,3},{3,4},{4,5},{5,6},{6,7},{7,8},{8,9},{9,10},{10,1... | collective-permute-start | bytes 737288 | tf_op jit(solution)/shard_map/ppermute | solution.py:399
  6.0 2.8 %collective-permute-start.1 = (f32[5,16,768]{2,1,0:T(8,128)S(1)}, f32[5,16,768]{2,1,0:T(8,128)S(1)}, u32[]{:S(2)}, u32[]{:S(2)}) collective-permute-start(f32[5,16,768]{2,1,0:T(8,128)S(1)} %get-tuple-element.68), channel_id=1, source_target_pairs={{1,0},{2,1},{3,2},{4,3},{5,4},{6,5},{7,6},{8,7},{9,8},{10,9},{11,1... | collective-permute-start | bytes 737288 | tf_op jit(solution)/shard_map/ppermute | solution.py:400
  8.9 1.3 prepare.1
  10.4 7.4 %collective-permute-done.low_ref = f32[5,16,768]{2,1,0:T(8,128)S(1)} collective-permute-done((f32[5,16,768]{2,1,0:T(8,128)S(1)}, f32[5,16,768]{2,1,0:T(8,128)S(1)}, u32[]{:S(2)}, u32[]{:S(2)}) %collective-permute-start) | collective-permute-done | bytes 245792 | tf_op jit(solution)/shard_map/ppermute | solution.py:399
  17.9 1.4 collective-permute-done.1.high_ref
  19.5 9.1 %collective-permute-start.2 = (f32[15,8,768]{2,1,0:T(8,128)S(1)}, f32[15,8,768]{2,1,0:T(8,128)S(1)}, u32[]{:S(2)}, u32[]{:S(2)}) collective-permute-start(f32[15,8,768]{2,1,0:T(8,128)S(1)} %get-tuple-element.69), channel_id=1, source_target_pairs={{0,16},{16,32},{32,48},{48,64},{64,80},{80,96},{96,112},{112,128},... | collective-permute-start | bytes 1105928 | tf_op jit(solution)/shard_map/ppermute | solution.py:399
  28.6 1.9 collective-permute-start.3
  31.3 4.9 %collective-permute-done.2.low_ref = f32[15,8,768]{2,1,0:T(8,128)S(1)} collective-permute-done((f32[15,8,768]{2,1,0:T(8,128)S(1)}, f32[15,8,768]{2,1,0:T(8,128)S(1)}, u32[]{:S(2)}, u32[]{:S(2)}) %collective-permute-start.2) | collective-permute-done | bytes 368672 | tf_op jit(solution)/shard_map/ppermute | solution.py:399
  36.2 2.2 collective-permute-done.3.high_ref
  38.4 1.3 shard_map.58
  39.6 3.1 %collective-permute-start.4 = (f32[15,8,768]{2,1,0:T(8,128)}, f32[15,8,768]{2,1,0:T(8,128)S(1)}, u32[]{:S(2)}, u32[]{:S(2)}) collective-permute-start(f32[15,8,768]{2,1,0:T(8,128)} %get-tuple-element.72), channel_id=1, source_target_pairs={{0,16},{16,32},{32,48},{48,64},{64,80},{80,96},{96,112},{112,128},... | collective-permute-start | bytes 1105928 | tf_op jit(solution)/shard_map/ppermute | solution.py:399
  42.8 1.9 collective-permute-start.5
  44.7 1.7 shard_map.66
  46.4 11.6 %all-to-all-start = ((f32[32,24,128]{2,1,0:T(8,128)}), f32[32,24,128]{2,1,0:T(8,128)S(1)}, u32[]{:S(2)}, u32[]{:S(2)}) async-start(f32[32,24,128]{2,1,0:T(8,128)} %shard_map.66), calls=%async_computation | async-start | bytes 786432 | tf_op jit(solution)/shard_map/all_to_all | solution.py:449
  59.0 4.3 %collective-permute-start.6 = (f32[5,16,768]{2,1,0:T(8,128)S(1)}, f32[5,16,768]{2,1,0:T(8,128)S(1)}, u32[]{:S(2)}, u32[]{:S(2)}) collective-permute-start(f32[5,16,768]{2,1,0:T(8,128)S(1)} %get-tuple-element.75), channel_id=1, source_target_pairs={{0,1},{1,2},{2,3},{3,4},{4,5},{5,6},{6,7},{7,8},{8,9},{9,10},{10,1... | collective-permute-start | bytes 737288 | tf_op jit(solution)/shard_map/ppermute | solution.py:399
  63.3 1.9 collective-permute-start.7
  65.4 9.2 %collective-permute-done.6.refs_0_ = f32[5,16,768]{2,1,0:T(8,128)S(1)} collective-permute-done((f32[5,16,768]{2,1,0:T(8,128)S(1)}, f32[5,16,768]{2,1,0:T(8,128)S(1)}, u32[]{:S(2)}, u32[]{:S(2)}) %collective-permute-start.6) | collective-permute-done | bytes 245792 | tf_op jit(solution)/shard_map/ppermute | solution.py:399
  74.6 6.5 %collective-permute-done.7.refs_2_ = f32[5,16,768]{2,1,0:T(8,128)S(1)} collective-permute-done((f32[5,16,768]{2,1,0:T(8,128)S(1)}, f32[5,16,768]{2,1,0:T(8,128)S(1)}, u32[]{:S(2)}, u32[]{:S(2)}) %collective-permute-start.7) | collective-permute-done | bytes 245792 | tf_op jit(solution)/shard_map/ppermute | solution.py:400
  81.0 0.8 shard_map.62
  81.9 1.9 collective-permute-start.8
  83.8 4.3 %collective-permute-start.9 = (f32[5,16,768]{2,1,0:T(8,128)S(1)}, f32[5,16,768]{2,1,0:T(8,128)S(1)}, u32[]{:S(2)}, u32[]{:S(2)}) collective-permute-start(f32[5,16,768]{2,1,0:T(8,128)S(1)} %get-tuple-element.83), channel_id=1, source_target_pairs={{1,0},{2,1},{3,2},{4,3},{5,4},{6,5},{7,6},{8,7},{9,8},{10,9},{11,1... | collective-permute-start | bytes 737288 | tf_op jit(solution)/shard_map/ppermute | solution.py:400
  88.3 8.7 %collective-permute-done.8.low_ref = f32[5,16,768]{2,1,0:T(8,128)S(1)} collective-permute-done((f32[5,16,768]{2,1,0:T(8,128)S(1)}, f32[5,16,768]{2,1,0:T(8,128)S(1)}, u32[]{:S(2)}, u32[]{:S(2)}) %collective-permute-start.8) | collective-permute-done | bytes 245792 | tf_op jit(solution)/shard_map/ppermute | solution.py:399
  97.0 4.0 %collective-permute-done.9.high_ref = f32[5,16,768]{2,1,0:T(8,128)S(1)} collective-permute-done((f32[5,16,768]{2,1,0:T(8,128)S(1)}, f32[5,16,768]{2,1,0:T(8,128)S(1)}, u32[]{:S(2)}, u32[]{:S(2)}) %collective-permute-start.9) | collective-permute-done | bytes 245792 | tf_op jit(solution)/shard_map/ppermute | solution.py:400
  101.3 1.9 collective-permute-start.10
  103.2 2.4 collective-permute-start.11
  105.8 4.1 %collective-permute-start.12 = (f32[5,8,768]{2,1,0:T(8,128)S(1)}, f32[5,8,768]{2,1,0:T(8,128)S(1)}, u32[]{:S(2)}, u32[]{:S(2)}) collective-permute-start(f32[5,8,768]{2,1,0:T(8,128)S(1)} %get-tuple-element.87), channel_id=1, source_target_pairs={{0,16},{16,32},{32,48},{48,64},{64,80},{80,96},{96,112},{112,128},... | collective-permute-start | bytes 368648 | tf_op jit(solution)/shard_map/ppermute | solution.py:399
  109.9 1.9 collective-permute-start.13
  112.1 4.9 %collective-permute-done.13.view_high_ref = f32[5,8,768]{2,1,0:T(8,128)S(1)} collective-permute-done((f32[5,8,768]{2,1,0:T(8,128)S(1)}, f32[5,8,768]{2,1,0:T(8,128)S(1)}, u32[]{:S(2)}, u32[]{:S(2)}) %collective-permute-start.13) | collective-permute-done | bytes 122912 | tf_op jit(solution)/shard_map/ppermute | solution.py:400
  117.6 1.9 collective-permute-start.14
  119.5 4.3 %collective-permute-start.15 = (f32[5,16,768]{2,1,0:T(8,128)S(1)}, f32[5,16,768]{2,1,0:T(8,128)S(1)}, u32[]{:S(2)}, u32[]{:S(2)}) collective-permute-start(f32[5,16,768]{2,1,0:T(8,128)S(1)} %get-tuple-element.92), channel_id=1, source_target_pairs={{1,0},{2,1},{3,2},{4,3},{5,4},{6,5},{7,6},{8,7},{9,8},{10,9},{11,1... | collective-permute-start | bytes 737288 | tf_op jit(solution)/shard_map/ppermute | solution.py:400
  124.0 7.2 %collective-permute-done.14.refs_0_ = f32[5,16,768]{2,1,0:T(8,128)S(1)} collective-permute-done((f32[5,16,768]{2,1,0:T(8,128)S(1)}, f32[5,16,768]{2,1,0:T(8,128)S(1)}, u32[]{:S(2)}, u32[]{:S(2)}) %collective-permute-start.14) | collective-permute-done | bytes 245792 | tf_op jit(solution)/shard_map/ppermute | solution.py:399
  131.2 3.9 %collective-permute-done.15.refs_2_ = f32[5,16,768]{2,1,0:T(8,128)S(1)} collective-permute-done((f32[5,16,768]{2,1,0:T(8,128)S(1)}, f32[5,16,768]{2,1,0:T(8,128)S(1)}, u32[]{:S(2)}, u32[]{:S(2)}) %collective-permute-start.15) | collective-permute-done | bytes 245792 | tf_op jit(solution)/shard_map/ppermute | solution.py:400
  135.1 0.8 shard_map.70
  135.9 2.3 collective-permute-start.16
  138.2 3.9 %collective-permute-start.17 = (f32[5,16,768]{2,1,0:T(8,128)S(1)}, f32[5,16,768]{2,1,0:T(8,128)S(1)}, u32[]{:S(2)}, u32[]{:S(2)}) collective-permute-start(f32[5,16,768]{2,1,0:T(8,128)S(1)} %get-tuple-element.97), channel_id=1, source_target_pairs={{1,0},{2,1},{3,2},{4,3},{5,4},{6,5},{7,6},{8,7},{9,8},{10,9},{11,1... | collective-permute-start | bytes 737288 | tf_op jit(solution)/shard_map/ppermute | solution.py:400
  142.3 6.2 %collective-permute-done.16.low_ref = f32[5,16,768]{2,1,0:T(8,128)S(1)} collective-permute-done((f32[5,16,768]{2,1,0:T(8,128)S(1)}, f32[5,16,768]{2,1,0:T(8,128)S(1)}, u32[]{:S(2)}, u32[]{:S(2)}) %collective-permute-start.16) | collective-permute-done | bytes 245792 | tf_op jit(solution)/shard_map/ppermute | solution.py:399
  148.6 5.5 %collective-permute-done.17.high_ref = f32[5,16,768]{2,1,0:T(8,128)S(1)} collective-permute-done((f32[5,16,768]{2,1,0:T(8,128)S(1)}, f32[5,16,768]{2,1,0:T(8,128)S(1)}, u32[]{:S(2)}, u32[]{:S(2)}) %collective-permute-start.17) | collective-permute-done | bytes 245792 | tf_op jit(solution)/shard_map/ppermute | solution.py:400
  154.3 5.7 %collective-permute-start.18 = (f32[15,8,768]{2,1,0:T(8,128)S(1)}, f32[15,8,768]{2,1,0:T(8,128)S(1)}, u32[]{:S(2)}, u32[]{:S(2)}) collective-permute-start(f32[15,8,768]{2,1,0:T(8,128)S(1)} %get-tuple-element.98), channel_id=1, source_target_pairs={{0,16},{16,32},{32,48},{48,64},{64,80},{80,96},{96,112},{112,128},... | collective-permute-start | bytes 1105928 | tf_op jit(solution)/shard_map/ppermute | solution.py:399
  160.0 1.9 collective-permute-start.19
  162.4 5.5 %collective-permute-done.18.low_ref = f32[15,8,768]{2,1,0:T(8,128)S(1)} collective-permute-done((f32[15,8,768]{2,1,0:T(8,128)S(1)}, f32[15,8,768]{2,1,0:T(8,128)S(1)}, u32[]{:S(2)}, u32[]{:S(2)}) %collective-permute-start.18) | collective-permute-done | bytes 368672 | tf_op jit(solution)/shard_map/ppermute | solution.py:399
  167.9 1.8 collective-permute-done.19.high_ref
  170.3 3.5 %collective-permute-start.20 = (f32[15,8,768]{2,1,0:T(8,128)S(1)}, f32[15,8,768]{2,1,0:T(8,128)S(1)}, u32[]{:S(2)}, u32[]{:S(2)}) collective-permute-start(f32[15,8,768]{2,1,0:T(8,128)S(1)} %get-tuple-element.101), channel_id=1, source_target_pairs={{0,16},{16,32},{32,48},{48,64},{64,80},{80,96},{96,112},{112,128},... | collective-permute-start | bytes 1105928 | tf_op jit(solution)/shard_map/ppermute | solution.py:399
  173.8 1.9 collective-permute-start.21
  176.1 4.5 %collective-permute-done.20.low_ref = f32[15,8,768]{2,1,0:T(8,128)S(1)} collective-permute-done((f32[15,8,768]{2,1,0:T(8,128)S(1)}, f32[15,8,768]{2,1,0:T(8,128)S(1)}, u32[]{:S(2)}, u32[]{:S(2)}) %collective-permute-start.20) | collective-permute-done | bytes 368672 | tf_op jit(solution)/shard_map/ppermute | solution.py:399
  180.6 2.9 %collective-permute-done.21.high_ref = f32[15,8,768]{2,1,0:T(8,128)S(1)} collective-permute-done((f32[15,8,768]{2,1,0:T(8,128)S(1)}, f32[15,8,768]{2,1,0:T(8,128)S(1)}, u32[]{:S(2)}, u32[]{:S(2)}) %collective-permute-start.21) | collective-permute-done | bytes 368672 | tf_op jit(solution)/shard_map/ppermute | solution.py:400
  184.0 1.9 collective-permute-start.22
  186.0 4.3 %collective-permute-start.23 = (f32[5,16,768]{2,1,0:T(8,128)S(1)}, f32[5,16,768]{2,1,0:T(8,128)S(1)}, u32[]{:S(2)}, u32[]{:S(2)}) collective-permute-start(f32[5,16,768]{2,1,0:T(8,128)S(1)} %get-tuple-element.106), channel_id=1, source_target_pairs={{1,0},{2,1},{3,2},{4,3},{5,4},{6,5},{7,6},{8,7},{9,8},{10,9},{11,1... | collective-permute-start | bytes 737288 | tf_op jit(solution)/shard_map/ppermute | solution.py:400
  190.4 7.9 %collective-permute-done.22.refs_0_ = f32[5,16,768]{2,1,0:T(8,128)S(1)} collective-permute-done((f32[5,16,768]{2,1,0:T(8,128)S(1)}, f32[5,16,768]{2,1,0:T(8,128)S(1)}, u32[]{:S(2)}, u32[]{:S(2)}) %collective-permute-start.22) | collective-permute-done | bytes 245792 | tf_op jit(solution)/shard_map/ppermute | solution.py:399
  198.3 4.5 %collective-permute-done.23.refs_2_ = f32[5,16,768]{2,1,0:T(8,128)S(1)} collective-permute-done((f32[5,16,768]{2,1,0:T(8,128)S(1)}, f32[5,16,768]{2,1,0:T(8,128)S(1)}, u32[]{:S(2)}, u32[]{:S(2)}) %collective-permute-start.23) | collective-permute-done | bytes 245792 | tf_op jit(solution)/shard_map/ppermute | solution.py:400
  202.8 0.8 shard_map.78
  203.6 1.9 collective-permute-start.24
  205.5 4.3 %collective-permute-start.25 = (f32[5,16,768]{2,1,0:T(8,128)S(1)}, f32[5,16,768]{2,1,0:T(8,128)S(1)}, u32[]{:S(2)}, u32[]{:S(2)}) collective-permute-start(f32[5,16,768]{2,1,0:T(8,128)S(1)} %get-tuple-element.110), channel_id=1, source_target_pairs={{1,0},{2,1},{3,2},{4,3},{5,4},{6,5},{7,6},{8,7},{9,8},{10,9},{11,1... | collective-permute-start | bytes 737288 | tf_op jit(solution)/shard_map/ppermute | solution.py:400
  210.0 6.1 %collective-permute-done.24.low_ref = f32[5,16,768]{2,1,0:T(8,128)S(1)} collective-permute-done((f32[5,16,768]{2,1,0:T(8,128)S(1)}, f32[5,16,768]{2,1,0:T(8,128)S(1)}, u32[]{:S(2)}, u32[]{:S(2)}) %collective-permute-start.24) | collective-permute-done | bytes 245792 | tf_op jit(solution)/shard_map/ppermute | solution.py:399
  216.1 4.5 %collective-permute-done.25.high_ref = f32[5,16,768]{2,1,0:T(8,128)S(1)} collective-permute-done((f32[5,16,768]{2,1,0:T(8,128)S(1)}, f32[5,16,768]{2,1,0:T(8,128)S(1)}, u32[]{:S(2)}, u32[]{:S(2)}) %collective-permute-start.25) | collective-permute-done | bytes 245792 | tf_op jit(solution)/shard_map/ppermute | solution.py:400
  220.9 2.5 collective-permute-start.26
  223.4 1.9 collective-permute-start.27
  225.6 0.9 collective-permute-done.26.low_ref
  226.5 5.3 %collective-permute-done.27.high_ref = f32[10,8,768]{2,1,0:T(8,128)S(1)} collective-permute-done((f32[10,8,768]{2,1,0:T(8,128)S(1)}, f32[10,8,768]{2,1,0:T(8,128)S(1)}, u32[]{:S(2)}, u32[]{:S(2)}) %collective-permute-start.27) | collective-permute-done | bytes 245792 | tf_op jit(solution)/shard_map/ppermute | solution.py:400
  232.4 4.1 %collective-permute-start.28 = (f32[5,16,768]{2,1,0:T(8,128)S(1)}, f32[5,16,768]{2,1,0:T(8,128)S(1)}, u32[]{:S(2)}, u32[]{:S(2)}) collective-permute-start(f32[5,16,768]{2,1,0:T(8,128)S(1)} %get-tuple-element.114), channel_id=1, source_target_pairs={{0,1},{1,2},{2,3},{3,4},{4,5},{5,6},{6,7},{7,8},{8,9},{9,10},{10,1... | collective-permute-start | bytes 737288 | tf_op jit(solution)/shard_map/ppermute | solution.py:399
  236.5 2.1 collective-permute-start.29
  238.8 8.1 %collective-permute-done.28.refs_0_ = f32[5,16,768]{2,1,0:T(8,128)S(1)} collective-permute-done((f32[5,16,768]{2,1,0:T(8,128)S(1)}, f32[5,16,768]{2,1,0:T(8,128)S(1)}, u32[]{:S(2)}, u32[]{:S(2)}) %collective-permute-start.28) | collective-permute-done | bytes 245792 | tf_op jit(solution)/shard_map/ppermute | solution.py:399
  246.9 6.5 %collective-permute-done.29.refs_2_ = f32[5,16,768]{2,1,0:T(8,128)S(1)} collective-permute-done((f32[5,16,768]{2,1,0:T(8,128)S(1)}, f32[5,16,768]{2,1,0:T(8,128)S(1)}, u32[]{:S(2)}, u32[]{:S(2)}) %collective-permute-start.29) | collective-permute-done | bytes 245792 | tf_op jit(solution)/shard_map/ppermute | solution.py:400
  253.4 1.3 shard_map.84
  (43 shorter events, 9.1 us)
Async XLA Ops:
  0.0 0.7 copy-start.2
  2.7 6.2 %copy-start.3 = (f32[2,2,11]{2,1,0:T(2,128)S(1)}, f32[2,2,11]{2,1,0:T(2,128)}, u32[]{:S(2)}) copy-start(f32[2,2,11]{2,1,0:T(2,128)} %lateral_ref.3) | copy-start | bytes 532
  2.7 6.2 %copy-start.4 = (f32[2,31]{1,0:T(2,128)S(1)}, f32[2,31]{1,0:T(2,128)}, u32[]{:S(2)}) copy-start(f32[2,31]{1,0:T(2,128)} %axial_ref.1) | copy-start | bytes 748
  2.7 15.1 %collective-permute-start = (f32[5,16,768]{2,1,0:T(8,128)S(1)}, f32[5,16,768]{2,1,0:T(8,128)S(1)}, u32[]{:S(2)}, u32[]{:S(2)}) collective-permute-start(f32[5,16,768]{2,1,0:T(8,128)S(1)} %get-tuple-element.66), channel_id=1, source_target_pairs={{0,1},{1,2},{2,3},{3,4},{4,5},{5,6},{6,7},{7,8},{8,9},{9,10},{10,1... | collective-permute-start | bytes 737288 | tf_op jit(solution)/shard_map/ppermute | solution.py:399
  6.0 13.2 %collective-permute-start.1 = (f32[5,16,768]{2,1,0:T(8,128)S(1)}, f32[5,16,768]{2,1,0:T(8,128)S(1)}, u32[]{:S(2)}, u32[]{:S(2)}) collective-permute-start(f32[5,16,768]{2,1,0:T(8,128)S(1)} %get-tuple-element.68), channel_id=1, source_target_pairs={{1,0},{2,1},{3,2},{4,3},{5,4},{6,5},{7,6},{8,7},{9,8},{10,9},{11,1... | collective-permute-start | bytes 737288 | tf_op jit(solution)/shard_map/ppermute | solution.py:400
  10.4 20.1 %copy-start.5 = (f32[8,16,768]{2,1,0:T(8,128)S(1)}, f32[8,16,768]{2,1,0:T(8,128)}, u32[]{:S(2)}) copy-start(f32[8,16,768]{2,1,0:T(8,128)} %param.5) | copy-start | bytes 1179652
  19.5 16.7 %collective-permute-start.2 = (f32[15,8,768]{2,1,0:T(8,128)S(1)}, f32[15,8,768]{2,1,0:T(8,128)S(1)}, u32[]{:S(2)}, u32[]{:S(2)}) collective-permute-start(f32[15,8,768]{2,1,0:T(8,128)S(1)} %get-tuple-element.69), channel_id=1, source_target_pairs={{0,16},{16,32},{32,48},{48,64},{64,80},{80,96},{96,112},{112,128},... | collective-permute-start | bytes 1105928 | tf_op jit(solution)/shard_map/ppermute | solution.py:399
  28.6 9.7 %collective-permute-start.3 = (f32[15,8,768]{2,1,0:T(8,128)S(1)}, f32[15,8,768]{2,1,0:T(8,128)S(1)}, u32[]{:S(2)}, u32[]{:S(2)}) collective-permute-start(f32[15,8,768]{2,1,0:T(8,128)S(1)} %get-tuple-element.71), channel_id=1, source_target_pairs={{16,0},{32,16},{48,32},{64,48},{80,64},{96,80},{112,96},{128,112},... | collective-permute-start | bytes 1105928 | tf_op jit(solution)/shard_map/ppermute | solution.py:400
  38.4 6.3 %copy-start.1 = (f32[8,24,512]{2,1,0:T(8,128)S(1)}, f32[8,24,512]{2,1,0:T(8,128)}, u32[]{:S(2)}) copy-start(f32[8,24,512]{2,1,0:T(8,128)} %view_ref.1) | copy-start | bytes 1179652
  39.6 18.8 %collective-permute-start.4 = (f32[15,8,768]{2,1,0:T(8,128)}, f32[15,8,768]{2,1,0:T(8,128)S(1)}, u32[]{:S(2)}, u32[]{:S(2)}) collective-permute-start(f32[15,8,768]{2,1,0:T(8,128)} %get-tuple-element.72), channel_id=1, source_target_pairs={{0,16},{16,32},{32,48},{48,64},{64,80},{80,96},{96,112},{112,128},... | collective-permute-start | bytes 1105928 | tf_op jit(solution)/shard_map/ppermute | solution.py:399
  42.8 15.7 %collective-permute-start.5 = (f32[15,8,768]{2,1,0:T(8,128)S(1)}, f32[15,8,768]{2,1,0:T(8,128)S(1)}, u32[]{:S(2)}, u32[]{:S(2)}) collective-permute-start(f32[15,8,768]{2,1,0:T(8,128)S(1)} %get-tuple-element.74), channel_id=1, source_target_pairs={{16,0},{32,16},{48,32},{64,48},{80,64},{96,80},{112,96},{128,112},... | collective-permute-start | bytes 1105928 | tf_op jit(solution)/shard_map/ppermute | solution.py:400
  46.4 59.3 %all-to-all-start = ((f32[32,24,128]{2,1,0:T(8,128)}), f32[32,24,128]{2,1,0:T(8,128)S(1)}, u32[]{:S(2)}, u32[]{:S(2)}) async-start(f32[32,24,128]{2,1,0:T(8,128)} %shard_map.66), calls=%async_computation | async-start | bytes 786432 | tf_op jit(solution)/shard_map/all_to_all | solution.py:449
  59.0 15.6 %collective-permute-start.6 = (f32[5,16,768]{2,1,0:T(8,128)S(1)}, f32[5,16,768]{2,1,0:T(8,128)S(1)}, u32[]{:S(2)}, u32[]{:S(2)}) collective-permute-start(f32[5,16,768]{2,1,0:T(8,128)S(1)} %get-tuple-element.75), channel_id=1, source_target_pairs={{0,1},{1,2},{2,3},{3,4},{4,5},{5,6},{6,7},{7,8},{8,9},{9,10},{10,1... | collective-permute-start | bytes 737288 | tf_op jit(solution)/shard_map/ppermute | solution.py:399
  63.3 17.8 %collective-permute-start.7 = (f32[5,16,768]{2,1,0:T(8,128)S(1)}, f32[5,16,768]{2,1,0:T(8,128)S(1)}, u32[]{:S(2)}, u32[]{:S(2)}) collective-permute-start(f32[5,16,768]{2,1,0:T(8,128)S(1)} %get-tuple-element.77), channel_id=1, source_target_pairs={{1,0},{2,1},{3,2},{4,3},{5,4},{6,5},{7,6},{8,7},{9,8},{10,9},{11,1... | collective-permute-start | bytes 737288 | tf_op jit(solution)/shard_map/ppermute | solution.py:400
  65.2 15.8 %copy-start = (f32[8,16,768]{2,1,0:T(8,128)S(1)}, f32[8,16,768]{2,1,0:T(8,128)}, u32[]{:S(2)}) copy-start(f32[8,16,768]{2,1,0:T(8,128)} %estimate_ref.3) | copy-start | bytes 1179652
  81.9 15.2 %collective-permute-start.8 = (f32[5,16,768]{2,1,0:T(8,128)S(1)}, f32[5,16,768]{2,1,0:T(8,128)S(1)}, u32[]{:S(2)}, u32[]{:S(2)}) collective-permute-start(f32[5,16,768]{2,1,0:T(8,128)S(1)} %get-tuple-element.81), channel_id=1, source_target_pairs={{0,1},{1,2},{2,3},{3,4},{4,5},{5,6},{6,7},{7,8},{8,9},{9,10},{10,1... | collective-permute-start | bytes 737288 | tf_op jit(solution)/shard_map/ppermute | solution.py:399
  83.8 17.2 %collective-permute-start.9 = (f32[5,16,768]{2,1,0:T(8,128)S(1)}, f32[5,16,768]{2,1,0:T(8,128)S(1)}, u32[]{:S(2)}, u32[]{:S(2)}) collective-permute-start(f32[5,16,768]{2,1,0:T(8,128)S(1)} %get-tuple-element.83), channel_id=1, source_target_pairs={{1,0},{2,1},{3,2},{4,3},{5,4},{6,5},{7,6},{8,7},{9,8},{10,9},{11,1... | collective-permute-start | bytes 737288 | tf_op jit(solution)/shard_map/ppermute | solution.py:400
  101.3 15.7 %collective-permute-start.10 = (f32[10,8,768]{2,1,0:T(8,128)S(1)}, f32[10,8,768]{2,1,0:T(8,128)S(1)}, u32[]{:S(2)}, u32[]{:S(2)}) collective-permute-start(f32[10,8,768]{2,1,0:T(8,128)S(1)} %get-tuple-element.84), channel_id=1, source_target_pairs={{0,16},{16,32},{32,48},{48,64},{64,80},{80,96},{96,112},{112,128},... | collective-permute-start | bytes 737288 | tf_op jit(solution)/shard_map/ppermute | solution.py:399
  103.2 13.8 %collective-permute-start.11 = (f32[10,8,768]{2,1,0:T(8,128)S(1)}, f32[10,8,768]{2,1,0:T(8,128)S(1)}, u32[]{:S(2)}, u32[]{:S(2)}) collective-permute-start(f32[10,8,768]{2,1,0:T(8,128)S(1)} %get-tuple-element.86), channel_id=1, source_target_pairs={{16,0},{32,16},{48,32},{64,48},{80,64},{96,80},{112,96},{128,112},... | collective-permute-start | bytes 737288 | tf_op jit(solution)/shard_map/ppermute | solution.py:400
  105.8 6.3 %collective-permute-start.12 = (f32[5,8,768]{2,1,0:T(8,128)S(1)}, f32[5,8,768]{2,1,0:T(8,128)S(1)}, u32[]{:S(2)}, u32[]{:S(2)}) collective-permute-start(f32[5,8,768]{2,1,0:T(8,128)S(1)} %get-tuple-element.87), channel_id=1, source_target_pairs={{0,16},{16,32},{32,48},{48,64},{64,80},{80,96},{96,112},{112,128},... | collective-permute-start | bytes 368648 | tf_op jit(solution)/shard_map/ppermute | solution.py:399
  109.9 7.1 %collective-permute-start.13 = (f32[5,8,768]{2,1,0:T(8,128)S(1)}, f32[5,8,768]{2,1,0:T(8,128)S(1)}, u32[]{:S(2)}, u32[]{:S(2)}) collective-permute-start(f32[5,8,768]{2,1,0:T(8,128)S(1)} %get-tuple-element.89), channel_id=1, source_target_pairs={{16,0},{32,16},{48,32},{64,48},{80,64},{96,80},{112,96},{128,112},... | collective-permute-start | bytes 368648 | tf_op jit(solution)/shard_map/ppermute | solution.py:400
  117.6 13.6 %collective-permute-start.14 = (f32[5,16,768]{2,1,0:T(8,128)S(1)}, f32[5,16,768]{2,1,0:T(8,128)S(1)}, u32[]{:S(2)}, u32[]{:S(2)}) collective-permute-start(f32[5,16,768]{2,1,0:T(8,128)S(1)} %get-tuple-element.90), channel_id=1, source_target_pairs={{0,1},{1,2},{2,3},{3,4},{4,5},{5,6},{6,7},{7,8},{8,9},{9,10},{10,1... | collective-permute-start | bytes 737288 | tf_op jit(solution)/shard_map/ppermute | solution.py:399
  119.5 15.6 %collective-permute-start.15 = (f32[5,16,768]{2,1,0:T(8,128)S(1)}, f32[5,16,768]{2,1,0:T(8,128)S(1)}, u32[]{:S(2)}, u32[]{:S(2)}) collective-permute-start(f32[5,16,768]{2,1,0:T(8,128)S(1)} %get-tuple-element.92), channel_id=1, source_target_pairs={{1,0},{2,1},{3,2},{4,3},{5,4},{6,5},{7,6},{8,7},{9,8},{10,9},{11,1... | collective-permute-start | bytes 737288 | tf_op jit(solution)/shard_map/ppermute | solution.py:400
  135.9 12.6 %collective-permute-start.16 = (f32[5,16,768]{2,1,0:T(8,128)S(1)}, f32[5,16,768]{2,1,0:T(8,128)S(1)}, u32[]{:S(2)}, u32[]{:S(2)}) collective-permute-start(f32[5,16,768]{2,1,0:T(8,128)S(1)} %get-tuple-element.95), channel_id=1, source_target_pairs={{0,1},{1,2},{2,3},{3,4},{4,5},{5,6},{6,7},{7,8},{8,9},{9,10},{10,1... | collective-permute-start | bytes 737288 | tf_op jit(solution)/shard_map/ppermute | solution.py:399
  138.2 15.8 %collective-permute-start.17 = (f32[5,16,768]{2,1,0:T(8,128)S(1)}, f32[5,16,768]{2,1,0:T(8,128)S(1)}, u32[]{:S(2)}, u32[]{:S(2)}) collective-permute-start(f32[5,16,768]{2,1,0:T(8,128)S(1)} %get-tuple-element.97), channel_id=1, source_target_pairs={{1,0},{2,1},{3,2},{4,3},{5,4},{6,5},{7,6},{8,7},{9,8},{10,9},{11,1... | collective-permute-start | bytes 737288 | tf_op jit(solution)/shard_map/ppermute | solution.py:400
  154.3 13.7 %collective-permute-start.18 = (f32[15,8,768]{2,1,0:T(8,128)S(1)}, f32[15,8,768]{2,1,0:T(8,128)S(1)}, u32[]{:S(2)}, u32[]{:S(2)}) collective-permute-start(f32[15,8,768]{2,1,0:T(8,128)S(1)} %get-tuple-element.98), channel_id=1, source_target_pairs={{0,16},{16,32},{32,48},{48,64},{64,80},{80,96},{96,112},{112,128},... | collective-permute-start | bytes 1105928 | tf_op jit(solution)/shard_map/ppermute | solution.py:399
  160.0 9.7 %collective-permute-start.19 = (f32[15,8,768]{2,1,0:T(8,128)S(1)}, f32[15,8,768]{2,1,0:T(8,128)S(1)}, u32[]{:S(2)}, u32[]{:S(2)}) collective-permute-start(f32[15,8,768]{2,1,0:T(8,128)S(1)} %get-tuple-element.100), channel_id=1, source_target_pairs={{16,0},{32,16},{48,32},{64,48},{80,64},{96,80},{112,96},{128,112},... | collective-permute-start | bytes 1105928 | tf_op jit(solution)/shard_map/ppermute | solution.py:400
  170.3 10.3 %collective-permute-start.20 = (f32[15,8,768]{2,1,0:T(8,128)S(1)}, f32[15,8,768]{2,1,0:T(8,128)S(1)}, u32[]{:S(2)}, u32[]{:S(2)}) collective-permute-start(f32[15,8,768]{2,1,0:T(8,128)S(1)} %get-tuple-element.101), channel_id=1, source_target_pairs={{0,16},{16,32},{32,48},{48,64},{64,80},{80,96},{96,112},{112,128},... | collective-permute-start | bytes 1105928 | tf_op jit(solution)/shard_map/ppermute | solution.py:399
  173.8 9.7 %collective-permute-start.21 = (f32[15,8,768]{2,1,0:T(8,128)S(1)}, f32[15,8,768]{2,1,0:T(8,128)S(1)}, u32[]{:S(2)}, u32[]{:S(2)}) collective-permute-start(f32[15,8,768]{2,1,0:T(8,128)S(1)} %get-tuple-element.103), channel_id=1, source_target_pairs={{16,0},{32,16},{48,32},{64,48},{80,64},{96,80},{112,96},{128,112},... | collective-permute-start | bytes 1105928 | tf_op jit(solution)/shard_map/ppermute | solution.py:400
  184.0 14.3 %collective-permute-start.22 = (f32[5,16,768]{2,1,0:T(8,128)S(1)}, f32[5,16,768]{2,1,0:T(8,128)S(1)}, u32[]{:S(2)}, u32[]{:S(2)}) collective-permute-start(f32[5,16,768]{2,1,0:T(8,128)S(1)} %get-tuple-element.104), channel_id=1, source_target_pairs={{0,1},{1,2},{2,3},{3,4},{4,5},{5,6},{6,7},{7,8},{8,9},{9,10},{10,1... | collective-permute-start | bytes 737288 | tf_op jit(solution)/shard_map/ppermute | solution.py:399
  186.0 16.8 %collective-permute-start.23 = (f32[5,16,768]{2,1,0:T(8,128)S(1)}, f32[5,16,768]{2,1,0:T(8,128)S(1)}, u32[]{:S(2)}, u32[]{:S(2)}) collective-permute-start(f32[5,16,768]{2,1,0:T(8,128)S(1)} %get-tuple-element.106), channel_id=1, source_target_pairs={{1,0},{2,1},{3,2},{4,3},{5,4},{6,5},{7,6},{8,7},{9,8},{10,9},{11,1... | collective-permute-start | bytes 737288 | tf_op jit(solution)/shard_map/ppermute | solution.py:400
  203.6 12.5 %collective-permute-start.24 = (f32[5,16,768]{2,1,0:T(8,128)S(1)}, f32[5,16,768]{2,1,0:T(8,128)S(1)}, u32[]{:S(2)}, u32[]{:S(2)}) collective-permute-start(f32[5,16,768]{2,1,0:T(8,128)S(1)} %get-tuple-element.108), channel_id=1, source_target_pairs={{0,1},{1,2},{2,3},{3,4},{4,5},{5,6},{6,7},{7,8},{8,9},{9,10},{10,1... | collective-permute-start | bytes 737288 | tf_op jit(solution)/shard_map/ppermute | solution.py:399
  205.5 15.1 %collective-permute-start.25 = (f32[5,16,768]{2,1,0:T(8,128)S(1)}, f32[5,16,768]{2,1,0:T(8,128)S(1)}, u32[]{:S(2)}, u32[]{:S(2)}) collective-permute-start(f32[5,16,768]{2,1,0:T(8,128)S(1)} %get-tuple-element.110), channel_id=1, source_target_pairs={{1,0},{2,1},{3,2},{4,3},{5,4},{6,5},{7,6},{8,7},{9,8},{10,9},{11,1... | collective-permute-start | bytes 737288 | tf_op jit(solution)/shard_map/ppermute | solution.py:400
  220.9 5.6 %collective-permute-start.26 = (f32[10,8,768]{2,1,0:T(8,128)S(1)}, f32[10,8,768]{2,1,0:T(8,128)S(1)}, u32[]{:S(2)}, u32[]{:S(2)}) collective-permute-start(f32[10,8,768]{2,1,0:T(8,128)S(1)} %get-tuple-element.111), channel_id=1, source_target_pairs={{0,16},{16,32},{32,48},{48,64},{64,80},{80,96},{96,112},{112,128},... | collective-permute-start | bytes 737288 | tf_op jit(solution)/shard_map/ppermute | solution.py:399
  223.4 8.4 %collective-permute-start.27 = (f32[10,8,768]{2,1,0:T(8,128)S(1)}, f32[10,8,768]{2,1,0:T(8,128)S(1)}, u32[]{:S(2)}, u32[]{:S(2)}) collective-permute-start(f32[10,8,768]{2,1,0:T(8,128)S(1)} %get-tuple-element.113), channel_id=1, source_target_pairs={{16,0},{32,16},{48,32},{64,48},{80,64},{96,80},{112,96},{128,112},... | collective-permute-start | bytes 737288 | tf_op jit(solution)/shard_map/ppermute | solution.py:400
  232.4 14.5 %collective-permute-start.28 = (f32[5,16,768]{2,1,0:T(8,128)S(1)}, f32[5,16,768]{2,1,0:T(8,128)S(1)}, u32[]{:S(2)}, u32[]{:S(2)}) collective-permute-start(f32[5,16,768]{2,1,0:T(8,128)S(1)} %get-tuple-element.114), channel_id=1, source_target_pairs={{0,1},{1,2},{2,3},{3,4},{4,5},{5,6},{6,7},{7,8},{8,9},{9,10},{10,1... | collective-permute-start | bytes 737288 | tf_op jit(solution)/shard_map/ppermute | solution.py:399
  236.5 16.9 %collective-permute-start.29 = (f32[5,16,768]{2,1,0:T(8,128)S(1)}, f32[5,16,768]{2,1,0:T(8,128)S(1)}, u32[]{:S(2)}, u32[]{:S(2)}) collective-permute-start(f32[5,16,768]{2,1,0:T(8,128)S(1)} %get-tuple-element.116), channel_id=1, source_target_pairs={{1,0},{2,1},{3,2},{4,3},{5,4},{6,5},{7,6},{8,7},{9,8},{10,9},{11,1... | collective-permute-start | bytes 737288 | tf_op jit(solution)/shard_map/ppermute | solution.py:400

commit v3 on v2

--- a/solution.py
+++ b/solution.py
@@ -165,7 +165,7 @@
                 out_ref[i, at:at + 8, lanes] = value
         return carry
 
-    lax.fori_loop(0, width // LANES, tile, 0)
+    lax.fori_loop(0, width // LANES, tile, 0, unroll=2)
 
 
 def own(taps, mid, margin, reverse):
@@ -202,7 +202,7 @@
             store(y, j, correlate(taps, outer_rows(low_ref, high_ref, extent, pick), extent, reverse, begun))
         return carry
 
-    lax.fori_loop(0, width // LANES, tile, 0)
+    lax.fori_loop(0, width // LANES, tile, 0, unroll=2)
 
 
 def depth_body(reverse, taps_ref, low_ref, mid_ref, high_ref, *out_refs):
@@ -308,16 +308,13 @@
 
 
 def first_body(lateral_ref, estimate_ref, *refs):
-    out_refs, (wide_ref, full_ref, band_ref, held_ref, sem) = refs[:-5], refs[-5:]
+    out_refs, (wide_ref, full_ref, band_ref) = refs[:-3], refs[-3:]
     nz, ny, nx = estimate_ref.shape
     count = lateral_ref.shape[2]
-    copy = pltpu.make_async_copy(estimate_ref, held_ref, sem)
-    copy.start()
     fill_band(full_ref, normalized(lambda k: lateral_ref[0, 1, k], count), 1)
     split_band(full_ref, band_ref)
     clear_edges(wide_ref)
-    copy.wait()
-    wide_ref[:, SHIFT:SHIFT + nx] = held_ref[...].reshape(nz * ny, nx)
+    wide_ref[:, SHIFT:SHIFT + nx] = estimate_ref[...].reshape(nz * ny, nx)
     put_ahead(wide_ref, band_ref, out_refs, ny)
 
 
@@ -337,18 +334,16 @@
     outs = pl.pallas_call(
         first_body,
         out_shape=shapes,
-        in_specs=[SMEM, pl.BlockSpec(memory_space=pltpu.HBM)],
+        in_specs=[SMEM, VMEM],
         out_specs=[VMEM] * len(shapes),
         scratch_shapes=[
             local(nz * ny, nx + LANES),
             local(2 * LANES, LANES),
             pltpu.VMEM((2 * LANES, 2 * LANES), jnp.bfloat16),
-            local(nz, ny, nx),
-            pltpu.SemaphoreType.DMA(()),
         ],
         compiler_params=LIMIT,
         name="first",
-    )(lateral_kernel, pltpu.with_memory_space_constraint(estimate, pltpu.HBM))
+    )(lateral_kernel, pltpu.with_memory_space_constraint(estimate, pltpu.VMEM))
     return chunked(outs)
 
 

time: 256 us -> 257 us (level)
  starting transfers between devices: 105 us -> 110 us
  waiting for transfers between devices: 130 us -> 126 us
    ppermute x15, waiting for transfers between devices: 76.5 us -> 71.9 us  [exchange(): low = lax.ppermute(last_rows, axis, forward)]
    ppermute x15, starting transfers between devices: 51.6 us -> 55.4 us  [exchange(): low = lax.ppermute(last_rows, axis, forward)]
where the time goes in v3:
time: 257 us; the launch traced here: 255 us
  waiting for transfers between devices  126 us (49%)
  starting transfers between devices  110 us (43%)
  Pallas kernels  16.9 us (7%)
    ppermute x15, waiting for transfers between devices, exchange(): low = lax.ppermute(last_rows, axis, forward)  71.9 us
    ppermute x15, starting transfers between devices, exchange(): low = lax.ppermute(last_rows, axis, forward)  55.4 us
    ppermute x15, waiting for transfers between devices, exchange(): high = lax.ppermute(first_rows, axis, backward)  53.9 us
    ppermute x15, starting transfers between devices, exchange(): high = lax.ppermute(first_rows, axis, backward)  43.4 us
    pallas_call x30, Pallas kernels, call(): pl.pallas_call(body, out_shape=shapes, in_specs=[VMEM] * len(operands), o...  14.6 us
    all_to_all x1, starting transfers between devices, reframe(): arrived = lax.all_to_all(pieces, 'row', 0, 0, tiled=True)  11.6 us
  transfers between devices with their start and end apart: 31, of which 25 were waited for; matrix products, arithmetic and copies ran while one was open for 0% of the time, Pallas kernels for 3%

profile of v3, /device:TPU:123, one launch (start us, length us, event | category | flops | bytes accessed | tf_op | source)
XLA Modules:
  0.0 255.5 jit_solution(2427920108649484003)
XLA Ops:
  0.0 1.0 copy-done
  1.7 1.1 first.1
  2.8 3.3 %collective-permute-start = (f32[5,16,768]{2,1,0:T(8,128)S(1)}, f32[5,16,768]{2,1,0:T(8,128)S(1)}, u32[]{:S(2)}, u32[]{:S(2)}) collective-permute-start(f32[5,16,768]{2,1,0:T(8,128)S(1)} %get-tuple-element.66), channel_id=1, source_target_pairs={{0,1},{1,2},{2,3},{3,4},{4,5},{5,6},{6,7},{7,8},{8,9},{9,10},{10,1... | collective-permute-start | bytes 737288 | tf_op jit(solution)/shard_map/ppermute | solution.py:394
  6.1 2.8 %collective-permute-start.1 = (f32[5,16,768]{2,1,0:T(8,128)S(1)}, f32[5,16,768]{2,1,0:T(8,128)S(1)}, u32[]{:S(2)}, u32[]{:S(2)}) collective-permute-start(f32[5,16,768]{2,1,0:T(8,128)S(1)} %get-tuple-element.68), channel_id=1, source_target_pairs={{1,0},{2,1},{3,2},{4,3},{5,4},{6,5},{7,6},{8,7},{9,8},{10,9},{11,1... | collective-permute-start | bytes 737288 | tf_op jit(solution)/shard_map/ppermute | solution.py:395
  9.0 1.3 prepare.1
  10.5 7.4 %collective-permute-done.low_ref = f32[5,16,768]{2,1,0:T(8,128)S(1)} collective-permute-done((f32[5,16,768]{2,1,0:T(8,128)S(1)}, f32[5,16,768]{2,1,0:T(8,128)S(1)}, u32[]{:S(2)}, u32[]{:S(2)}) %collective-permute-start) | collective-permute-done | bytes 245792 | tf_op jit(solution)/shard_map/ppermute | solution.py:394
  17.9 1.4 collective-permute-done.1.high_ref
  19.5 9.1 %collective-permute-start.2 = (f32[15,8,768]{2,1,0:T(8,128)S(1)}, f32[15,8,768]{2,1,0:T(8,128)S(1)}, u32[]{:S(2)}, u32[]{:S(2)}) collective-permute-start(f32[15,8,768]{2,1,0:T(8,128)S(1)} %get-tuple-element.69), channel_id=1, source_target_pairs={{0,16},{16,32},{32,48},{48,64},{64,80},{80,96},{96,112},{112,128},... | collective-permute-start | bytes 1105928 | tf_op jit(solution)/shard_map/ppermute | solution.py:394
  28.7 1.9 collective-permute-start.3
  31.3 5.0 %collective-permute-done.2.low_ref = f32[15,8,768]{2,1,0:T(8,128)S(1)} collective-permute-done((f32[15,8,768]{2,1,0:T(8,128)S(1)}, f32[15,8,768]{2,1,0:T(8,128)S(1)}, u32[]{:S(2)}, u32[]{:S(2)}) %collective-permute-start.2) | collective-permute-done | bytes 368672 | tf_op jit(solution)/shard_map/ppermute | solution.py:394
  36.2 2.2 collective-permute-done.3.high_ref
  38.4 1.3 shard_map.58
  39.7 3.1 %collective-permute-start.4 = (f32[15,8,768]{2,1,0:T(8,128)}, f32[15,8,768]{2,1,0:T(8,128)S(1)}, u32[]{:S(2)}, u32[]{:S(2)}) collective-permute-start(f32[15,8,768]{2,1,0:T(8,128)} %get-tuple-element.72), channel_id=1, source_target_pairs={{0,16},{16,32},{32,48},{48,64},{64,80},{80,96},{96,112},{112,128},... | collective-permute-start | bytes 1105928 | tf_op jit(solution)/shard_map/ppermute | solution.py:394
  42.8 1.9 collective-permute-start.5
  44.8 1.7 shard_map.66
  46.4 11.6 %all-to-all-start = ((f32[32,24,128]{2,1,0:T(8,128)}), f32[32,24,128]{2,1,0:T(8,128)S(1)}, u32[]{:S(2)}, u32[]{:S(2)}) async-start(f32[32,24,128]{2,1,0:T(8,128)} %shard_map.66), calls=%async_computation | async-start | bytes 786432 | tf_op jit(solution)/shard_map/all_to_all | solution.py:444
  59.0 4.3 %collective-permute-start.6 = (f32[5,16,768]{2,1,0:T(8,128)S(1)}, f32[5,16,768]{2,1,0:T(8,128)S(1)}, u32[]{:S(2)}, u32[]{:S(2)}) collective-permute-start(f32[5,16,768]{2,1,0:T(8,128)S(1)} %get-tuple-element.75), channel_id=1, source_target_pairs={{0,1},{1,2},{2,3},{3,4},{4,5},{5,6},{6,7},{7,8},{8,9},{9,10},{10,1... | collective-permute-start | bytes 737288 | tf_op jit(solution)/shard_map/ppermute | solution.py:394
  63.3 1.9 collective-permute-start.7
  65.4 9.2 %collective-permute-done.6.refs_0_ = f32[5,16,768]{2,1,0:T(8,128)S(1)} collective-permute-done((f32[5,16,768]{2,1,0:T(8,128)S(1)}, f32[5,16,768]{2,1,0:T(8,128)S(1)}, u32[]{:S(2)}, u32[]{:S(2)}) %collective-permute-start.6) | collective-permute-done | bytes 245792 | tf_op jit(solution)/shard_map/ppermute | solution.py:394
  74.6 6.5 %collective-permute-done.7.refs_2_ = f32[5,16,768]{2,1,0:T(8,128)S(1)} collective-permute-done((f32[5,16,768]{2,1,0:T(8,128)S(1)}, f32[5,16,768]{2,1,0:T(8,128)S(1)}, u32[]{:S(2)}, u32[]{:S(2)}) %collective-permute-start.7) | collective-permute-done | bytes 245792 | tf_op jit(solution)/shard_map/ppermute | solution.py:395
  81.1 0.8 shard_map.62
  81.9 2.9 %collective-permute-start.8 = (f32[5,16,768]{2,1,0:T(8,128)S(1)}, f32[5,16,768]{2,1,0:T(8,128)S(1)}, u32[]{:S(2)}, u32[]{:S(2)}) collective-permute-start(f32[5,16,768]{2,1,0:T(8,128)S(1)} %get-tuple-element.81), channel_id=1, source_target_pairs={{0,1},{1,2},{2,3},{3,4},{4,5},{5,6},{6,7},{7,8},{8,9},{9,10},{10,1... | collective-permute-start | bytes 737288 | tf_op jit(solution)/shard_map/ppermute | solution.py:394
  84.8 3.2 %collective-permute-start.9 = (f32[5,16,768]{2,1,0:T(8,128)S(1)}, f32[5,16,768]{2,1,0:T(8,128)S(1)}, u32[]{:S(2)}, u32[]{:S(2)}) collective-permute-start(f32[5,16,768]{2,1,0:T(8,128)S(1)} %get-tuple-element.83), channel_id=1, source_target_pairs={{1,0},{2,1},{3,2},{4,3},{5,4},{6,5},{7,6},{8,7},{9,8},{10,9},{11,1... | collective-permute-start | bytes 737288 | tf_op jit(solution)/shard_map/ppermute | solution.py:395
  88.3 8.7 %collective-permute-done.8.low_ref = f32[5,16,768]{2,1,0:T(8,128)S(1)} collective-permute-done((f32[5,16,768]{2,1,0:T(8,128)S(1)}, f32[5,16,768]{2,1,0:T(8,128)S(1)}, u32[]{:S(2)}, u32[]{:S(2)}) %collective-permute-start.8) | collective-permute-done | bytes 245792 | tf_op jit(solution)/shard_map/ppermute | solution.py:394
  97.0 3.3 %collective-permute-done.9.high_ref = f32[5,16,768]{2,1,0:T(8,128)S(1)} collective-permute-done((f32[5,16,768]{2,1,0:T(8,128)S(1)}, f32[5,16,768]{2,1,0:T(8,128)S(1)}, u32[]{:S(2)}, u32[]{:S(2)}) %collective-permute-start.9) | collective-permute-done | bytes 245792 | tf_op jit(solution)/shard_map/ppermute | solution.py:395
  100.5 4.5 %collective-permute-start.10 = (f32[10,8,768]{2,1,0:T(8,128)S(1)}, f32[10,8,768]{2,1,0:T(8,128)S(1)}, u32[]{:S(2)}, u32[]{:S(2)}) collective-permute-start(f32[10,8,768]{2,1,0:T(8,128)S(1)} %get-tuple-element.84), channel_id=1, source_target_pairs={{0,16},{16,32},{32,48},{48,64},{64,80},{80,96},{96,112},{112,128},... | collective-permute-start | bytes 737288 | tf_op jit(solution)/shard_map/ppermute | solution.py:394
  105.1 1.9 collective-permute-start.11
  107.2 4.5 %collective-permute-start.12 = (f32[5,8,768]{2,1,0:T(8,128)S(1)}, f32[5,8,768]{2,1,0:T(8,128)S(1)}, u32[]{:S(2)}, u32[]{:S(2)}) collective-permute-start(f32[5,8,768]{2,1,0:T(8,128)S(1)} %get-tuple-element.87), channel_id=1, source_target_pairs={{0,16},{16,32},{32,48},{48,64},{64,80},{80,96},{96,112},{112,128},... | collective-permute-start | bytes 368648 | tf_op jit(solution)/shard_map/ppermute | solution.py:394
  111.7 1.9 collective-permute-start.13
  114.0 4.9 %collective-permute-done.13.view_high_ref = f32[5,8,768]{2,1,0:T(8,128)S(1)} collective-permute-done((f32[5,8,768]{2,1,0:T(8,128)S(1)}, f32[5,8,768]{2,1,0:T(8,128)S(1)}, u32[]{:S(2)}, u32[]{:S(2)}) %collective-permute-start.13) | collective-permute-done | bytes 122912 | tf_op jit(solution)/shard_map/ppermute | solution.py:395
  119.5 1.9 collective-permute-start.14
  121.4 4.3 %collective-permute-start.15 = (f32[5,16,768]{2,1,0:T(8,128)S(1)}, f32[5,16,768]{2,1,0:T(8,128)S(1)}, u32[]{:S(2)}, u32[]{:S(2)}) collective-permute-start(f32[5,16,768]{2,1,0:T(8,128)S(1)} %get-tuple-element.92), channel_id=1, source_target_pairs={{1,0},{2,1},{3,2},{4,3},{5,4},{6,5},{7,6},{8,7},{9,8},{10,9},{11,1... | collective-permute-start | bytes 737288 | tf_op jit(solution)/shard_map/ppermute | solution.py:395
  125.9 4.5 %collective-permute-done.14.refs_0_ = f32[5,16,768]{2,1,0:T(8,128)S(1)} collective-permute-done((f32[5,16,768]{2,1,0:T(8,128)S(1)}, f32[5,16,768]{2,1,0:T(8,128)S(1)}, u32[]{:S(2)}, u32[]{:S(2)}) %collective-permute-start.14) | collective-permute-done | bytes 245792 | tf_op jit(solution)/shard_map/ppermute | solution.py:394
  130.4 4.9 %collective-permute-done.15.refs_2_ = f32[5,16,768]{2,1,0:T(8,128)S(1)} collective-permute-done((f32[5,16,768]{2,1,0:T(8,128)S(1)}, f32[5,16,768]{2,1,0:T(8,128)S(1)}, u32[]{:S(2)}, u32[]{:S(2)}) %collective-permute-start.15) | collective-permute-done | bytes 245792 | tf_op jit(solution)/shard_map/ppermute | solution.py:395
  135.3 0.8 shard_map.70
  136.1 1.9 collective-permute-start.16
  138.1 4.3 %collective-permute-start.17 = (f32[5,16,768]{2,1,0:T(8,128)S(1)}, f32[5,16,768]{2,1,0:T(8,128)S(1)}, u32[]{:S(2)}, u32[]{:S(2)}) collective-permute-start(f32[5,16,768]{2,1,0:T(8,128)S(1)} %get-tuple-element.97), channel_id=1, source_target_pairs={{1,0},{2,1},{3,2},{4,3},{5,4},{6,5},{7,6},{8,7},{9,8},{10,9},{11,1... | collective-permute-start | bytes 737288 | tf_op jit(solution)/shard_map/ppermute | solution.py:395
  142.5 9.2 %collective-permute-done.16.low_ref = f32[5,16,768]{2,1,0:T(8,128)S(1)} collective-permute-done((f32[5,16,768]{2,1,0:T(8,128)S(1)}, f32[5,16,768]{2,1,0:T(8,128)S(1)}, u32[]{:S(2)}, u32[]{:S(2)}) %collective-permute-start.16) | collective-permute-done | bytes 245792 | tf_op jit(solution)/shard_map/ppermute | solution.py:394
  151.7 4.1 %collective-permute-done.17.high_ref = f32[5,16,768]{2,1,0:T(8,128)S(1)} collective-permute-done((f32[5,16,768]{2,1,0:T(8,128)S(1)}, f32[5,16,768]{2,1,0:T(8,128)S(1)}, u32[]{:S(2)}, u32[]{:S(2)}) %collective-permute-start.17) | collective-permute-done | bytes 245792 | tf_op jit(solution)/shard_map/ppermute | solution.py:395
  156.1 3.9 %collective-permute-start.18 = (f32[15,8,768]{2,1,0:T(8,128)S(1)}, f32[15,8,768]{2,1,0:T(8,128)S(1)}, u32[]{:S(2)}, u32[]{:S(2)}) collective-permute-start(f32[15,8,768]{2,1,0:T(8,128)S(1)} %get-tuple-element.98), channel_id=1, source_target_pairs={{0,16},{16,32},{32,48},{48,64},{64,80},{80,96},{96,112},{112,128},... | collective-permute-start | bytes 1105928 | tf_op jit(solution)/shard_map/ppermute | solution.py:394
  160.0 1.9 collective-permute-start.19
  162.4 3.7 %collective-permute-done.18.low_ref = f32[15,8,768]{2,1,0:T(8,128)S(1)} collective-permute-done((f32[15,8,768]{2,1,0:T(8,128)S(1)}, f32[15,8,768]{2,1,0:T(8,128)S(1)}, u32[]{:S(2)}, u32[]{:S(2)}) %collective-permute-start.18) | collective-permute-done | bytes 368672 | tf_op jit(solution)/shard_map/ppermute | solution.py:394
  166.1 3.7 %collective-permute-done.19.high_ref = f32[15,8,768]{2,1,0:T(8,128)S(1)} collective-permute-done((f32[15,8,768]{2,1,0:T(8,128)S(1)}, f32[15,8,768]{2,1,0:T(8,128)S(1)}, u32[]{:S(2)}, u32[]{:S(2)}) %collective-permute-start.19) | collective-permute-done | bytes 368672 | tf_op jit(solution)/shard_map/ppermute | solution.py:395
  170.3 1.9 collective-permute-start.20
  172.2 2.4 collective-permute-start.21
  175.1 2.5 collective-permute-done.20.low_ref
  177.5 4.4 %collective-permute-done.21.high_ref = f32[15,8,768]{2,1,0:T(8,128)S(1)} collective-permute-done((f32[15,8,768]{2,1,0:T(8,128)S(1)}, f32[15,8,768]{2,1,0:T(8,128)S(1)}, u32[]{:S(2)}, u32[]{:S(2)}) %collective-permute-start.21) | collective-permute-done | bytes 368672 | tf_op jit(solution)/shard_map/ppermute | solution.py:395
  182.5 1.9 collective-permute-start.22
  184.4 4.3 %collective-permute-start.23 = (f32[5,16,768]{2,1,0:T(8,128)S(1)}, f32[5,16,768]{2,1,0:T(8,128)S(1)}, u32[]{:S(2)}, u32[]{:S(2)}) collective-permute-start(f32[5,16,768]{2,1,0:T(8,128)S(1)} %get-tuple-element.106), channel_id=1, source_target_pairs={{1,0},{2,1},{3,2},{4,3},{5,4},{6,5},{7,6},{8,7},{9,8},{10,9},{11,1... | collective-permute-start | bytes 737288 | tf_op jit(solution)/shard_map/ppermute | solution.py:395
  188.9 9.1 %collective-permute-done.22.refs_0_ = f32[5,16,768]{2,1,0:T(8,128)S(1)} collective-permute-done((f32[5,16,768]{2,1,0:T(8,128)S(1)}, f32[5,16,768]{2,1,0:T(8,128)S(1)}, u32[]{:S(2)}, u32[]{:S(2)}) %collective-permute-start.22) | collective-permute-done | bytes 245792 | tf_op jit(solution)/shard_map/ppermute | solution.py:394
  198.0 4.0 %collective-permute-done.23.refs_2_ = f32[5,16,768]{2,1,0:T(8,128)S(1)} collective-permute-done((f32[5,16,768]{2,1,0:T(8,128)S(1)}, f32[5,16,768]{2,1,0:T(8,128)S(1)}, u32[]{:S(2)}, u32[]{:S(2)}) %collective-permute-start.23) | collective-permute-done | bytes 245792 | tf_op jit(solution)/shard_map/ppermute | solution.py:395
  202.0 0.8 shard_map.78
  202.8 1.9 collective-permute-start.24
  204.7 4.3 %collective-permute-start.25 = (f32[5,16,768]{2,1,0:T(8,128)S(1)}, f32[5,16,768]{2,1,0:T(8,128)S(1)}, u32[]{:S(2)}, u32[]{:S(2)}) collective-permute-start(f32[5,16,768]{2,1,0:T(8,128)S(1)} %get-tuple-element.110), channel_id=1, source_target_pairs={{1,0},{2,1},{3,2},{4,3},{5,4},{6,5},{7,6},{8,7},{9,8},{10,9},{11,1... | collective-permute-start | bytes 737288 | tf_op jit(solution)/shard_map/ppermute | solution.py:395
  209.2 6.0 %collective-permute-done.24.low_ref = f32[5,16,768]{2,1,0:T(8,128)S(1)} collective-permute-done((f32[5,16,768]{2,1,0:T(8,128)S(1)}, f32[5,16,768]{2,1,0:T(8,128)S(1)}, u32[]{:S(2)}, u32[]{:S(2)}) %collective-permute-start.24) | collective-permute-done | bytes 245792 | tf_op jit(solution)/shard_map/ppermute | solution.py:394
  215.2 1.7 collective-permute-done.25.high_ref
  217.1 8.1 %collective-permute-start.26 = (f32[10,8,768]{2,1,0:T(8,128)S(1)}, f32[10,8,768]{2,1,0:T(8,128)S(1)}, u32[]{:S(2)}, u32[]{:S(2)}) collective-permute-start(f32[10,8,768]{2,1,0:T(8,128)S(1)} %get-tuple-element.111), channel_id=1, source_target_pairs={{0,16},{16,32},{32,48},{48,64},{64,80},{80,96},{96,112},{112,128},... | collective-permute-start | bytes 737288 | tf_op jit(solution)/shard_map/ppermute | solution.py:394
  225.2 2.1 collective-permute-start.27
  228.3 8.3 %collective-permute-done.27.high_ref = f32[10,8,768]{2,1,0:T(8,128)S(1)} collective-permute-done((f32[10,8,768]{2,1,0:T(8,128)S(1)}, f32[10,8,768]{2,1,0:T(8,128)S(1)}, u32[]{:S(2)}, u32[]{:S(2)}) %collective-permute-start.27) | collective-permute-done | bytes 245792 | tf_op jit(solution)/shard_map/ppermute | solution.py:395
  237.3 1.9 collective-permute-start.28
  239.2 4.3 %collective-permute-start.29 = (f32[5,16,768]{2,1,0:T(8,128)S(1)}, f32[5,16,768]{2,1,0:T(8,128)S(1)}, u32[]{:S(2)}, u32[]{:S(2)}) collective-permute-start(f32[5,16,768]{2,1,0:T(8,128)S(1)} %get-tuple-element.116), channel_id=1, source_target_pairs={{1,0},{2,1},{3,2},{4,3},{5,4},{6,5},{7,6},{8,7},{9,8},{10,9},{11,1... | collective-permute-start | bytes 737288 | tf_op jit(solution)/shard_map/ppermute | solution.py:395
  243.7 5.9 %collective-permute-done.28.refs_0_ = f32[5,16,768]{2,1,0:T(8,128)S(1)} collective-permute-done((f32[5,16,768]{2,1,0:T(8,128)S(1)}, f32[5,16,768]{2,1,0:T(8,128)S(1)}, u32[]{:S(2)}, u32[]{:S(2)}) %collective-permute-start.28) | collective-permute-done | bytes 245792 | tf_op jit(solution)/shard_map/ppermute | solution.py:394
  249.6 4.6 %collective-permute-done.29.refs_2_ = f32[5,16,768]{2,1,0:T(8,128)S(1)} collective-permute-done((f32[5,16,768]{2,1,0:T(8,128)S(1)}, f32[5,16,768]{2,1,0:T(8,128)S(1)}, u32[]{:S(2)}, u32[]{:S(2)}) %collective-permute-start.29) | collective-permute-done | bytes 245792 | tf_op jit(solution)/shard_map/ppermute | solution.py:395
  254.2 1.3 shard_map.84
  (45 shorter events, 9.6 us)
Async XLA Ops:
  0.0 1.0 copy-start
  1.0 0.7 copy-start.3
  2.7 6.2 %copy-start.4 = (f32[2,2,11]{2,1,0:T(2,128)S(1)}, f32[2,2,11]{2,1,0:T(2,128)}, u32[]{:S(2)}) copy-start(f32[2,2,11]{2,1,0:T(2,128)} %lateral_ref.3) | copy-start | bytes 532
  2.7 6.2 %copy-start.5 = (f32[2,31]{1,0:T(2,128)S(1)}, f32[2,31]{1,0:T(2,128)}, u32[]{:S(2)}) copy-start(f32[2,31]{1,0:T(2,128)} %axial_ref.1) | copy-start | bytes 748
  2.8 15.1 %collective-permute-start = (f32[5,16,768]{2,1,0:T(8,128)S(1)}, f32[5,16,768]{2,1,0:T(8,128)S(1)}, u32[]{:S(2)}, u32[]{:S(2)}) collective-permute-start(f32[5,16,768]{2,1,0:T(8,128)S(1)} %get-tuple-element.66), channel_id=1, source_target_pairs={{0,1},{1,2},{2,3},{3,4},{4,5},{5,6},{6,7},{7,8},{8,9},{9,10},{10,1... | collective-permute-start | bytes 737288 | tf_op jit(solution)/shard_map/ppermute | solution.py:394
  6.1 13.2 %collective-permute-start.1 = (f32[5,16,768]{2,1,0:T(8,128)S(1)}, f32[5,16,768]{2,1,0:T(8,128)S(1)}, u32[]{:S(2)}, u32[]{:S(2)}) collective-permute-start(f32[5,16,768]{2,1,0:T(8,128)S(1)} %get-tuple-element.68), channel_id=1, source_target_pairs={{1,0},{2,1},{3,2},{4,3},{5,4},{6,5},{7,6},{8,7},{9,8},{10,9},{11,1... | collective-permute-start | bytes 737288 | tf_op jit(solution)/shard_map/ppermute | solution.py:395
  10.5 20.1 %copy-start.6 = (f32[8,16,768]{2,1,0:T(8,128)S(1)}, f32[8,16,768]{2,1,0:T(8,128)}, u32[]{:S(2)}) copy-start(f32[8,16,768]{2,1,0:T(8,128)} %param.5) | copy-start | bytes 1179652
  19.5 16.7 %collective-permute-start.2 = (f32[15,8,768]{2,1,0:T(8,128)S(1)}, f32[15,8,768]{2,1,0:T(8,128)S(1)}, u32[]{:S(2)}, u32[]{:S(2)}) collective-permute-start(f32[15,8,768]{2,1,0:T(8,128)S(1)} %get-tuple-element.69), channel_id=1, source_target_pairs={{0,16},{16,32},{32,48},{48,64},{64,80},{80,96},{96,112},{112,128},... | collective-permute-start | bytes 1105928 | tf_op jit(solution)/shard_map/ppermute | solution.py:394
  28.7 9.7 %collective-permute-start.3 = (f32[15,8,768]{2,1,0:T(8,128)S(1)}, f32[15,8,768]{2,1,0:T(8,128)S(1)}, u32[]{:S(2)}, u32[]{:S(2)}) collective-permute-start(f32[15,8,768]{2,1,0:T(8,128)S(1)} %get-tuple-element.71), channel_id=1, source_target_pairs={{16,0},{32,16},{48,32},{64,48},{80,64},{96,80},{112,96},{128,112},... | collective-permute-start | bytes 1105928 | tf_op jit(solution)/shard_map/ppermute | solution.py:395
  38.4 6.3 %copy-start.2 = (f32[8,24,512]{2,1,0:T(8,128)S(1)}, f32[8,24,512]{2,1,0:T(8,128)}, u32[]{:S(2)}) copy-start(f32[8,24,512]{2,1,0:T(8,128)} %view_ref.1) | copy-start | bytes 1179652
  39.7 18.7 %collective-permute-start.4 = (f32[15,8,768]{2,1,0:T(8,128)}, f32[15,8,768]{2,1,0:T(8,128)S(1)}, u32[]{:S(2)}, u32[]{:S(2)}) collective-permute-start(f32[15,8,768]{2,1,0:T(8,128)} %get-tuple-element.72), channel_id=1, source_target_pairs={{0,16},{16,32},{32,48},{48,64},{64,80},{80,96},{96,112},{112,128},... | collective-permute-start | bytes 1105928 | tf_op jit(solution)/shard_map/ppermute | solution.py:394
  42.8 15.6 %collective-permute-start.5 = (f32[15,8,768]{2,1,0:T(8,128)S(1)}, f32[15,8,768]{2,1,0:T(8,128)S(1)}, u32[]{:S(2)}, u32[]{:S(2)}) collective-permute-start(f32[15,8,768]{2,1,0:T(8,128)S(1)} %get-tuple-element.74), channel_id=1, source_target_pairs={{16,0},{32,16},{48,32},{64,48},{80,64},{96,80},{112,96},{128,112},... | collective-permute-start | bytes 1105928 | tf_op jit(solution)/shard_map/ppermute | solution.py:395
  46.4 60.6 %all-to-all-start = ((f32[32,24,128]{2,1,0:T(8,128)}), f32[32,24,128]{2,1,0:T(8,128)S(1)}, u32[]{:S(2)}, u32[]{:S(2)}) async-start(f32[32,24,128]{2,1,0:T(8,128)} %shard_map.66), calls=%async_computation | async-start | bytes 786432 | tf_op jit(solution)/shard_map/all_to_all | solution.py:444
  59.0 15.6 %collective-permute-start.6 = (f32[5,16,768]{2,1,0:T(8,128)S(1)}, f32[5,16,768]{2,1,0:T(8,128)S(1)}, u32[]{:S(2)}, u32[]{:S(2)}) collective-permute-start(f32[5,16,768]{2,1,0:T(8,128)S(1)} %get-tuple-element.75), channel_id=1, source_target_pairs={{0,1},{1,2},{2,3},{3,4},{4,5},{5,6},{6,7},{7,8},{8,9},{9,10},{10,1... | collective-permute-start | bytes 737288 | tf_op jit(solution)/shard_map/ppermute | solution.py:394
  63.3 17.8 %collective-permute-start.7 = (f32[5,16,768]{2,1,0:T(8,128)S(1)}, f32[5,16,768]{2,1,0:T(8,128)S(1)}, u32[]{:S(2)}, u32[]{:S(2)}) collective-permute-start(f32[5,16,768]{2,1,0:T(8,128)S(1)} %get-tuple-element.77), channel_id=1, source_target_pairs={{1,0},{2,1},{3,2},{4,3},{5,4},{6,5},{7,6},{8,7},{9,8},{10,9},{11,1... | collective-permute-start | bytes 737288 | tf_op jit(solution)/shard_map/ppermute | solution.py:395
  65.2 15.9 %copy-start.1 = (f32[8,16,768]{2,1,0:T(8,128)S(1)}, f32[8,16,768]{2,1,0:T(8,128)}, u32[]{:S(2)}) copy-start(f32[8,16,768]{2,1,0:T(8,128)} %estimate_ref.3) | copy-start | bytes 1179652
  81.9 15.1 %collective-permute-start.8 = (f32[5,16,768]{2,1,0:T(8,128)S(1)}, f32[5,16,768]{2,1,0:T(8,128)S(1)}, u32[]{:S(2)}, u32[]{:S(2)}) collective-permute-start(f32[5,16,768]{2,1,0:T(8,128)S(1)} %get-tuple-element.81), channel_id=1, source_target_pairs={{0,1},{1,2},{2,3},{3,4},{4,5},{5,6},{6,7},{7,8},{8,9},{9,10},{10,1... | collective-permute-start | bytes 737288 | tf_op jit(solution)/shard_map/ppermute | solution.py:394
  84.8 15.5 %collective-permute-start.9 = (f32[5,16,768]{2,1,0:T(8,128)S(1)}, f32[5,16,768]{2,1,0:T(8,128)S(1)}, u32[]{:S(2)}, u32[]{:S(2)}) collective-permute-start(f32[5,16,768]{2,1,0:T(8,128)S(1)} %get-tuple-element.83), channel_id=1, source_target_pairs={{1,0},{2,1},{3,2},{4,3},{5,4},{6,5},{7,6},{8,7},{9,8},{10,9},{11,1... | collective-permute-start | bytes 737288 | tf_op jit(solution)/shard_map/ppermute | solution.py:395
  100.5 18.3 %collective-permute-start.10 = (f32[10,8,768]{2,1,0:T(8,128)S(1)}, f32[10,8,768]{2,1,0:T(8,128)S(1)}, u32[]{:S(2)}, u32[]{:S(2)}) collective-permute-start(f32[10,8,768]{2,1,0:T(8,128)S(1)} %get-tuple-element.84), channel_id=1, source_target_pairs={{0,16},{16,32},{32,48},{48,64},{64,80},{80,96},{96,112},{112,128},... | collective-permute-start | bytes 737288 | tf_op jit(solution)/shard_map/ppermute | solution.py:394
  105.1 13.8 %collective-permute-start.11 = (f32[10,8,768]{2,1,0:T(8,128)S(1)}, f32[10,8,768]{2,1,0:T(8,128)S(1)}, u32[]{:S(2)}, u32[]{:S(2)}) collective-permute-start(f32[10,8,768]{2,1,0:T(8,128)S(1)} %get-tuple-element.86), channel_id=1, source_target_pairs={{16,0},{32,16},{48,32},{64,48},{80,64},{96,80},{112,96},{128,112},... | collective-permute-start | bytes 737288 | tf_op jit(solution)/shard_map/ppermute | solution.py:395
  107.2 6.8 %collective-permute-start.12 = (f32[5,8,768]{2,1,0:T(8,128)S(1)}, f32[5,8,768]{2,1,0:T(8,128)S(1)}, u32[]{:S(2)}, u32[]{:S(2)}) collective-permute-start(f32[5,8,768]{2,1,0:T(8,128)S(1)} %get-tuple-element.87), channel_id=1, source_target_pairs={{0,16},{16,32},{32,48},{48,64},{64,80},{80,96},{96,112},{112,128},... | collective-permute-start | bytes 368648 | tf_op jit(solution)/shard_map/ppermute | solution.py:394
  111.7 7.1 %collective-permute-start.13 = (f32[5,8,768]{2,1,0:T(8,128)S(1)}, f32[5,8,768]{2,1,0:T(8,128)S(1)}, u32[]{:S(2)}, u32[]{:S(2)}) collective-permute-start(f32[5,8,768]{2,1,0:T(8,128)S(1)} %get-tuple-element.89), channel_id=1, source_target_pairs={{16,0},{32,16},{48,32},{64,48},{80,64},{96,80},{112,96},{128,112},... | collective-permute-start | bytes 368648 | tf_op jit(solution)/shard_map/ppermute | solution.py:395
  119.5 10.9 %collective-permute-start.14 = (f32[5,16,768]{2,1,0:T(8,128)S(1)}, f32[5,16,768]{2,1,0:T(8,128)S(1)}, u32[]{:S(2)}, u32[]{:S(2)}) collective-permute-start(f32[5,16,768]{2,1,0:T(8,128)S(1)} %get-tuple-element.90), channel_id=1, source_target_pairs={{0,1},{1,2},{2,3},{3,4},{4,5},{5,6},{6,7},{7,8},{8,9},{9,10},{10,1... | collective-permute-start | bytes 737288 | tf_op jit(solution)/shard_map/ppermute | solution.py:394
  121.4 13.9 %collective-permute-start.15 = (f32[5,16,768]{2,1,0:T(8,128)S(1)}, f32[5,16,768]{2,1,0:T(8,128)S(1)}, u32[]{:S(2)}, u32[]{:S(2)}) collective-permute-start(f32[5,16,768]{2,1,0:T(8,128)S(1)} %get-tuple-element.92), channel_id=1, source_target_pairs={{1,0},{2,1},{3,2},{4,3},{5,4},{6,5},{7,6},{8,7},{9,8},{10,9},{11,1... | collective-permute-start | bytes 737288 | tf_op jit(solution)/shard_map/ppermute | solution.py:395
  136.1 15.6 %collective-permute-start.16 = (f32[5,16,768]{2,1,0:T(8,128)S(1)}, f32[5,16,768]{2,1,0:T(8,128)S(1)}, u32[]{:S(2)}, u32[]{:S(2)}) collective-permute-start(f32[5,16,768]{2,1,0:T(8,128)S(1)} %get-tuple-element.95), channel_id=1, source_target_pairs={{0,1},{1,2},{2,3},{3,4},{4,5},{5,6},{6,7},{7,8},{8,9},{9,10},{10,1... | collective-permute-start | bytes 737288 | tf_op jit(solution)/shard_map/ppermute | solution.py:394
  138.1 17.8 %collective-permute-start.17 = (f32[5,16,768]{2,1,0:T(8,128)S(1)}, f32[5,16,768]{2,1,0:T(8,128)S(1)}, u32[]{:S(2)}, u32[]{:S(2)}) collective-permute-start(f32[5,16,768]{2,1,0:T(8,128)S(1)} %get-tuple-element.97), channel_id=1, source_target_pairs={{1,0},{2,1},{3,2},{4,3},{5,4},{6,5},{7,6},{8,7},{9,8},{10,9},{11,1... | collective-permute-start | bytes 737288 | tf_op jit(solution)/shard_map/ppermute | solution.py:395
  156.1 10.0 %collective-permute-start.18 = (f32[15,8,768]{2,1,0:T(8,128)S(1)}, f32[15,8,768]{2,1,0:T(8,128)S(1)}, u32[]{:S(2)}, u32[]{:S(2)}) collective-permute-start(f32[15,8,768]{2,1,0:T(8,128)S(1)} %get-tuple-element.98), channel_id=1, source_target_pairs={{0,16},{16,32},{32,48},{48,64},{64,80},{80,96},{96,112},{112,128},... | collective-permute-start | bytes 1105928 | tf_op jit(solution)/shard_map/ppermute | solution.py:394
  160.0 9.7 %collective-permute-start.19 = (f32[15,8,768]{2,1,0:T(8,128)S(1)}, f32[15,8,768]{2,1,0:T(8,128)S(1)}, u32[]{:S(2)}, u32[]{:S(2)}) collective-permute-start(f32[15,8,768]{2,1,0:T(8,128)S(1)} %get-tuple-element.100), channel_id=1, source_target_pairs={{16,0},{32,16},{48,32},{64,48},{80,64},{96,80},{112,96},{128,112},... | collective-permute-start | bytes 1105928 | tf_op jit(solution)/shard_map/ppermute | solution.py:395
  170.3 7.3 %collective-permute-start.20 = (f32[15,8,768]{2,1,0:T(8,128)S(1)}, f32[15,8,768]{2,1,0:T(8,128)S(1)}, u32[]{:S(2)}, u32[]{:S(2)}) collective-permute-start(f32[15,8,768]{2,1,0:T(8,128)S(1)} %get-tuple-element.101), channel_id=1, source_target_pairs={{0,16},{16,32},{32,48},{48,64},{64,80},{80,96},{96,112},{112,128},... | collective-permute-start | bytes 1105928 | tf_op jit(solution)/shard_map/ppermute | solution.py:394
  172.2 9.7 %collective-permute-start.21 = (f32[15,8,768]{2,1,0:T(8,128)S(1)}, f32[15,8,768]{2,1,0:T(8,128)S(1)}, u32[]{:S(2)}, u32[]{:S(2)}) collective-permute-start(f32[15,8,768]{2,1,0:T(8,128)S(1)} %get-tuple-element.103), channel_id=1, source_target_pairs={{16,0},{32,16},{48,32},{64,48},{80,64},{96,80},{112,96},{128,112},... | collective-permute-start | bytes 1105928 | tf_op jit(solution)/shard_map/ppermute | solution.py:395
  182.5 15.5 %collective-permute-start.22 = (f32[5,16,768]{2,1,0:T(8,128)S(1)}, f32[5,16,768]{2,1,0:T(8,128)S(1)}, u32[]{:S(2)}, u32[]{:S(2)}) collective-permute-start(f32[5,16,768]{2,1,0:T(8,128)S(1)} %get-tuple-element.104), channel_id=1, source_target_pairs={{0,1},{1,2},{2,3},{3,4},{4,5},{5,6},{6,7},{7,8},{8,9},{9,10},{10,1... | collective-permute-start | bytes 737288 | tf_op jit(solution)/shard_map/ppermute | solution.py:394
  184.4 17.6 %collective-permute-start.23 = (f32[5,16,768]{2,1,0:T(8,128)S(1)}, f32[5,16,768]{2,1,0:T(8,128)S(1)}, u32[]{:S(2)}, u32[]{:S(2)}) collective-permute-start(f32[5,16,768]{2,1,0:T(8,128)S(1)} %get-tuple-element.106), channel_id=1, source_target_pairs={{1,0},{2,1},{3,2},{4,3},{5,4},{6,5},{7,6},{8,7},{9,8},{10,9},{11,1... | collective-permute-start | bytes 737288 | tf_op jit(solution)/shard_map/ppermute | solution.py:395
  202.8 12.4 %collective-permute-start.24 = (f32[5,16,768]{2,1,0:T(8,128)S(1)}, f32[5,16,768]{2,1,0:T(8,128)S(1)}, u32[]{:S(2)}, u32[]{:S(2)}) collective-permute-start(f32[5,16,768]{2,1,0:T(8,128)S(1)} %get-tuple-element.108), channel_id=1, source_target_pairs={{0,1},{1,2},{2,3},{3,4},{4,5},{5,6},{6,7},{7,8},{8,9},{9,10},{10,1... | collective-permute-start | bytes 737288 | tf_op jit(solution)/shard_map/ppermute | solution.py:394
  204.7 12.1 %collective-permute-start.25 = (f32[5,16,768]{2,1,0:T(8,128)S(1)}, f32[5,16,768]{2,1,0:T(8,128)S(1)}, u32[]{:S(2)}, u32[]{:S(2)}) collective-permute-start(f32[5,16,768]{2,1,0:T(8,128)S(1)} %get-tuple-element.110), channel_id=1, source_target_pairs={{1,0},{2,1},{3,2},{4,3},{5,4},{6,5},{7,6},{8,7},{9,8},{10,9},{11,1... | collective-permute-start | bytes 737288 | tf_op jit(solution)/shard_map/ppermute | solution.py:395
  217.1 11.2 %collective-permute-start.26 = (f32[10,8,768]{2,1,0:T(8,128)S(1)}, f32[10,8,768]{2,1,0:T(8,128)S(1)}, u32[]{:S(2)}, u32[]{:S(2)}) collective-permute-start(f32[10,8,768]{2,1,0:T(8,128)S(1)} %get-tuple-element.111), channel_id=1, source_target_pairs={{0,16},{16,32},{32,48},{48,64},{64,80},{80,96},{96,112},{112,128},... | collective-permute-start | bytes 737288 | tf_op jit(solution)/shard_map/ppermute | solution.py:394
  225.2 11.4 %collective-permute-start.27 = (f32[10,8,768]{2,1,0:T(8,128)S(1)}, f32[10,8,768]{2,1,0:T(8,128)S(1)}, u32[]{:S(2)}, u32[]{:S(2)}) collective-permute-start(f32[10,8,768]{2,1,0:T(8,128)S(1)} %get-tuple-element.113), channel_id=1, source_target_pairs={{16,0},{32,16},{48,32},{64,48},{80,64},{96,80},{112,96},{128,112},... | collective-permute-start | bytes 737288 | tf_op jit(solution)/shard_map/ppermute | solution.py:395
  237.3 12.3 %collective-permute-start.28 = (f32[5,16,768]{2,1,0:T(8,128)S(1)}, f32[5,16,768]{2,1,0:T(8,128)S(1)}, u32[]{:S(2)}, u32[]{:S(2)}) collective-permute-start(f32[5,16,768]{2,1,0:T(8,128)S(1)} %get-tuple-element.114), channel_id=1, source_target_pairs={{0,1},{1,2},{2,3},{3,4},{4,5},{5,6},{6,7},{7,8},{8,9},{9,10},{10,1... | collective-permute-start | bytes 737288 | tf_op jit(solution)/shard_map/ppermute | solution.py:394
  239.2 15.0 %collective-permute-start.29 = (f32[5,16,768]{2,1,0:T(8,128)S(1)}, f32[5,16,768]{2,1,0:T(8,128)S(1)}, u32[]{:S(2)}, u32[]{:S(2)}) collective-permute-start(f32[5,16,768]{2,1,0:T(8,128)S(1)} %get-tuple-element.116), channel_id=1, source_target_pairs={{1,0},{2,1},{3,2},{4,3},{5,4},{6,5},{7,6},{8,7},{9,8},{10,9},{11,1... | collective-permute-start | bytes 737288 | tf_op jit(solution)/shard_map/ppermute | solution.py:395
